TPU v7x, 32 devices: a whole 2x2x4 slice. The times are simulated.
32 devices in a mesh: dp: 8 (over z, y), hg: 2 (over x), hid: 2 (over core).
Axes of the slice: x: 2, y: 2, z: 4, core: 2. Of those that a mesh axis runs over, the one named last changes fastest.
Arguments:
- tokens: bfloat16 [18816, 768], P(('dp', 'hid')), may hold values from -6 to 6
- big_images: int32 [16], P(('dp', 'hid')), may hold values from 0 to 1, as said below
- norm_gain: bfloat16 [768], replicated, may hold values from 0.5 to 1.5
- w_qkv: bfloat16 [768, 2304], P(None, 'hg'), may hold values from -0.21875 to 0.21875
- qk_gains: bfloat16 [2, 64], replicated, may hold values from 0.099609375 to 1.8984375
- w_out_t: bfloat16 [768, 768], P(None, 'hg'), may hold values from -0.625 to 0.625
- w_in: bfloat16 [768, 3072], P(None, ('hg', 'hid')), may hold values from -0.21875 to 0.21875
- w_back: bfloat16 [768, 3072], P(None, ('hg', 'hid')), may hold values from -0.109375 to 0.109375
- cotangent: bfloat16 [18816, 768], P(('dp', 'hid'), 'hg'), may hold values from -6 to 6
Outputs:
- output: bfloat16 [18816, 768], P(('dp', 'hid'), 'hg')
- token_grad: bfloat16 [18816, 768], P(('dp', 'hid'))
- norm_gain_grad: float32 [768], P(('dp', 'hid'))
- w_qkv_grad: float32 [768, 2304], P(('dp', 'hid'), 'hg')
- qk_gains_grad: float32 [2, 64], replicated
- w_out_t_grad: float32 [768, 768], P(('dp', 'hid'), 'hg')
- w_in_grad: float32 [768, 3072], P('dp', ('hg', 'hid'))
- w_back_grad: float32 [768, 3072], P('dp', ('hg', 'hid'))
Inputs may be any that keep to these rules, and one draw needn't show every extreme that they name: `big_images`: 1 where the 1176 tokens of a group form one image, 0 where they form 6 images of 196 tokens each in order; every draw has groups of both kinds.
All inputs are finite; a program needn't handle non-finite values.
Results may differ from a plain program's by a relative error of at most 0.012.
Values may be sent and summed in bfloat16 or wider, within the bound.
No kernel may reach another device: no remote copies, remote signals or barrier semaphores. Data moves between devices by JAX's collectives and lax.ppermute only.
A program may use at most 256 MiB of HBM per device.

v0:
```python
import functools
import math

import jax
import jax.numpy as jnp
from jax import lax
from jax.experimental import pallas as pl
from jax.experimental.pallas import tpu as pltpu
from jax.sharding import PartitionSpec as P

PATCHES = 196
EPSILON = 1e-06
LOG2E = math.log2(math.e)
LANES = 128
VMEM = pltpu.VMEM
SCALE = 1.0


def cost(microseconds):
    return pl.CostEstimate(
        flops=int(microseconds * SCALE * 1e9), bytes_accessed=2**20, transcendentals=0
    )


def times_t(left, right):
    return lax.dot_general(
        left, right, (((1,), (1,)), ((), ())), preferred_element_type=jnp.float32
    )


def rows_t(left, right):
    return lax.dot_general(
        left, right, (((0,), (0,)), ((), ())), preferred_element_type=jnp.float32
    )


def times(left, right):
    return jnp.dot(left, right, preferred_element_type=jnp.float32)


def low(value):
    return value.astype(jnp.bfloat16)


def wide(value):
    return value.astype(jnp.float32)


def lane_of(shape):
    return lax.broadcasted_iota(jnp.int32, shape, 1)


def row_of(shape):
    return lax.broadcasted_iota(jnp.int32, shape, 0)


def other_half(value):
    return pltpu.roll(value, LANES // 2, 1)


def spread_terms(whole):
    lane = lane_of(whole.shape)
    first = wide(low(whole))
    second = wide(low(whole - first))
    third = whole - first - second
    return jnp.where(lane == 64, first, jnp.where(lane == 65, second, jnp.where(lane == 66, third, 0.0)))


def three_terms(column, shape):
    return spread_terms(jnp.broadcast_to(column, shape))


def two_terms(value):
    first = low(value)
    return first, low(value - wide(first))


def pair_mask(block, shape, first_lane):
    start = 2 * PATCHES * block - first_lane
    place = lane_of(shape) - start
    second = row_of(shape) >= PATCHES
    begin = jnp.where(second, PATCHES, 0)
    return (place >= begin) & (place < begin + PATCHES)


def window_of(block):
    return (2 * PATCHES * block // LANES) * LANES, 4 * LANES


def forward_kernel(
    flag_ref, tok_ref, gain_ref, w_ref, qk_ref, normed_ref, q_ref, k_ref, v_ref, att_ref, inv_ref
):
    rows = tok_ref.shape[0]
    heads, padded, _ = q_ref.shape
    tile = 2 * PATCHES
    size = qk_ref.shape[1]
    columns = w_ref.shape[1]
    gain = wide(gain_ref[...])
    q_gain = wide(qk_ref[0:1, :]) * (size**-0.5 * LOG2E)
    k_gain = wide(qk_ref[1:2, :])
    ones = jnp.ones_like(k_gain)
    gains = jnp.concatenate([q_gain, k_gain, ones, q_gain, k_gain, ones], axis=1)
    is_value = jnp.concatenate([0 * ones, 0 * ones, ones, 0 * ones, 0 * ones, ones], axis=1)
    group_a = row_of((256, 256)) // size
    group_b = lane_of((256, 256)) // size
    mean_of = low(jnp.where(group_a == group_b, 1.0 / size, 0.0))
    stride = rows // (3 * LANES) and 3 * LANES
    strip = rows - (rows // stride - 1) * stride
    lane = lane_of((strip, LANES))

    def project(step, _):
        here = pl.ds(pl.multiple_of(step * stride, LANES), strip)
        x = wide(tok_ref[here, :])
        x = x - jnp.mean(x, axis=1, keepdims=True)
        x = x * lax.rsqrt(jnp.mean(x * x, axis=1, keepdims=True) + EPSILON)
        normed = low(x * gain)
        normed_ref[here, :] = normed
        compact = jnp.zeros((strip, LANES), jnp.float32)
        for pair in range(heads // 2):
            joined = times(normed, w_ref[:, 384 * pair : 384 * pair + 384])
            parts = []
            for at in (0, 256):
                wid = min(256, 384 - at)
                block = joined[:, at : at + wid]
                means = mean_of[:wid, :wid]
                centred = block - times(low(block), means)
                squares = low(centred * centred)
                variance = times(squares, means)
                place = 6 * pair + at // size
                pick = low(
                    jnp.where(
                        row_of((wid, LANES)) // size + place == lane_of((wid, LANES)), 1.0 / size, 0.0
                    )
                )
                compact = compact + times(squares, pick)
                hat = centred * lax.rsqrt(variance + EPSILON)
                parts.append(
                    jnp.where(is_value[:, at : at + wid] > 0, block, hat * gains[:, at : at + wid])
                )
            b0, b1, b2 = parts[0][:, :128], parts[0][:, 128:], parts[1]
            first = lane < 64
            unit = jnp.where(lane < 67, 1.0, 0.0)
            q_ref[2 * pair, here, :] = low(jnp.where(first, b0, 0.0))
            k_ref[2 * pair, here, :] = low(jnp.where(first, other_half(b0), unit))
            v_ref[2 * pair, here, :] = low(jnp.where(first, b1, unit))
            q_ref[2 * pair + 1, here, :] = low(jnp.where(first, other_half(b1), 0.0))
            k_ref[2 * pair + 1, here, :] = low(jnp.where(first, b2, unit))
            v_ref[2 * pair + 1, here, :] = low(jnp.where(first, other_half(b2), unit))
        inv_ref[here, :] = lax.rsqrt(compact + EPSILON)
        return 0

    lax.fori_loop(0, rows // stride, project, 0)
    lane = lane_of((tile, LANES))
    for ref in (q_ref, k_ref, v_ref):
        ref[:, rows:, :] = jnp.zeros((heads, padded - rows, LANES), jnp.bfloat16)

    def attend(pair, _, big):
        for start in range(0, rows, tile):
            here = slice(start, start + tile)
            if big:
                keys = slice(0, padded)
            else:
                begin, length = window_of(start // tile)
                keys = slice(begin, begin + length)
            found = []
            for side in range(2):
                head = 2 * pair + side
                queries = q_ref[head, here, :]
                scores = times_t(queries, k_ref[head, keys, :])
                if not big:
                    scores = jnp.where(
                        pair_mask(start // tile, scores.shape, keys.start), scores, -1e30
                    )
                expo = low(jnp.exp2(scores))
                out = times(expo, v_ref[head, keys, :])
                total = out[:, 64:65]
                found.append(out * (1.0 / total))
                log_total = jnp.log(total) * (-LOG2E)
                q_ref[head, here, :] = low(
                    jnp.where(lane < 64, wide(queries), three_terms(log_total, lane.shape))
                )
            att_ref[here, pl.ds(pl.multiple_of(pair * LANES, LANES), LANES)] = low(
                jnp.where(lane < 64, found[0], other_half(found[1]))
            )
        return 0

    @pl.when(flag_ref[0] > 0)
    def _():
        lax.fori_loop(0, heads // 2, functools.partial(attend, big=True), 0)

    @pl.when(flag_ref[0] <= 0)
    def _():
        lax.fori_loop(0, heads // 2, functools.partial(attend, big=False), 0)


def forward(big_images, tokens, norm_gain, w_qkv, qk_gains):
    rows, width = tokens.shape
    size = qk_gains.shape[1]
    heads = w_qkv.shape[1] // (3 * size)
    padded = -(-rows // 256) * 256
    whole = pl.BlockSpec(memory_space=VMEM)
    head_rows = jax.ShapeDtypeStruct((heads, padded, LANES), jnp.bfloat16)
    return pl.pallas_call(
        forward_kernel,
        name="forward",
        out_shape=[
            jax.ShapeDtypeStruct((rows, width), jnp.bfloat16),
            head_rows,
            head_rows,
            head_rows,
            jax.ShapeDtypeStruct((rows, heads * size), jnp.bfloat16),
            jax.ShapeDtypeStruct((rows, LANES), jnp.float32),
        ],
        in_specs=[pl.BlockSpec(memory_space=pltpu.SMEM)] + [whole] * 4,
        out_specs=[whole] * 6,
        compiler_params=pltpu.CompilerParams(vmem_limit_bytes=56 * 2**20),
        cost_estimate=cost(24),
    )(big_images, tokens, norm_gain.reshape(1, -1), w_qkv, qk_gains)


def backward_kernel(
    flag_ref, q_ref, k_ref, v_ref, do_ref, inv_ref, qk_ref, joined_ref, small_ref, dq_ref, dk_ref, dv_ref, turned_ref
):
    pair = pl.program_id(0)
    rows = inv_ref.shape[0]
    padded = q_ref.shape[1]
    tile = 2 * PATCHES
    size = qk_ref.shape[1]
    scale = size**-0.5
    zeros = jnp.zeros((1, LANES - size), jnp.float32)
    q_gain = wide(qk_ref[0:1, :])
    k_gain = wide(qk_ref[1:2, :])
    q_back = jnp.concatenate([1.0 / (q_gain * (scale * LOG2E)), zeros], axis=1)
    k_back = jnp.concatenate([1.0 / k_gain, zeros], axis=1)
    q_gain = jnp.concatenate([q_gain, zeros], axis=1)
    k_gain = jnp.concatenate([k_gain, zeros], axis=1)

    def attend(side, _, big):
        for start in range(0, rows, tile):
            here = slice(start, start + tile)
            if big:
                over = slice(0, padded)
            else:
                begin, length = window_of(start // tile)
                over = slice(begin, begin + length)
            keys = k_ref[side, here, :]
            queries = q_ref[side, over, :]
            grads = do_ref[side, over, :]
            scores = times_t(keys, queries)
            if not big:
                scores = jnp.where(pair_mask(start // tile, scores.shape, over.start), scores, -1e30)
            probs = jnp.exp2(scores)
            grad_probs = times_t(v_ref[side, here, :], grads)
            grad_scores = low(probs * grad_probs)
            dv_ref[side, here, :] = times(low(probs), grads)
            dk_ref[side, here, :] = times(grad_scores, queries)
            more = rows_t(keys, grad_scores)
            if big and start == 0:
                dq_ref[side, :, over] = more
            elif big:
                dq_ref[side, :, over] += more
            else:
                place = lane_of(more.shape) - (start - over.start)
                dq_ref[side, :, over] = jnp.where(
                    (place >= 0) & (place < tile), more, dq_ref[side, :, over]
                )
        return 0

    @pl.when(flag_ref[0] > 0)
    def _():
        lax.fori_loop(0, 2, functools.partial(attend, big=True), 0)

    @pl.when(flag_ref[0] <= 0)
    def _():
        lax.fori_loop(0, 2, functools.partial(attend, big=False), 0)

    @pl.when(pair == 0)
    def _():
        small_ref[...] = jnp.zeros_like(small_ref)

    lane = lane_of((tile, LANES))
    first = lane < 64
    shape = (2 * LANES, 2 * LANES)
    row, column = row_of(shape), lane_of(shape)
    means = (row // LANES == column // LANES) & (row % LANES < size)
    means = low(jnp.where(means, 1.0 / size, 0.0))
    gains = jnp.concatenate([q_gain * scale, k_gain * math.log(2.0)], axis=1)
    factors = jnp.concatenate([jnp.full_like(q_gain, scale), jnp.full_like(k_gain, math.log(2.0))], axis=1)
    backs = jnp.concatenate([q_back, k_back], axis=1)
    for side in range(2):
        turned_ref[side] = dq_ref[side].T
    for start in range(0, rows, tile):
        here = slice(start, start + tile)
        inverse_first, inverse_second = two_terms(inv_ref[here, :])
        blocks = []
        for side in range(2):
            shape = (LANES, 2 * LANES)
            source = 6 * pair + 3 * side + lane_of(shape) // LANES
            pick = low(jnp.where(row_of(shape) == source, 1.0, 0.0))
            inverse = times(inverse_first, pick) + times(inverse_second, pick)
            hat = jnp.concatenate([q_ref[side, here, :], k_ref[side, here, :]], axis=1)
            hat = wide(hat) * backs
            grad = jnp.concatenate([turned_ref[side, here, :], dk_ref[side, here, :]], axis=1)
            small_ref[0:1, :] += jnp.sum(grad * hat, axis=0, keepdims=True) * factors
            grad = grad * gains
            inner = times(low(grad * hat), means)
            grad = inverse * (grad - times(low(grad), means) - hat * inner)
            blocks.append((grad[:, :LANES], grad[:, LANES:], dv_ref[side, here, :]))
        (q0, k0, v0), (q1, k1, v1) = blocks
        joined_ref[here, 0:128] = low(jnp.where(first, q0, other_half(k0)))
        joined_ref[here, 128:256] = low(jnp.where(first, v0, other_half(q1)))
        joined_ref[here, 256:384] = low(jnp.where(first, k1, other_half(v1)))


def backward(big_images, q_rows, k_rows, v_rows, do_rows, inverses, qk_gains):
    heads, padded, _ = q_rows.shape
    rows = inverses.shape[0]
    pair_spec = pl.BlockSpec((2, padded, LANES), lambda pair: (pair, 0, 0))
    return pl.pallas_call(
        backward_kernel,
        name="backward",
        grid=(heads // 2,),
        out_shape=[
            jax.ShapeDtypeStruct((rows, heads * 3 * LANES // 2), jnp.bfloat16),
            jax.ShapeDtypeStruct((8, 2 * LANES), jnp.float32),
        ],
        in_specs=[pl.BlockSpec(memory_space=pltpu.SMEM)]
        + [pair_spec] * 4
        + [pl.BlockSpec((rows, LANES), lambda pair: (0, 0)), pl.BlockSpec(qk_gains.shape, lambda pair: (0, 0))],
        out_specs=[
            pl.BlockSpec((rows, 3 * LANES), lambda pair: (0, pair)),
            pl.BlockSpec((8, 2 * LANES), lambda pair: (0, 0)),
        ],
        scratch_shapes=[
            VMEM((2, LANES, padded), jnp.float32),
            VMEM((2, rows, LANES), jnp.float32),
            VMEM((2, rows, LANES), jnp.float32),
            VMEM((2, padded, LANES), jnp.float32),
        ],
        compiler_params=pltpu.CompilerParams(vmem_limit_bytes=56 * 2**20),
        cost_estimate=cost(36),
    )(big_images, q_rows, k_rows, v_rows, do_rows, inverses, qk_gains)


def in_order(mine, other):
    first = lax.axis_index("hg") == 0
    return jnp.where(first, mine, other), jnp.where(first, other, mine)


def dense_kernel(count, tiles, normed_ref, mine_ref, other_ref, *refs):
    w_in_refs, w_back_refs = refs[:count], refs[count : 2 * count]
    refs = refs[2 * count :]
    part_ref, grad_ref, dy_ref = refs[:3]
    grad_refs, refs = refs[3 : 3 + count], refs[3 + count :]
    normed_rows, dy_rows = refs[:2]
    act_refs, gup_refs = refs[2 : 2 + count], refs[2 + count :]
    step = pl.program_id(0)
    half = mine_ref.shape[1]
    curve = math.sqrt(2.0 / math.pi)
    normed = normed_ref[...]
    first, second = in_order(mine_ref[...], other_ref[...])
    dy_ref[:, :half], dy_ref[:, half:] = first, second
    dy = dy_ref[...]
    normed_rows[step] = normed
    dy_rows[step] = dy
    for w_in_ref, w_back_ref, act_ref, gup_ref in zip(w_in_refs, w_back_refs, act_refs, gup_refs):
        columns = w_in_ref.shape[1]
        width = min(256, columns)
        for at in range(0, columns, width):
            cols = slice(at, min(at + width, columns))
            up = times(normed, w_in_ref[:, cols])
            grad_act = times(dy, w_back_ref[:, cols])
            square = up * up
            bent = jnp.tanh(up * (curve + (curve * 0.044715) * square))
            gate = 0.5 + 0.5 * bent
            act = up * gate
            slope = gate + act * ((1.0 - gate) * (2 * curve + (6 * curve * 0.044715) * square))
            act_ref[step, :, cols] = low(act)
            gup_ref[step, :, cols] = low(grad_act * slope)
    total, grad = None, None
    for act_ref, w_back_ref, gup_ref, w_in_ref in zip(act_refs, w_back_refs, gup_refs, w_in_refs):
        part = times_t(act_ref[step], w_back_ref[...])
        total = part if total is None else total + part
        part = times_t(gup_ref[step], w_in_ref[...])
        grad = part if grad is None else grad + part
    part_ref[...] = total
    grad_ref[...] = low(grad)

    @pl.when(step == tiles - 1)
    def _():
        for act_ref, gup_ref, ref in zip(act_refs, gup_refs, grad_refs):
            columns = act_ref.shape[2]
            for left, right, at in ((normed_rows, gup_ref, 0), (dy_rows, act_ref, columns)):
                rows = tiles * left.shape[1]
                total = rows_t(left[...].reshape(rows, -1), right[...].reshape(rows, columns))
                ref[:, at : at + columns] = total.astype(ref.dtype)


def dense(normed, mine, other, w_in_pieces, w_back_pieces):
    rows, width = normed.shape
    tile = 2 * PATCHES
    tiles = rows // tile
    count = len(w_in_pieces)
    shape = jax.ShapeDtypeStruct
    sizes = [piece.shape[1] for piece in w_in_pieces]
    kinds = [jnp.float32] * (count - 1) + [jnp.bfloat16] if count > 1 else [jnp.float32]
    row_tile = lambda columns: pl.BlockSpec((tile, columns), lambda step: (step, 0))
    fixed = lambda columns: pl.BlockSpec((width, columns), lambda step: (0, 0))
    once = lambda columns: pl.BlockSpec((width, columns), lambda step: (0, 0), pipeline_mode=pl.Buffered(1))
    return pl.pallas_call(
        functools.partial(dense_kernel, count, tiles),
        name="dense",
        grid=(tiles,),
        out_shape=[
            shape((rows, width), jnp.float32),
            shape((rows, width), jnp.bfloat16),
            shape((rows, width), jnp.bfloat16),
        ]
        + [shape((width, 2 * size), kind) for size, kind in zip(sizes, kinds)],
        in_specs=[row_tile(width), row_tile(width // 2), row_tile(width // 2)]
        + [once(size) for size in sizes] * 2,
        out_specs=[row_tile(width)] * 3 + [fixed(2 * size) for size in sizes],
        scratch_shapes=[VMEM((tiles, tile, width), jnp.bfloat16)] * 2
        + [VMEM((tiles, tile, size), jnp.bfloat16) for size in sizes] * 2,
        compiler_params=pltpu.CompilerParams(vmem_limit_bytes=60 * 2**20),
        cost_estimate=cost(24),
    )(normed, mine, other, *w_in_pieces, *w_back_pieces)


def outputs_kernel(part_ref, tok_ref, att_ref, mine_ref, other_ref, w_out_ref, keep_ref, send_ref, do_ref):
    tile, width = part_ref.shape
    half = width // 2
    heads, padded, _ = do_ref.shape
    lane = lane_of((tile, LANES))
    attended = att_ref[...]
    left = times_t(attended, w_out_ref[...]) + part_ref[...]
    token = tok_ref[...]
    keep, send = in_order(left[:, :half], left[:, half:])
    keep_ref[...] = keep + in_order(wide(token[:, :half]), wide(token[:, half:]))[0]
    send_ref[...] = low(send)
    first, second = in_order(mine_ref[...], other_ref[...])
    grad_att = times(first, w_out_ref[:half, :]) + times(second, w_out_ref[half:, :])
    shape = (LANES, 2 * LANES)
    row, column = row_of(shape), lane_of(shape)
    inners = (row // 64 == column // LANES) & (column % LANES >= 64) & (column % LANES < 67)
    inners = low(jnp.where(inners, -1.0, 0.0))
    found = []
    for pair in range(heads // 2):
        cols = slice(pair * LANES, pair * LANES + LANES)
        low_block = wide(low(grad_att[:, cols]))
        weighed, rest = two_terms(low_block * wide(attended[:, cols]))
        inner = times(weighed, inners) + times(rest, inners)
        for side in range(2):
            value = low_block if side == 0 else other_half(low_block)
            term = spread_terms(inner[:, side * LANES : (side + 1) * LANES])
            found.append(low(jnp.where(lane < 64, value, term)))
    for step in range(3):

        @pl.when(pl.program_id(0) == step)
        def _(step=step):
            for head in range(heads):
                do_ref[head, step * tile : (step + 1) * tile, :] = found[head]
            if step == 2:
                do_ref[:, 3 * tile :, :] = jnp.zeros((heads, padded - 3 * tile, LANES), jnp.bfloat16)


def outputs(part, tokens, attended, mine, other, w_out_t):
    rows, width = tokens.shape
    tile = 2 * PATCHES
    heads = w_out_t.shape[1] // 64
    padded = -(-rows // 256) * 256
    shape = jax.ShapeDtypeStruct
    row_tile = lambda columns: pl.BlockSpec((tile, columns), lambda step: (step, 0))
    return pl.pallas_call(
        outputs_kernel,
        name="outputs",
        grid=(rows // tile,),
        out_shape=[
            shape((rows, width // 2), jnp.float32),
            shape((rows, width // 2), jnp.bfloat16),
            shape((heads, padded, LANES), jnp.bfloat16),
        ],
        in_specs=[row_tile(columns) for columns in (width, width, width // 2, width // 2, width // 2)]
        + [pl.BlockSpec(w_out_t.shape, lambda step: (0, 0))],
        out_specs=[
            row_tile(width // 2),
            row_tile(width // 2),
            pl.BlockSpec((heads, padded, LANES), lambda step: (0, 0, 0)),
        ],
        compiler_params=pltpu.CompilerParams(vmem_limit_bytes=56 * 2**20),
        cost_estimate=cost(6),
    )(part, tokens, attended, mine, other, w_out_t)


def features_kernel(joined_ref, w_ref, mlp_ref, tok_ref, sent_ref, gain_ref):
    grad = times_t(joined_ref[...], w_ref[...]) + wide(mlp_ref[...])
    sent_ref[...] = low(grad)
    x = wide(tok_ref[...])
    x = x - jnp.mean(x, axis=1, keepdims=True)
    x = x * lax.rsqrt(jnp.mean(x * x, axis=1, keepdims=True) + EPSILON)

    @pl.when(pl.program_id(0) == 0)
    def _():
        gain_ref[...] = jnp.zeros_like(gain_ref)

    gain_ref[0:1, :] += jnp.sum(grad * x, axis=0, keepdims=True)


def features(first, count, grad_joined, w_qkv, grad_mlp, tokens):
    rows, width = tokens.shape
    tile = 2 * PATCHES
    row_tile = lambda columns: pl.BlockSpec((tile, columns), lambda step: (step + first, 0))
    return pl.pallas_call(
        features_kernel,
        name="features",
        grid=(count,),
        out_shape=[
            jax.ShapeDtypeStruct((tile * count, width), jnp.bfloat16),
            jax.ShapeDtypeStruct((8, width), jnp.float32),
        ],
        in_specs=[
            row_tile(grad_joined.shape[1]),
            pl.BlockSpec(w_qkv.shape, lambda step: (0, 0)),
            row_tile(width),
            row_tile(width),
        ],
        out_specs=[
            pl.BlockSpec((tile, width), lambda step: (step, 0)),
            pl.BlockSpec((8, width), lambda step: (0, 0)),
        ],
        compiler_params=pltpu.CompilerParams(vmem_limit_bytes=40 * 2**20),
        cost_estimate=cost(0.3 * count),
    )(grad_joined, w_qkv, grad_mlp, tokens)


def weights_kernel(*refs):
    keep_ref, send_ref = refs[-2:]
    groups, rows, _ = keep_ref.shape
    first_side = lax.axis_index("hid") == 0
    at = 0
    for left_ref, right_ref in zip(refs[:-2:2], refs[1:-2:2]):
        total = rows_t(left_ref[...], right_ref[...])
        cols = slice(at, at + total.shape[1])
        at = cols.stop
        for group in range(groups):
            even, odd = (total[(2 * group + side) * rows : (2 * group + side + 1) * rows] for side in (0, 1))
            keep_ref[group, :, cols] = jnp.where(first_side, even, odd)
            send_ref[group, :, cols] = low(jnp.where(first_side, odd, even))


def weights(*pairs):
    whole = pl.BlockSpec(memory_space=VMEM)
    groups = lax.axis_size("dp")
    columns = sum(right.shape[1] for right in pairs[1::2])
    shape = (groups, pairs[0].shape[1] // (2 * groups), columns)
    return pl.pallas_call(
        weights_kernel,
        name="weights",
        out_shape=[jax.ShapeDtypeStruct(shape, jnp.float32), jax.ShapeDtypeStruct(shape, jnp.bfloat16)],
        in_specs=[whole] * len(pairs),
        out_specs=[whole] * 2,
        compiler_params=pltpu.CompilerParams(vmem_limit_bytes=48 * 2**20),
        cost_estimate=cost(1),
    )(*pairs)


def tokens_kernel(sent_ref, came_ref, tok_ref, gain_ref, mine_ref, other_ref, *refs):
    out_ref = refs[-1]
    half = mine_ref.shape[1]
    grad = (wide(sent_ref[...]) + wide(came_ref[...])) * wide(gain_ref[...])
    x = wide(tok_ref[...])
    x = x - jnp.mean(x, axis=1, keepdims=True)
    inverse = lax.rsqrt(jnp.mean(x * x, axis=1, keepdims=True) + EPSILON)
    x = x * inverse
    inner = jnp.mean(grad * x, axis=1, keepdims=True)
    grad = inverse * (grad - jnp.mean(grad, axis=1, keepdims=True) - x * inner)
    first, second = in_order(wide(mine_ref[...]), wide(other_ref[...]))
    out_ref[:, :half] = low(grad[:, :half] + first)
    out_ref[:, half:] = low(grad[:, half:] + second)


def token_rows(first, sent, came, tokens, norm_gain, mine, other, before):
    rows, width = tokens.shape
    tile = 2 * PATCHES
    count = sent.shape[0] // tile
    near = lambda columns: pl.BlockSpec((tile, columns), lambda step: (step, 0))
    far = lambda columns: pl.BlockSpec((tile, columns), lambda step: (step + first, 0))
    more = [] if before is None else [before]
    return pl.pallas_call(
        tokens_kernel,
        name="token_rows",
        grid=(count,),
        out_shape=jax.ShapeDtypeStruct((rows, width), jnp.bfloat16),
        in_specs=[
            near(width),
            near(width),
            far(width),
            pl.BlockSpec((1, width), lambda step: (0, 0)),
            far(width // 2),
            far(width // 2),
        ]
        + [pl.BlockSpec(memory_space=pl.ANY)] * len(more),
        out_specs=far(width),
        input_output_aliases={6: 0} if more else {},
        compiler_params=pltpu.CompilerParams(vmem_limit_bytes=40 * 2**20),
        cost_estimate=cost(0.3 * count),
    )(sent, came, tokens, norm_gain.reshape(1, -1), mine, other, *more)


def swap(value, axis, bit):
    size = lax.axis_size(axis)
    return lax.ppermute(value, axis, [(place, place ^ bit) for place in range(size)])


def bits_of(axis):
    size = lax.axis_size(axis)
    return [1 << place for place in range(size.bit_length() - 1)]


def gather_pieces(block, axis):
    pieces = [block]
    for bit in bits_of(axis):
        held = pieces[0] if len(pieces) == 1 else jnp.concatenate(pieces, axis=1)
        pieces.append(swap(held, axis, bit))
    return pieces


def scatter_pieces(pieces, axis):
    for bit in reversed(bits_of(axis)):
        sent = swap(low(pieces[-1]), axis, bit)
        kept, at, half = [], 0, sent.shape[1] // 2
        for piece in pieces[:-1]:
            size = piece.shape[1] // 2
            parts = (sent[:, at : at + size], sent[:, half + at : half + at + size])
            kept.append(wide(piece) + wide(jnp.concatenate(parts, axis=1) if size < half else sent))
            at += size
        pieces = kept
    return pieces[0]


def row_blocks(*pairs):
    groups, sides = lax.axis_size("dp"), lax.axis_size("hid")
    if sides == 2 and pairs[0].shape[1] % (16 * groups * sides) == 0:
        keep, send = weights(*pairs)
        return keep + wide(swap(send, "hid", 1))
    total = jnp.concatenate([rows_t(*pairs[at : at + 2]) for at in range(0, len(pairs), 2)], axis=1)
    shaped = total.reshape(groups, sides, -1, total.shape[1])
    shaped = shaped[:, lax.axis_index("hid") ^ jnp.arange(sides)]
    for bit in reversed(bits_of("hid")):
        shaped = shaped[:, :bit] + wide(swap(low(shaped[:, bit:]), "hid", bit))
    return shaped[:, 0]


def halve(shaped):
    count, rows, columns = shaped.shape
    shaped = shaped.reshape(count // 2, 2, rows, columns)
    odd = (lax.axis_index("dp") & 1) > 0
    sent = low(jnp.where(odd, shaped[:, 0], shaped[:, 1]))
    return jnp.where(odd, shaped[:, 1], shaped[:, 0]), swap(sent, "dp", 1)


def sum_rest(kept, came):
    count = lax.axis_size("dp")
    groups = [list(range(odd, count, 2)) for odd in (0, 1)]
    total = low(wide(kept) + wide(came))
    total = lax.all_to_all(total, "dp", 0, 0, axis_index_groups=groups, tiled=True)
    return jnp.sum(wide(total), axis=0)


def sum_far(kept, came):
    total = low(wide(kept) + wide(came))
    me = lax.axis_index("dp") // 2
    terms = [lax.dynamic_index_in_dim(total, me, keepdims=False)]
    for step in range(1, total.shape[0]):
        block = lax.dynamic_index_in_dim(total, me ^ step, keepdims=False)
        terms.append(swap(block, "dp", 2 * step))
    return sum(wide(term) for term in terms)


def sum_everywhere(value, axes):
    for axis in axes:
        for bit in bits_of(axis):
            value = value + swap(value, axis, bit)
    return value


def shards(tokens, big_images, norm_gain, w_qkv, qk_gains, w_out_t, w_in, w_back, cotangent):
    width = tokens.shape[1]
    size = qk_gains.shape[1]
    groups = lax.axis_size("dp")
    other = swap(cotangent, "hg", 1)
    w_in_pieces = gather_pieces(w_in, "hid")
    w_back_pieces = gather_pieces(w_back, "hid")
    normed, q_rows, k_rows, v_rows, attended, inverses = forward(
        big_images, tokens, norm_gain, w_qkv, qk_gains
    )
    part, grad_mlp, grad_out, *grads = dense(normed, cotangent, other, w_in_pieces, w_back_pieces)
    kept, sent, do_rows = outputs(part, tokens, attended, cotangent, other, w_out_t)
    out_came = swap(sent, "hg", 1)
    mlp_kept, mlp_came = halve(scatter_pieces(grads, "hid").reshape(groups, width // groups, -1))
    do_rows, mlp_kept = lax.optimization_barrier((do_rows, mlp_kept))

    grad_joined, qk_part = backward(big_images, q_rows, k_rows, v_rows, do_rows, inverses, qk_gains)
    grad_joined, out_came, mlp_came = lax.optimization_barrier((grad_joined, out_came, mlp_came))
    mine, gain_part = features(0, tokens.shape[0] // (2 * PATCHES), grad_joined, w_qkv, grad_mlp, tokens)
    came = swap(mine, "hg", 1)

    def weight_sums(normed, grad_joined, grad_out, attended, mlp_kept, mlp_came, gain_part, qk_part, kept, out_came):
        blocks = row_blocks(normed, grad_joined, grad_out, attended)
        mlp_grads = sum_rest(mlp_kept, mlp_came)
        both = sum_far(*halve(blocks))
        small = jnp.concatenate([gain_part[0], qk_part[0, :size], qk_part[0, LANES : LANES + size]])
        small = sum_everywhere(small, ("hid", "dp"))
        return mlp_grads, both, small, low(kept + wide(out_came))

    def no_sums(*operands):
        return tuple(jnp.zeros(kind.shape, kind.dtype) for kind in kinds)

    operands = (normed, grad_joined, grad_out, attended, mlp_kept, mlp_came, gain_part, qk_part, kept, out_came)
    kinds = jax.eval_shape(weight_sums, *operands)
    mlp_grads, both, small, output = lax.cond(big_images[0] >= 0, weight_sums, no_sums, *operands)
    came, small = lax.optimization_barrier((came, small))
    small = sum_everywhere(small, ("hg",))
    w_in_grad, w_back_grad = jnp.split(mlp_grads, 2, axis=1)
    w_qkv_grad, w_out_t_grad = both[:, : w_qkv.shape[1]], both[:, w_qkv.shape[1] :]
    own = lax.axis_index("dp") * lax.axis_size("hid") + lax.axis_index("hid")
    gain_rows = width // (groups * lax.axis_size("hid"))
    norm_gain_grad = lax.dynamic_slice_in_dim(small, own * gain_rows, gain_rows, 0)
    qk_gains_grad = small[width:].reshape(2, size)
    token_grad = token_rows(0, mine, came, tokens, norm_gain, cotangent, other, None)
    return (
        output,
        token_grad,
        norm_gain_grad,
        w_qkv_grad,
        qk_gains_grad,
        w_out_t_grad,
        w_in_grad,
        w_back_grad,
    )


def solution(mesh):
    return jax.shard_map(
        shards,
        mesh=mesh,
        in_specs=(
            P(("dp", "hid"), None),
            P(("dp", "hid")),
            P(),
            P(None, "hg"),
            P(),
            P(None, "hg"),
            P(None, ("hg", "hid")),
            P(None, ("hg", "hid")),
            P(("dp", "hid"), "hg"),
        ),
        out_specs=(
            P(("dp", "hid"), "hg"),
            P(("dp", "hid"), None),
            P(("dp", "hid")),
            P(("dp", "hid"), "hg"),
            P(),
            P(("dp", "hid"), "hg"),
            P("dp", ("hg", "hid")),
            P("dp", ("hg", "hid")),
        ),
        check_vma=False,
    )
```

profile of v0, /device:TPU:0, one launch (start us, length us, event | category | flops | bytes accessed | tf_op | source)
XLA Modules:
  0.0 193.5 jit_solution(10729874919831762831)
XLA Ops:
  0.6 3.0 %collective-permute-start.9 = (bf16[1176,384]{1,0:T(8,128)(2,1)}, bf16[1176,384]{1,0:T(8,128)(2,1)S(1)}, u32[]{:S(2)}, u32[]{:S(2)}) collective-permute-start(bf16[1176,384]{1,0:T(8,128)(2,1)} %mine_ref.5), channel_id=1, source_target_pairs={{0,2},{2,0},{1,3},{3,1},{4,6},{6,4},{5,7},{7,5},{8,10},{10,8},{9,1... | collective-permute-start | bytes 2709512 | tf_op jit(solution)/shard_map/ppermute | solution.py:612
  6.1 19.0 %forward.1 = (bf16[1176,768]{1,0:T(8,128)(2,1)S(1)}, bf16[6,1280,128]{2,1,0:T(8,128)(2,1)}, bf16[6,1280,128]{2,1,0:T(8,128)(2,1)}, bf16[6,1280,128]{2,1,0:T(8,12...) custom-call(s32[1]{0:T(128)S(6)} %copy.41.flag_ref, bf16[1176,768]{1,0:T(8,128)(2,1)} %tok_ref.7, ...), custom_call_target="tpu_custom_call" | custom-call | flops 24000000000 | bytes 1048576 | tf_op jit(solution)/shard_map/forward/pallas_call | solution.py:203
  26.4 25.9 %dense.1 = (f32[1176,768]{1,0:T(8,128)}, bf16[1176,768]{1,0:T(8,128)(2,1)}, bf16[1176,768]{1,0:T(8,128)(2,1)}, f32[768,1536]{1,0:T(8,128)}, bf16[768,1536]{1,0:T(8,128)(2,1)}) custom-call(bf16[1176,768]{1,0:T(8,128)(2,1)S(1)} %get-tuple-element.78.normed_ref, bf16[1176,384]{1,0:T(8,128)(2,1)} %mine_ref.5, bf16[1176,384]{1,0:T(8,128)(2,1)} %copy-done.5, ...), custom_call_target="tpu_custom_call" | custom-call | flops 24000000000 | bytes 1048576 | tf_op jit(solution)/shard_map/dense/pallas_call | solution.py:410
  52.5 9.1 %outputs.1 = (f32[1176,384]{1,0:T(8,128)}, bf16[1176,384]{1,0:T(8,128)(2,1)}, bf16[6,1280,128]{2,1,0:T(8,128)(2,1)}) custom-call(f32[1176,768]{1,0:T(8,128)} %get-tuple-element.79.part_ref, bf16[1176,768]{1,0:T(8,128)(2,1)} %tok_ref.7, bf16[1176,384]{1,0:T(8,128)(2,1)} %get-tuple-element.80.att_ref, bf16[1176,384]{1,0:T(8,128)(2,1)} %mine_ref.5, ...), custom_call_target="tpu_custom_call" | custom-call | flops 6000000000 | bytes 1048576 | tf_op jit(solution)/shard_map/outputs/pallas_call | solution.py:474
  63.1 1.8 select_bitcast_fusion
  66.2 1.6 collective-permute-start.14
  67.7 18.8 %backward.1 = (bf16[1176,1152]{1,0:T(8,128)(2,1)}, f32[8,256]{1,0:T(8,128)S(1)}) custom-call(s32[1]{0:T(128)S(6)} %copy.41.flag_ref, bf16[6,1280,128]{2,1,0:T(8,128)(2,1)} %get-tuple-element.75.q_ref, bf16[6,1280,128]{2,1,0:T(8,128)(2,1)} %get-tuple-element.76.k_ref, bf16[6,1280,128]{2,1,0:T(8,128)(2,1)} %get-tuple-element.77.v_ref, ...), custom_call_target="tpu_custom_call" | custom-call | flops 35999997952 | bytes 1048576 | tf_op jit(solution)/shard_map/backward/pallas_call | solution.py:319
  86.6 7.9 %collective-permute-done.14 = bf16[4,96,1536]{2,1,0:T(8,128)(2,1)S(1)} collective-permute-done((bf16[4,96,1536]{2,1,0:T(8,128)(2,1)}, bf16[4,96,1536]{2,1,0:T(8,128)(2,1)S(1)}, u32[]{:S(2)}, u32[]{:S(2)}) %collective-permute-start.14) | collective-permute-done | bytes 1179680 | tf_op jit(solution)/shard_map/ppermute | solution.py:612
  94.4 6.0 %features.1 = (bf16[1176,768]{1,0:T(8,128)(2,1)}, f32[8,768]{1,0:T(8,128)S(1)}) custom-call(bf16[1176,1152]{1,0:T(8,128)(2,1)} %get-tuple-element.90.joined_ref, bf16[768,1152]{1,0:T(8,128)(2,1)S(1)} %copy-done.3, bf16[1176,768]{1,0:T(8,128)(2,1)S(1)} %copy-done.2, bf16[1176,768]{1,0:T(8,128)(2,1)S(1)} %copy-done), custom_call_target="tpu_custom_call" | custom-call | flops 900000000 | bytes 1048576 | tf_op jit(solution)/shard_map/features/pallas_call | solution.py:513
  100.4 1.5 collective-permute-start.15
  101.9 82.5 %conditional.1 = (f32[96,1536]{1,0:T(8,128)}, f32[48,1536]{1,0:T(8,128)}, f32[896]{0:T(1024)S(1)}, bf16[1176,384]{1,0:T(8,128)(2,1)}, f32[96,768]{1,0:T(8,128)},...) conditional(s32[]{:T(128)} %bitcast.10, () %tuple.23, (bf16[4,96,1536]{2,1,0:T(8,128)(2,1)}, ...), branch_computations={%region_0.1_spmd, %region_1.3_spmd} | conditional | flops 1007333888 | bytes 78652360 | solution.py:721
  101.9 8.0 %weights.1 = (f32[8,48,1536]{2,1,0:T(8,128)S(1)}, bf16[8,48,1536]{2,1,0:T(8,128)(2,1)}) custom-call(bf16[1176,768]{1,0:T(8,128)(2,1)} %get-tuple-element.26.refs_0_, bf16[1176,1152]{1,0:T(8,128)(2,1)} %get-tuple-element.27.refs_1_, bf16[1176,768]{1,0:T(8,128)(2,1)} %get-tuple-element.28.refs_2_, bf16[1176,384]{1,0:T(8,128)(2,1)} %get-tuple-element.29.refs_3_), custom_call_target="tpu_custom_call" | custom-call | flops 1000000000 | bytes 1048576 | tf_op jit(solution)/shard_map/cond/branch_1_fun/weights/pallas_call | solution.py:556
  109.9 1.4 copy-done.1
  111.9 1.9 collective-permute-done.5
  113.9 1.5 collective-permute-start.6
  115.4 2.1 %collective-permute-done.6 = f32[896]{0:T(1024)S(1)} collective-permute-done((f32[896]{0:T(1024)S(1)}, f32[896]{0:T(1024)S(1)}, u32[]{:S(2)}, u32[]{:S(2)}) %collective-permute-start.6) | collective-permute-done | bytes 3616 | tf_op jit(solution)/shard_map/cond/branch_1_fun/ppermute | solution.py:612
  117.5 1.6 collective-permute-start.7
  119.1 1.4 add_convert_fusion
  120.4 15.3 %all-to-all-start = ((bf16[4,96,1536]{2,1,0:T(8,128)(2,1)}), bf16[4,96,1536]{2,1,0:T(8,128)(2,1)}, u32[]{:S(2)}, u32[]{:S(2)}) async-start(bf16[4,96,1536]{2,1,0:T(8,128)(2,1)} %add_convert_fusion), calls=%async_computation | async-start | bytes 2359296 | tf_op jit(solution)/shard_map/cond/branch_1_fun/all_to_all | solution.py:666
  135.7 2.9 %collective-permute-start.8 = (f32[896]{0:T(1024)S(1)}, f32[896]{0:T(1024)S(1)}, u32[]{:S(2)}, u32[]{:S(2)}) collective-permute-start(f32[896]{0:T(1024)S(1)} %add.52), channel_id=1, source_target_pairs={{0,16},{4,20},{8,24},{12,28},{16,0},{20,4},{24,8},{28,12},{1,17},{... | collective-permute-start | bytes 10760 | tf_op jit(solution)/shard_map/cond/branch_1_fun/ppermute | solution.py:612
  138.7 2.4 %convert_add_fusion = f32[8,48,1536]{2,1,0:T(8,128)S(1)} fusion(f32[8,48,1536]{2,1,0:T(8,128)} %copy-done.1, bf16[8,48,1536]{2,1,0:T(8,128)(2,1)} %collective-permute-done), kind=kLoop, calls=%fused_computation | loop fusion | flops 1179648 | bytes 5898240 | tf_op jit(solution)/shard_map/cond/branch_1_fun/add | solution.py:645
  141.1 1.4 copy-done.8
  143.2 2.3 %add_convert_fusion.1 = bf16[1176,384]{1,0:T(8,128)(2,1)} fusion(f32[1176,384]{1,0:T(8,128)S(1)} %copy-done.11, bf16[1176,384]{1,0:T(8,128)(2,1)} %get-tuple-element.35), kind=kLoop, calls=%fused_computation.3 | loop fusion | flops 1354752 | bytes 3612672 | tf_op jit(solution)/shard_map/cond/branch_1_fun/convert_element_type | solution.py:42
  145.5 18.5 %collective-permute-done.8 = f32[896]{0:T(1024)S(1)} collective-permute-done((f32[896]{0:T(1024)S(1)}, f32[896]{0:T(1024)S(1)}, u32[]{:S(2)}, u32[]{:S(2)}) %collective-permute-start.8) | collective-permute-done | bytes 3616 | tf_op jit(solution)/shard_map/cond/branch_1_fun/ppermute | solution.py:612
  164.0 2.1 %fusion = bf16[4,48,1536]{2,1,0:T(8,128)(2,1)S(1)} fusion(bf16[4,48,1536]{2,1,0:T(8,128)(2,1)} %collective-permute-done.1, f32[4,2,48,1536]{3,2,1,0:T(8,128)} %bitcast.61, pred[]{:T(512)S(6)} %gt.4), kind=kLoop, calls=%fused_computation.7 | loop fusion | flops 1179648 | bytes 3538945 | tf_op jit(solution)/shard_map/cond/branch_1_fun/convert_element_type | solution.py:42
  166.8 2.0 %collective-permute-start.3 = (bf16[48,1536]{1,0:T(8,128)(2,1)}, bf16[48,1536]{1,0:T(8,128)(2,1)}, u32[]{:S(2)}, u32[]{:S(2)}) collective-permute-start(bf16[48,1536]{1,0:T(8,128)(2,1)} %get-tuple-element.110), channel_id=1, source_target_pairs={{0,16},{4,20},{8,24},{12,28},{16,0},{20,4},{24,8},{28,12},{1,17},{... | collective-permute-start | bytes 442376 | tf_op jit(solution)/shard_map/cond/branch_1_fun/ppermute | solution.py:612
  168.9 2.4 %collective-permute-start.4 = (bf16[48,1536]{1,0:T(8,128)(2,1)}, bf16[48,1536]{1,0:T(8,128)(2,1)}, u32[]{:S(2)}, u32[]{:S(2)}) collective-permute-start(bf16[48,1536]{1,0:T(8,128)(2,1)} %get-tuple-element.109), channel_id=1, source_target_pairs={{0,24},{4,28},{8,16},{12,20},{16,8},{20,12},{24,0},{28,4},{1,25},{... | collective-permute-start | bytes 442376 | tf_op jit(solution)/shard_map/cond/branch_1_fun/ppermute | solution.py:612
  171.2 2.3 %convert_reduce_fusion = f32[96,1536]{1,0:T(8,128)} fusion(bf16[4,96,1536]{2,1,0:T(8,128)(2,1)} %all-to-all-done), kind=kLoop, calls=%fused_computation.1 | loop fusion | flops 1032192 | bytes 1769472 | tf_op jit(solution)/shard_map/cond/branch_1_fun/reduce_sum | solution.py:667
  173.5 1.9 fusion.5
  175.4 5.4 %collective-permute-done.3 = bf16[48,1536]{1,0:T(8,128)(2,1)} collective-permute-done((bf16[48,1536]{1,0:T(8,128)(2,1)}, bf16[48,1536]{1,0:T(8,128)(2,1)}, u32[]{:S(2)}, u32[]{:S(2)}) %collective-permute-start.3) | collective-permute-done | bytes 147488 | tf_op jit(solution)/shard_map/cond/branch_1_fun/ppermute | solution.py:612
  180.8 1.8 fusion.3
  186.8 5.4 %token_rows.1 = bf16[1176,768]{1,0:T(8,128)(2,1)} custom-call(bf16[1176,768]{1,0:T(8,128)(2,1)} %get-tuple-element.98.sent_ref, bf16[1176,768]{1,0:T(8,128)(2,1)} %collective-permute-done.15.came_ref, bf16[1176,768]{1,0:T(8,128)(2,1)S(1)} %copy-done, bf16[1,768]{1,0:T(2,128)(2,1)S(1)} %copy-done.7, bf16[1176,384]{1,0:T(8,128)(2,1)S(1)} %copy-done.4, ...), custom_call_target="tpu_custom_call" | custom-call | flops 900000000 | bytes 1048576 | tf_op jit(solution)/shard_map/token_rows/pallas_call | solution.py:589
  (77 shorter events, 13.6 us)
Async XLA Ops:
  0.6 24.4 %collective-permute-start.9 = (bf16[1176,384]{1,0:T(8,128)(2,1)}, bf16[1176,384]{1,0:T(8,128)(2,1)S(1)}, u32[]{:S(2)}, u32[]{:S(2)}) collective-permute-start(bf16[1176,384]{1,0:T(8,128)(2,1)} %mine_ref.5), channel_id=1, source_target_pairs={{0,2},{2,0},{1,3},{3,1},{4,6},{6,4},{5,7},{7,5},{8,10},{10,8},{9,1... | collective-permute-start | bytes 2709512 | tf_op jit(solution)/shard_map/ppermute | solution.py:612
  3.6 21.4 %collective-permute-start.10 = (bf16[768,768]{1,0:T(8,128)(2,1)}, bf16[768,768]{1,0:T(8,128)(2,1)S(1)}, u32[]{:S(2)}, u32[]{:S(2)}) collective-permute-start(bf16[768,768]{1,0:T(8,128)(2,1)} %refs_0_.1), channel_id=1, source_target_pairs={{0,1},{1,0},{2,3},{3,2},{4,5},{5,4},{6,7},{7,6},{8,9},{9,8},{10,11... | collective-permute-start | bytes 3538952 | tf_op jit(solution)/shard_map/ppermute | solution.py:612
  3.6 21.4 %collective-permute-start.11 = (bf16[768,768]{1,0:T(8,128)(2,1)}, bf16[768,768]{1,0:T(8,128)(2,1)}, u32[]{:S(2)}, u32[]{:S(2)}) collective-permute-start(bf16[768,768]{1,0:T(8,128)(2,1)} %refs_2_.1), channel_id=1, source_target_pairs={{0,1},{1,0},{2,3},{3,2},{4,5},{5,4},{6,7},{7,6},{8,9},{9,8},{10,11... | collective-permute-start | bytes 3538952 | tf_op jit(solution)/shard_map/ppermute | solution.py:612
  25.0 27.3 %copy-start.10 = (bf16[1176,768]{1,0:T(8,128)(2,1)}, bf16[1176,768]{1,0:T(8,128)(2,1)S(1)}, u32[]{:S(2)}) copy-start(bf16[1176,768]{1,0:T(8,128)(2,1)S(1)} %get-tuple-element.78.normed_ref) | copy-start | bytes 5419012
  52.4 9.9 %collective-permute-start.12 = (bf16[768,1536]{1,0:T(8,128)(2,1)}, bf16[768,1536]{1,0:T(8,128)(2,1)S(1)}, u32[]{:S(2)}, u32[]{:S(2)}) collective-permute-start(bf16[768,1536]{1,0:T(8,128)(2,1)} %get-tuple-element.83), channel_id=1, source_target_pairs={{0,1},{1,0},{2,3},{3,2},{4,5},{5,4},{6,7},{7,6},{8,9},{9,8},{10,11... | collective-permute-start | bytes 7077896 | tf_op jit(solution)/shard_map/ppermute | solution.py:612
  52.4 9.8 %slice-start = ((s8[4718592]{0:T(1024)(128)(4,1)}), s8[4194304]{0:T(1024)(128)(4,1)S(1)}, s32[]{:S(2)}) async-start(s8[4718592]{0:T(1024)(128)(4,1)} %bitcast.62), calls=%async_computation.1 | async-start | bytes 8388608
  52.5 9.8 %slice-start.1 = ((s8[4718592]{0:T(1024)(128)(4,1)}), s8[524288]{0:T(1024)(128)(4,1)S(1)}, s32[]{:S(2)}) async-start(s8[4718592]{0:T(1024)(128)(4,1)} %bitcast.62), calls=%async_computation.2 | async-start | bytes 1048576
  61.6 25.0 %collective-permute-start.13 = (bf16[1176,384]{1,0:T(8,128)(2,1)}, bf16[1176,384]{1,0:T(8,128)(2,1)}, u32[]{:S(2)}, u32[]{:S(2)}) collective-permute-start(bf16[1176,384]{1,0:T(8,128)(2,1)} %get-tuple-element.87), channel_id=1, source_target_pairs={{0,2},{2,0},{1,3},{3,1},{4,6},{6,4},{5,7},{7,5},{8,10},{10,8},{9,1... | collective-permute-start | bytes 2709512 | tf_op jit(solution)/shard_map/ppermute | solution.py:612
  66.2 28.3 %collective-permute-start.14 = (bf16[4,96,1536]{2,1,0:T(8,128)(2,1)}, bf16[4,96,1536]{2,1,0:T(8,128)(2,1)S(1)}, u32[]{:S(2)}, u32[]{:S(2)}) collective-permute-start(bf16[4,96,1536]{2,1,0:T(8,128)(2,1)} %fusion.4), channel_id=1, source_target_pairs={{0,4},{4,0},{8,12},{12,8},{16,20},{20,16},{24,28},{28,24},{1,5},{5... | collective-permute-start | bytes 3538952 | tf_op jit(solution)/shard_map/ppermute | solution.py:612
  67.7 26.7 %copy-start = (bf16[1176,768]{1,0:T(8,128)(2,1)S(1)}, bf16[1176,768]{1,0:T(8,128)(2,1)}, u32[]{:S(2)}) copy-start(bf16[1176,768]{1,0:T(8,128)(2,1)} %tok_ref.7) | copy-start | bytes 5419012
  67.7 26.7 %copy-start.2 = (bf16[1176,768]{1,0:T(8,128)(2,1)S(1)}, bf16[1176,768]{1,0:T(8,128)(2,1)}, u32[]{:S(2)}) copy-start(bf16[1176,768]{1,0:T(8,128)(2,1)} %get-tuple-element.92.mlp_ref) | copy-start | bytes 5419012
  67.7 26.7 %copy-start.3 = (bf16[768,1152]{1,0:T(8,128)(2,1)S(1)}, bf16[768,1152]{1,0:T(8,128)(2,1)}, u32[]{:S(2)}) copy-start(bf16[768,1152]{1,0:T(8,128)(2,1)} %w_ref.3) | copy-start | bytes 5308420
  94.4 6.0 %copy-start.12 = (bf16[4,96,1536]{2,1,0:T(8,128)(2,1)}, bf16[4,96,1536]{2,1,0:T(8,128)(2,1)S(1)}, u32[]{:S(2)}) copy-start(bf16[4,96,1536]{2,1,0:T(8,128)(2,1)S(1)} %collective-permute-done.14) | copy-start | bytes 3538948
  100.4 84.0 %collective-permute-start.15 = (bf16[1176,768]{1,0:T(8,128)(2,1)}, bf16[1176,768]{1,0:T(8,128)(2,1)}, u32[]{:S(2)}, u32[]{:S(2)}) collective-permute-start(bf16[1176,768]{1,0:T(8,128)(2,1)} %get-tuple-element.98.sent_ref), channel_id=1, source_target_pairs={{0,2},{2,0},{1,3},{3,1},{4,6},{6,4},{5,7},{7,5},{8,10},{10,8},{9,1... | collective-permute-start | bytes 5419016 | tf_op jit(solution)/shard_map/ppermute | solution.py:612
  101.9 83.7 %copy-start.4 = (bf16[1176,384]{1,0:T(8,128)(2,1)S(1)}, bf16[1176,384]{1,0:T(8,128)(2,1)}, u32[]{:S(2)}) copy-start(bf16[1176,384]{1,0:T(8,128)(2,1)} %mine_ref.5) | copy-start | bytes 2709508
  101.9 83.7 %copy-start.7 = (bf16[1,768]{1,0:T(2,128)(2,1)S(1)}, bf16[1,768]{1,0:T(2,128)(2,1)}, u32[]{:S(2)}) copy-start(bf16[1,768]{1,0:T(2,128)(2,1)} %reshape.48.gain_ref) | copy-start | bytes 4612
  101.9 17.2 %copy-start.9 = (f32[4,96,1536]{2,1,0:T(8,128)S(1)}, f32[4,96,1536]{2,1,0:T(8,128)}, u32[]{:S(2)}) copy-start(f32[4,96,1536]{2,1,0:T(8,128)} %get-tuple-element.24) | copy-start | bytes 7077892 | tf_op jit(solution)/shard_map/cond
  101.9 17.2 %copy-start.13 = (bf16[4,96,1536]{2,1,0:T(8,128)(2,1)S(1)}, bf16[4,96,1536]{2,1,0:T(8,128)(2,1)}, u32[]{:S(2)}) copy-start(bf16[4,96,1536]{2,1,0:T(8,128)(2,1)} %get-tuple-element.25) | copy-start | bytes 3538948 | tf_op jit(solution)/shard_map/cond
  111.3 27.3 %collective-permute-start = (bf16[8,48,1536]{2,1,0:T(8,128)(2,1)}, bf16[8,48,1536]{2,1,0:T(8,128)(2,1)}, u32[]{:S(2)}, u32[]{:S(2)}) collective-permute-start(bf16[8,48,1536]{2,1,0:T(8,128)(2,1)} %get-tuple-element.31), channel_id=1, source_target_pairs={{0,1},{1,0},{2,3},{3,2},{4,5},{5,4},{6,7},{7,6},{8,9},{9,8},{10,11... | collective-permute-start | bytes 3538952 | tf_op jit(solution)/shard_map/cond/branch_1_fun/ppermute | solution.py:612
  111.4 2.4 %collective-permute-start.5 = (f32[896]{0:T(1024)S(1)}, f32[896]{0:T(1024)S(1)}, u32[]{:S(2)}, u32[]{:S(2)}) collective-permute-start(f32[896]{0:T(1024)S(1)} %pad_maximum_fusion), channel_id=1, source_target_pairs={{0,1},{1,0},{2,3},{3,2},{4,5},{5,4},{6,7},{7,6},{8,9},{9,8},{10,11... | collective-permute-start | bytes 10760 | tf_op jit(solution)/shard_map/cond/branch_1_fun/ppermute | solution.py:612
  113.9 3.6 %collective-permute-start.6 = (f32[896]{0:T(1024)S(1)}, f32[896]{0:T(1024)S(1)}, u32[]{:S(2)}, u32[]{:S(2)}) collective-permute-start(f32[896]{0:T(1024)S(1)} %fusion.6), channel_id=1, source_target_pairs={{0,4},{4,0},{8,12},{12,8},{16,20},{20,16},{24,28},{28,24},{1,5},{5... | collective-permute-start | bytes 10760 | tf_op jit(solution)/shard_map/cond/branch_1_fun/ppermute | solution.py:612
  117.5 18.2 %collective-permute-start.7 = (f32[896]{0:T(1024)S(1)}, f32[896]{0:T(1024)S(1)}, u32[]{:S(2)}, u32[]{:S(2)}) collective-permute-start(f32[896]{0:T(1024)S(1)} %add.51), channel_id=1, source_target_pairs={{0,8},{4,12},{8,0},{12,4},{16,24},{20,28},{24,16},{28,20},{1,9},{5... | collective-permute-start | bytes 10760 | tf_op jit(solution)/shard_map/cond/branch_1_fun/ppermute | solution.py:612
  120.4 50.8 %all-to-all-start = ((bf16[4,96,1536]{2,1,0:T(8,128)(2,1)}), bf16[4,96,1536]{2,1,0:T(8,128)(2,1)}, u32[]{:S(2)}, u32[]{:S(2)}) async-start(bf16[4,96,1536]{2,1,0:T(8,128)(2,1)} %add_convert_fusion), calls=%async_computation | async-start | bytes 2359296 | tf_op jit(solution)/shard_map/cond/branch_1_fun/all_to_all | solution.py:666
  135.7 28.3 %collective-permute-start.8 = (f32[896]{0:T(1024)S(1)}, f32[896]{0:T(1024)S(1)}, u32[]{:S(2)}, u32[]{:S(2)}) collective-permute-start(f32[896]{0:T(1024)S(1)} %add.52), channel_id=1, source_target_pairs={{0,16},{4,20},{8,24},{12,28},{16,0},{20,4},{24,8},{28,12},{1,17},{... | collective-permute-start | bytes 10760 | tf_op jit(solution)/shard_map/cond/branch_1_fun/ppermute | solution.py:612
  138.7 4.5 %copy-start.11 = (f32[1176,384]{1,0:T(8,128)S(1)}, f32[1176,384]{1,0:T(8,128)}, u32[]{:S(2)}) copy-start(f32[1176,384]{1,0:T(8,128)} %get-tuple-element.34) | copy-start | bytes 5419012 | tf_op jit(solution)/shard_map/cond
  141.1 1.4 copy-start.8
  142.6 21.4 %collective-permute-start.1 = (bf16[4,48,1536]{2,1,0:T(8,128)(2,1)S(1)}, bf16[4,48,1536]{2,1,0:T(8,128)(2,1)}, u32[]{:S(2)}, u32[]{:S(2)}) collective-permute-start(bf16[4,48,1536]{2,1,0:T(8,128)(2,1)S(1)} %fusion.1), channel_id=1, source_target_pairs={{0,4},{4,0},{8,12},{12,8},{16,20},{20,16},{24,28},{28,24},{1,5},{5... | collective-permute-start | bytes 1769480 | tf_op jit(solution)/shard_map/cond/branch_1_fun/ppermute | solution.py:612
  166.8 8.6 %collective-permute-start.2 = (bf16[48,1536]{1,0:T(8,128)(2,1)}, bf16[48,1536]{1,0:T(8,128)(2,1)S(1)}, u32[]{:S(2)}, u32[]{:S(2)}) collective-permute-start(bf16[48,1536]{1,0:T(8,128)(2,1)} %get-tuple-element.108), channel_id=1, source_target_pairs={{0,8},{4,12},{8,0},{12,4},{16,24},{20,28},{24,16},{28,20},{1,9},{5... | collective-permute-start | bytes 442376 | tf_op jit(solution)/shard_map/cond/branch_1_fun/ppermute | solution.py:612
  166.8 14.0 %collective-permute-start.3 = (bf16[48,1536]{1,0:T(8,128)(2,1)}, bf16[48,1536]{1,0:T(8,128)(2,1)}, u32[]{:S(2)}, u32[]{:S(2)}) collective-permute-start(bf16[48,1536]{1,0:T(8,128)(2,1)} %get-tuple-element.110), channel_id=1, source_target_pairs={{0,16},{4,20},{8,24},{12,28},{16,0},{20,4},{24,8},{28,12},{1,17},{... | collective-permute-start | bytes 442376 | tf_op jit(solution)/shard_map/cond/branch_1_fun/ppermute | solution.py:612
  168.9 11.9 %collective-permute-start.4 = (bf16[48,1536]{1,0:T(8,128)(2,1)}, bf16[48,1536]{1,0:T(8,128)(2,1)}, u32[]{:S(2)}, u32[]{:S(2)}) collective-permute-start(bf16[48,1536]{1,0:T(8,128)(2,1)} %get-tuple-element.109), channel_id=1, source_target_pairs={{0,24},{4,28},{8,16},{12,20},{16,8},{20,12},{24,0},{28,4},{1,25},{... | collective-permute-start | bytes 442376 | tf_op jit(solution)/shard_map/cond/branch_1_fun/ppermute | solution.py:612
  184.4 7.8 %copy-start.14 = (f32[48,1152]{1,0:T(8,128)}, f32[48,1152]{1,0:T(8,128)S(1)}, u32[]{:S(2)}) copy-start(f32[48,1152]{1,0:T(8,128)S(1)} %get-tuple-element.70) | copy-start | bytes 663556
  185.1 7.2 %collective-permute-start.16 = (f32[896]{0:T(1024)S(1)}, f32[896]{0:T(1024)S(1)}, u32[]{:S(2)}, u32[]{:S(2)}) collective-permute-start(f32[896]{0:T(1024)S(1)} %get-tuple-element.101), channel_id=1, source_target_pairs={{0,2},{2,0},{1,3},{3,1},{4,6},{6,4},{5,7},{7,5},{8,10},{10,8},{9,1... | collective-permute-start | bytes 10760 | tf_op jit(solution)/shard_map/ppermute | solution.py:612
  (5 other events, 5.6 us)
where the time goes:
time: 194 us; the launch traced here: 193 us
  Pallas kernels  92.3 us (48%)
  waiting for transfers between devices  35.7 us (18%)
  starting transfers between devices  34.6 us (18%)
  other arithmetic  16.5 us (9%)
  local copies, waits for them, and re-layouts  13 us (7%)
    ppermute x17, waiting for transfers between devices, swap(): lax.ppermute(value, axis, [(place, place ^ bit) for place in range(size)])  35.7 us
    pallas_call x1, Pallas kernels, dense(): pl.pallas_call(functools.partial(dense_kernel, count, tiles), name='dense...  25.9 us
    ppermute x17, starting transfers between devices, swap(): lax.ppermute(value, axis, [(place, place ^ bit) for place in range(size)])  19.3 us
    pallas_call x1, Pallas kernels, forward(): pl.pallas_call(forward_kernel, name='forward', out_shape=[jax.ShapeDtypeS...  19 us
    pallas_call x1, Pallas kernels, backward(): pl.pallas_call(backward_kernel, name='backward', grid=(heads // 2,), out_...  18.8 us
    all_to_all x1, starting transfers between devices, sum_rest(): lax.all_to_all(total, 'dp', 0, 0, axis_index_groups=groups, tiled=True)  15.3 us
    pallas_call x1, Pallas kernels, outputs(): pl.pallas_call(outputs_kernel, name='outputs', grid=(rows // tile,), out_...  9.1 us
    pallas_call x1, Pallas kernels, weights(): pl.pallas_call(weights_kernel, name='weights', out_shape=[jax.ShapeDtypeS...  8.03 us
  transfers between devices with their start and end apart: 18, of which 5 were waited for; matrix products, arithmetic and copies ran while one was open for 11% of the time, Pallas kernels for 31%

commit v1 on v0

--- a/solution.py
+++ b/solution.py
@@ -342,6 +342,9 @@
     )(big_images, q_rows, k_rows, v_rows, do_rows, inverses, qk_gains)
 
 
+FINE = 6 * PATCHES // 7
+
+
 def in_order(mine, other):
     first = lax.axis_index("hg") == 0
     return jnp.where(first, mine, other), jnp.where(first, other, mine)
@@ -350,19 +353,17 @@
 def dense_kernel(count, tiles, normed_ref, mine_ref, other_ref, *refs):
     w_in_refs, w_back_refs = refs[:count], refs[count : 2 * count]
     refs = refs[2 * count :]
-    part_ref, grad_ref, dy_ref = refs[:3]
-    grad_refs, refs = refs[3 : 3 + count], refs[3 + count :]
+    part_ref, grad_ref, normed_t_ref, dy_t_ref = refs[:4]
+    grad_refs, refs = refs[4 : 4 + count], refs[4 + count :]
     normed_rows, dy_rows = refs[:2]
     act_refs, gup_refs = refs[2 : 2 + count], refs[2 + count :]
     step = pl.program_id(0)
     half = mine_ref.shape[1]
     curve = math.sqrt(2.0 / math.pi)
     normed = normed_ref[...]
-    first, second = in_order(mine_ref[...], other_ref[...])
-    dy_ref[:, :half], dy_ref[:, half:] = first, second
-    dy = dy_ref[...]
+    dy_rows[step, :, :half], dy_rows[step, :, half:] = in_order(mine_ref[...], other_ref[...])
+    dy = dy_rows[step]
     normed_rows[step] = normed
-    dy_rows[step] = dy
     for w_in_ref, w_back_ref, act_ref, gup_ref in zip(w_in_refs, w_back_refs, act_refs, gup_refs):
         columns = w_in_ref.shape[1]
         width = min(256, columns)
@@ -388,12 +389,24 @@
 
     @pl.when(step == tiles - 1)
     def _():
+        rows, width = tiles * normed_rows.shape[1], normed_rows.shape[2]
+        for source, turned in ((normed_rows, normed_t_ref), (dy_rows, dy_t_ref)):
+            turned[:, :rows] = source[...].reshape(rows, width).T
+            turned[:, rows:] = jnp.zeros((width, turned.shape[1] - rows), jnp.bfloat16)
         for act_ref, gup_ref, ref in zip(act_refs, gup_refs, grad_refs):
             columns = act_ref.shape[2]
-            for left, right, at in ((normed_rows, gup_ref, 0), (dy_rows, act_ref, columns)):
-                rows = tiles * left.shape[1]
-                total = rows_t(left[...].reshape(rows, -1), right[...].reshape(rows, columns))
-                ref[:, at : at + columns] = total.astype(ref.dtype)
+            for turned, right, at in ((normed_t_ref, gup_ref, 0), (dy_t_ref, act_ref, columns)):
+                total = times(turned[:, :rows], right[...].reshape(rows, columns))
+                by_parity(total, ref, slice(at, at + columns))
+
+
+def by_parity(total, ref, cols):
+    halves, rows = ref.shape[1:3]
+    odd = lax.axis_index("dp") & 1
+    for half in range(halves):
+        for side in range(2):
+            start = (2 * half + side) * rows
+            ref[odd ^ side, half, :, cols] = total[start : start + rows].astype(ref.dtype)
 
 
 def dense(normed, mine, other, w_in_pieces, w_back_pieces):
@@ -403,9 +416,10 @@
     count = len(w_in_pieces)
     shape = jax.ShapeDtypeStruct
     sizes = [piece.shape[1] for piece in w_in_pieces]
-    kinds = [jnp.float32] * (count - 1) + [jnp.bfloat16] if count > 1 else [jnp.float32]
+    groups = lax.axis_size("dp")
+    padded = -(-rows // 256) * 256
     row_tile = lambda columns: pl.BlockSpec((tile, columns), lambda step: (step, 0))
-    fixed = lambda columns: pl.BlockSpec((width, columns), lambda step: (0, 0))
+    turned = pl.BlockSpec((width, padded), lambda step: (0, 0))
     once = lambda columns: pl.BlockSpec((width, columns), lambda step: (0, 0), pipeline_mode=pl.Buffered(1))
     return pl.pallas_call(
         functools.partial(dense_kernel, count, tiles),
@@ -414,12 +428,18 @@
         out_shape=[
             shape((rows, width), jnp.float32),
             shape((rows, width), jnp.bfloat16),
-            shape((rows, width), jnp.bfloat16),
+            shape((width, padded), jnp.bfloat16),
+            shape((width, padded), jnp.bfloat16),
         ]
-        + [shape((width, 2 * size), kind) for size, kind in zip(sizes, kinds)],
+        + [shape((2, groups // 2, width // groups, 2 * size), jnp.bfloat16) for size in sizes],
         in_specs=[row_tile(width), row_tile(width // 2), row_tile(width // 2)]
         + [once(size) for size in sizes] * 2,
-        out_specs=[row_tile(width)] * 3 + [fixed(2 * size) for size in sizes],
+        out_specs=[row_tile(width)] * 2
+        + [turned] * 2
+        + [
+            pl.BlockSpec((2, groups // 2, width // groups, 2 * size), lambda step: (0, 0, 0, 0))
+            for size in sizes
+        ],
         scratch_shapes=[VMEM((tiles, tile, width), jnp.bfloat16)] * 2
         + [VMEM((tiles, tile, size), jnp.bfloat16) for size in sizes] * 2,
         compiler_params=pltpu.CompilerParams(vmem_limit_bytes=60 * 2**20),
@@ -508,7 +528,7 @@
 
 def features(first, count, grad_joined, w_qkv, grad_mlp, tokens):
     rows, width = tokens.shape
-    tile = 2 * PATCHES
+    tile = FINE
     row_tile = lambda columns: pl.BlockSpec((tile, columns), lambda step: (step + first, 0))
     return pl.pallas_call(
         features_kernel,
@@ -533,35 +553,52 @@
     )(grad_joined, w_qkv, grad_mlp, tokens)
 
 
-def weights_kernel(*refs):
-    keep_ref, send_ref = refs[-2:]
-    groups, rows, _ = keep_ref.shape
-    first_side = lax.axis_index("hid") == 0
-    at = 0
-    for left_ref, right_ref in zip(refs[:-2:2], refs[1:-2:2]):
-        total = rows_t(left_ref[...], right_ref[...])
-        cols = slice(at, at + total.shape[1])
-        at = cols.stop
-        for group in range(groups):
-            even, odd = (total[(2 * group + side) * rows : (2 * group + side + 1) * rows] for side in (0, 1))
-            keep_ref[group, :, cols] = jnp.where(first_side, even, odd)
-            send_ref[group, :, cols] = low(jnp.where(first_side, odd, even))
-
-
-def weights(*pairs):
-    whole = pl.BlockSpec(memory_space=VMEM)
+def weights_kernel(chunks, normed_t_ref, dy_t_ref, joined_ref, att_ref, keep_ref, send_ref):
+    halves, rows, columns = keep_ref.shape[1:]
+    tokens = att_ref.shape[0]
+    odd, side = lax.axis_index("dp") & 1, lax.axis_index("hid")
+
+    def finish(left_ref, right_ref):
+        total = times(left_ref[:, :tokens], right_ref[...])
+        for half in range(halves):
+            for parity in range(2):
+                start = 2 * (2 * half + parity) * rows
+                even, uneven = total[start : start + rows], total[start + rows : start + 2 * rows]
+                keep_ref[odd ^ parity, half] = low(jnp.where(side == 0, even, uneven))
+                send_ref[odd ^ parity, half] = low(jnp.where(side == 0, uneven, even))
+
+    @pl.when(pl.program_id(0) < chunks)
+    def _():
+        finish(normed_t_ref, joined_ref)
+
+    @pl.when(pl.program_id(0) == chunks)
+    def _():
+        finish(dy_t_ref, att_ref)
+
+
+def weights(normed_t, dy_t, grad_joined, attended):
     groups = lax.axis_size("dp")
-    columns = sum(right.shape[1] for right in pairs[1::2])
-    shape = (groups, pairs[0].shape[1] // (2 * groups), columns)
+    rows, columns = attended.shape
+    chunks = grad_joined.shape[1] // columns
+    shape = (2, groups // 2, normed_t.shape[0] // (2 * groups), columns)
+    whole = jax.ShapeDtypeStruct(shape[:3] + (columns * (chunks + 1),), jnp.bfloat16)
+    turned = pl.BlockSpec(normed_t.shape, lambda step: (0, 0))
+    out = pl.BlockSpec(shape, lambda step: (0, 0, 0, step))
     return pl.pallas_call(
-        weights_kernel,
+        functools.partial(weights_kernel, chunks),
         name="weights",
-        out_shape=[jax.ShapeDtypeStruct(shape, jnp.float32), jax.ShapeDtypeStruct(shape, jnp.bfloat16)],
-        in_specs=[whole] * len(pairs),
-        out_specs=[whole] * 2,
+        grid=(chunks + 1,),
+        out_shape=[whole, whole],
+        in_specs=[
+            turned,
+            turned,
+            pl.BlockSpec((rows, columns), lambda step: (0, jnp.minimum(step, chunks - 1))),
+            pl.BlockSpec((rows, columns), lambda step: (0, 0)),
+        ],
+        out_specs=[out, out],
         compiler_params=pltpu.CompilerParams(vmem_limit_bytes=48 * 2**20),
         cost_estimate=cost(1),
-    )(*pairs)
+    )(normed_t, dy_t, grad_joined, attended)
 
 
 def tokens_kernel(sent_ref, came_ref, tok_ref, gain_ref, mine_ref, other_ref, *refs):
@@ -581,7 +618,7 @@
 
 def token_rows(first, sent, came, tokens, norm_gain, mine, other, before):
     rows, width = tokens.shape
-    tile = 2 * PATCHES
+    tile = FINE
     count = sent.shape[0] // tile
     near = lambda columns: pl.BlockSpec((tile, columns), lambda step: (step, 0))
     far = lambda columns: pl.BlockSpec((tile, columns), lambda step: (step + first, 0))
@@ -628,35 +665,35 @@
 def scatter_pieces(pieces, axis):
     for bit in reversed(bits_of(axis)):
         sent = swap(low(pieces[-1]), axis, bit)
-        kept, at, half = [], 0, sent.shape[1] // 2
+        kept, at, half = [], 0, sent.shape[-1] // 2
         for piece in pieces[:-1]:
-            size = piece.shape[1] // 2
-            parts = (sent[:, at : at + size], sent[:, half + at : half + at + size])
-            kept.append(wide(piece) + wide(jnp.concatenate(parts, axis=1) if size < half else sent))
+            size = piece.shape[-1] // 2
+            parts = (sent[..., at : at + size], sent[..., half + at : half + at + size])
+            kept.append(wide(piece) + wide(jnp.concatenate(parts, axis=-1) if size < half else sent))
             at += size
         pieces = kept
     return pieces[0]
 
 
-def row_blocks(*pairs):
+def row_blocks(normed_t, dy_t, grad_joined, attended):
     groups, sides = lax.axis_size("dp"), lax.axis_size("hid")
-    if sides == 2 and pairs[0].shape[1] % (16 * groups * sides) == 0:
-        keep, send = weights(*pairs)
-        return keep + wide(swap(send, "hid", 1))
-    total = jnp.concatenate([rows_t(*pairs[at : at + 2]) for at in range(0, len(pairs), 2)], axis=1)
-    shaped = total.reshape(groups, sides, -1, total.shape[1])
-    shaped = shaped[:, lax.axis_index("hid") ^ jnp.arange(sides)]
+    width = normed_t.shape[0]
+    if sides == 2 and width % (16 * groups * sides) == 0:
+        keep, send = weights(normed_t, dy_t, grad_joined, attended)
+        return wide(keep) + wide(swap(send, "hid", 1))
+    tokens = attended.shape[0]
+    parts = [times(normed_t[:, :tokens], grad_joined), times(dy_t[:, :tokens], attended)]
+    shaped = jnp.concatenate(parts, axis=1).reshape(groups // 2, 2, sides, width // (groups * sides), -1)
+    odd = lax.axis_index("dp") & 1
+    shaped = shaped[:, odd ^ jnp.arange(2)][:, :, lax.axis_index("hid") ^ jnp.arange(sides)]
+    shaped = shaped.transpose(1, 0, 2, 3, 4)
     for bit in reversed(bits_of("hid")):
-        shaped = shaped[:, :bit] + wide(swap(low(shaped[:, bit:]), "hid", bit))
-    return shaped[:, 0]
+        shaped = shaped[:, :, :bit] + wide(swap(low(shaped[:, :, bit:]), "hid", bit))
+    return shaped[:, :, 0]
 
 
 def halve(shaped):
-    count, rows, columns = shaped.shape
-    shaped = shaped.reshape(count // 2, 2, rows, columns)
-    odd = (lax.axis_index("dp") & 1) > 0
-    sent = low(jnp.where(odd, shaped[:, 0], shaped[:, 1]))
-    return jnp.where(odd, shaped[:, 1], shaped[:, 0]), swap(sent, "dp", 1)
+    return low(shaped[0]), swap(low(shaped[1]), "dp", 1)
 
 
 def sum_rest(kept, came):
@@ -664,17 +701,33 @@
     groups = [list(range(odd, count, 2)) for odd in (0, 1)]
     total = low(wide(kept) + wide(came))
     total = lax.all_to_all(total, "dp", 0, 0, axis_index_groups=groups, tiled=True)
-    return jnp.sum(wide(total), axis=0)
-
-
-def sum_far(kept, came):
+    half = total.shape[2] // 2
+    return tuple(jnp.sum(wide(part), axis=0) for part in (total[:, :, :half], total[:, :, half:]))
+
+
+def sum_far(kept, came, extra, extra_came, columns):
+    half, rows, width = kept.shape
+    extra = low(wide(extra) + wide(extra_came))
+    extra = jnp.pad(extra, (0, 8 * width - extra.shape[0])).reshape(1, 8, width)
     total = low(wide(kept) + wide(came))
+    total = jnp.concatenate([total, jnp.broadcast_to(extra, (half, 8, width))], axis=1)
     me = lax.axis_index("dp") // 2
     terms = [lax.dynamic_index_in_dim(total, me, keepdims=False)]
-    for step in range(1, total.shape[0]):
+    for step in range(1, half):
         block = lax.dynamic_index_in_dim(total, me ^ step, keepdims=False)
         terms.append(swap(block, "dp", 2 * step))
-    return sum(wide(term) for term in terms)
+
+    def added(part):
+        values = [wide(part(term)) for term in terms]
+        while len(values) > 1:
+            values = [first + second for first, second in zip(values[::2], values[1::2])]
+        return values[0]
+
+    return (
+        added(lambda term: term[:rows, :columns]),
+        added(lambda term: term[:rows, columns:]),
+        added(lambda term: term[rows]),
+    )
 
 
 def sum_everywhere(value, axes):
@@ -694,39 +747,52 @@
     normed, q_rows, k_rows, v_rows, attended, inverses = forward(
         big_images, tokens, norm_gain, w_qkv, qk_gains
     )
-    part, grad_mlp, grad_out, *grads = dense(normed, cotangent, other, w_in_pieces, w_back_pieces)
+    part, grad_mlp, normed_t, dy_t, *grads = dense(normed, cotangent, other, w_in_pieces, w_back_pieces)
     kept, sent, do_rows = outputs(part, tokens, attended, cotangent, other, w_out_t)
     out_came = swap(sent, "hg", 1)
-    mlp_kept, mlp_came = halve(scatter_pieces(grads, "hid").reshape(groups, width // groups, -1))
+    mlp_kept, mlp_came = halve(scatter_pieces(grads, "hid"))
     do_rows, mlp_kept = lax.optimization_barrier((do_rows, mlp_kept))
 
     grad_joined, qk_part = backward(big_images, q_rows, k_rows, v_rows, do_rows, inverses, qk_gains)
     grad_joined, out_came, mlp_came = lax.optimization_barrier((grad_joined, out_came, mlp_came))
-    mine, gain_part = features(0, tokens.shape[0] // (2 * PATCHES), grad_joined, w_qkv, grad_mlp, tokens)
+    mine, gain_part = features(0, tokens.shape[0] // FINE, grad_joined, w_qkv, grad_mlp, tokens)
     came = swap(mine, "hg", 1)
 
-    def weight_sums(normed, grad_joined, grad_out, attended, mlp_kept, mlp_came, gain_part, qk_part, kept, out_came):
-        blocks = row_blocks(normed, grad_joined, grad_out, attended)
+    def weight_sums(normed_t, dy_t, grad_joined, attended, mlp_kept, mlp_came, gain_part, qk_part, kept, out_came):
+        blocks = row_blocks(normed_t, dy_t, grad_joined, attended)
         mlp_grads = sum_rest(mlp_kept, mlp_came)
-        both = sum_far(*halve(blocks))
         small = jnp.concatenate([gain_part[0], qk_part[0, :size], qk_part[0, LANES : LANES + size]])
-        small = sum_everywhere(small, ("hid", "dp"))
-        return mlp_grads, both, small, low(kept + wide(out_came))
+        small = low(sum_everywhere(small, ("hid",)))
+        small, blocks = lax.optimization_barrier((small, blocks))
+        blocks_kept, blocks_came = halve(blocks)
+        sums = sum_far(blocks_kept, blocks_came, small, swap(small, "dp", 1), grad_joined.shape[1])
+        return mlp_grads, sums, low(kept + wide(out_came))
 
     def no_sums(*operands):
-        return tuple(jnp.zeros(kind.shape, kind.dtype) for kind in kinds)
-
-    operands = (normed, grad_joined, grad_out, attended, mlp_kept, mlp_came, gain_part, qk_part, kept, out_came)
+        return jax.tree.map(lambda kind: jnp.zeros(kind.shape, kind.dtype), kinds)
+
+    operands = (
+        normed_t,
+        dy_t,
+        grad_joined,
+        attended,
+        mlp_kept,
+        mlp_came,
+        gain_part,
+        qk_part,
+        kept,
+        out_came,
+    )
     kinds = jax.eval_shape(weight_sums, *operands)
-    mlp_grads, both, small, output = lax.cond(big_images[0] >= 0, weight_sums, no_sums, *operands)
+    mlp_grads, sums, output = lax.cond(big_images[0] >= 0, weight_sums, no_sums, *operands)
+    w_in_grad, w_back_grad = mlp_grads
+    w_qkv_grad, w_out_t_grad, small = sums
     came, small = lax.optimization_barrier((came, small))
     small = sum_everywhere(small, ("hg",))
-    w_in_grad, w_back_grad = jnp.split(mlp_grads, 2, axis=1)
-    w_qkv_grad, w_out_t_grad = both[:, : w_qkv.shape[1]], both[:, w_qkv.shape[1] :]
     own = lax.axis_index("dp") * lax.axis_size("hid") + lax.axis_index("hid")
     gain_rows = width // (groups * lax.axis_size("hid"))
     norm_gain_grad = lax.dynamic_slice_in_dim(small, own * gain_rows, gain_rows, 0)
-    qk_gains_grad = small[width:].reshape(2, size)
+    qk_gains_grad = small[width : width + 2 * size].reshape(2, size)
     token_grad = token_rows(0, mine, came, tokens, norm_gain, cotangent, other, None)
     return (
         output,

time: 194 us -> 183 us (0.943)
  Pallas kernels: 92.3 us -> 97.3 us
  local copies, waits for them, and re-layouts: 13 us -> 8.12 us
  other arithmetic: 16.5 us -> 11.7 us
  starting transfers between devices: 34.6 us -> 30.2 us
  waiting for transfers between devices: 35.7 us -> 33.1 us
    ppermute x17 -> x15, waiting for transfers between devices: 35.7 us -> 19.8 us  [swap(): lax.ppermute(value, axis, [(place, place ^ bit) for place in range(size)])]
    all_to_all x1, waiting for transfers between devices: 0.01 us -> 13.3 us  [sum_rest(): lax.all_to_all(total, 'dp', 0, 0, axis_index_groups=groups, tiled=True)]
    ppermute x17 -> x15, starting transfers between devices: 19.3 us -> 16 us  [swap(): lax.ppermute(value, axis, [(place, place ^ bit) for place in range(size)])]
    pallas_call x1, Pallas kernels: 5.99 us -> 8.2 us  [features(): pl.pallas_call(features_kernel, name='features', grid=(count,), out_shape...]
    cond x10, local copies, waits for them, and re-layouts: 2.78 us -> 0.59 us
    add x3 -> x5, other arithmetic: 5.02 us -> 3.37 us  [the longest x1 1.73 us: row_blocks(): return wide(keep) + wide(swap(send, 'hid', 1))]
  transfers between devices with their start and end apart: 18 -> 16, of which waited for: 5 -> 4; matrix products, arithmetic and copies ran while one was open for 11% -> 8% of each run, Pallas kernels for 31% -> 34%
where the time goes in v1:
time: 183 us; the launch traced here: 182 us
  Pallas kernels  97.3 us (53%)
  waiting for transfers between devices  33.1 us (18%)
  starting transfers between devices  30.2 us (17%)
  other arithmetic  11.7 us (6%)
  local copies, waits for them, and re-layouts  8.12 us (4%)
    pallas_call x1, Pallas kernels, dense(): pl.pallas_call(functools.partial(dense_kernel, count, tiles), name='dense...  26.5 us
    ppermute x15, waiting for transfers between devices, swap(): lax.ppermute(value, axis, [(place, place ^ bit) for place in range(size)])  19.8 us
    pallas_call x1, Pallas kernels, forward(): pl.pallas_call(forward_kernel, name='forward', out_shape=[jax.ShapeDtypeS...  19.4 us
    pallas_call x1, Pallas kernels, backward(): pl.pallas_call(backward_kernel, name='backward', grid=(heads // 2,), out_...  18.8 us
    ppermute x15, starting transfers between devices, swap(): lax.ppermute(value, axis, [(place, place ^ bit) for place in range(size)])  16 us
    all_to_all x1, starting transfers between devices, sum_rest(): lax.all_to_all(total, 'dp', 0, 0, axis_index_groups=groups, tiled=True)  14.2 us
    all_to_all x1, waiting for transfers between devices, sum_rest(): lax.all_to_all(total, 'dp', 0, 0, axis_index_groups=groups, tiled=True)  13.3 us
    pallas_call x1, Pallas kernels, outputs(): pl.pallas_call(outputs_kernel, name='outputs', grid=(rows // tile,), out_...  8.85 us
  transfers between devices with their start and end apart: 16, of which 4 were waited for; matrix products, arithmetic and copies ran while one was open for 8% of the time, Pallas kernels for 34%

profile of v1, /device:TPU:0, one launch (start us, length us, event | category | flops | bytes accessed | tf_op | source)
XLA Modules:
  0.0 182.0 jit_solution(11947620582216315736)
XLA Ops:
  0.6 3.0 %collective-permute-start.7 = (bf16[1176,384]{1,0:T(8,128)(2,1)}, bf16[1176,384]{1,0:T(8,128)(2,1)S(1)}, u32[]{:S(2)}, u32[]{:S(2)}) collective-permute-start(bf16[1176,384]{1,0:T(8,128)(2,1)} %mine_ref.5), channel_id=1, source_target_pairs={{0,2},{2,0},{1,3},{3,1},{4,6},{6,4},{5,7},{7,5},{8,10},{10,8},{9,1... | collective-permute-start | bytes 2709512 | tf_op jit(solution)/shard_map/ppermute | solution.py:649
  4.8 1.3 reshape.50.gain_ref
  6.1 19.4 %forward.1 = (bf16[1176,768]{1,0:T(8,128)(2,1)}, bf16[6,1280,128]{2,1,0:T(8,128)(2,1)}, bf16[6,1280,128]{2,1,0:T(8,128)(2,1)}, bf16[6,1280,128]{2,1,0:T(8,128)(2...) custom-call(s32[1]{0:T(128)S(6)} %copy.29.flag_ref, bf16[1176,768]{1,0:T(8,128)(2,1)} %tok_ref.7, ...), custom_call_target="tpu_custom_call" | custom-call | flops 24000000000 | bytes 1048576 | tf_op jit(solution)/shard_map/forward/pallas_call | solution.py:203
  25.5 0.9 copy-done.4
  26.8 26.5 %dense.1 = (f32[1176,768]{1,0:T(8,128)}, bf16[1176,768]{1,0:T(8,128)(2,1)}, bf16[768,1280]{1,0:T(8,128)(2,1)}, bf16[768,1280]{1,0:T(8,128)(2,1)}, bf16[2,4,96,15...) custom-call(bf16[1176,768]{1,0:T(8,128)(2,1)} %get-tuple-element.74.normed_ref, bf16[1176,384]{1,0:T(8,128)(2,1)} %mine_ref.5, ...), custom_call_target="tpu_custom_call" | custom-call | flops 24000000000 | bytes 1048576 | tf_op jit(solution)/shard_map/dense/pallas_call | solution.py:424
  53.4 8.8 %outputs.1 = (f32[1176,384]{1,0:T(8,128)}, bf16[1176,384]{1,0:T(8,128)(2,1)}, bf16[6,1280,128]{2,1,0:T(8,128)(2,1)}) custom-call(f32[1176,768]{1,0:T(8,128)} %get-tuple-element.75.part_ref, bf16[1176,768]{1,0:T(8,128)(2,1)} %tok_ref.7, bf16[1176,384]{1,0:T(8,128)(2,1)S(1)} %get-tuple-element.76.att_ref, bf16[1176,384]{1,0:T(8,128)(2,1)} %mine_ref.5, ...), custom_call_target="tpu_custom_call" | custom-call | flops 6000000000 | bytes 1048576 | tf_op jit(solution)/shard_map/outputs/pallas_call | solution.py:494
  62.5 0.7 add_convert_fusion.4
  63.2 1.2 slice_bitcast_fusion.4
  64.4 1.9 %collective-permute-start.12 = (bf16[4,96,1536]{2,1,0:T(8,128)(2,1)S(1)}, bf16[4,96,1536]{2,1,0:T(8,128)(2,1)S(1)}, u32[]{:S(2)}, u32[]{:S(2)}) collective-permute-start(bf16[4,96,1536]{2,1,0:T(8,128)(2,1)S(1)} %get-tuple-element.114), channel_id=1, source_target_pairs={{0,4},{4,0},{8,12},{12,8},{16,20},{20,16},{24,28},{28,24},{1,5},{5... | collective-permute-start | bytes 3538952 | tf_op jit(solution)/shard_map/ppermute | solution.py:649
  66.2 18.8 %backward.1 = (bf16[1176,1152]{1,0:T(8,128)(2,1)}, f32[8,256]{1,0:T(8,128)S(1)}) custom-call(s32[1]{0:T(128)S(6)} %copy.29.flag_ref, bf16[6,1280,128]{2,1,0:T(8,128)(2,1)} %get-tuple-element.81.q_ref, bf16[6,1280,128]{2,1,0:T(8,128)(2,1)} %get-tuple-element.82.k_ref, bf16[6,1280,128]{2,1,0:T(8,128)(2,1)} %get-tuple-element.83.v_ref, ...), custom_call_target="tpu_custom_call" | custom-call | flops 35999997952 | bytes 1048576 | tf_op jit(solution)/shard_map/backward/pallas_call | solution.py:319
  85.0 7.5 %collective-permute-done.12 = bf16[4,96,1536]{2,1,0:T(8,128)(2,1)S(1)} collective-permute-done((bf16[4,96,1536]{2,1,0:T(8,128)(2,1)S(1)}, bf16[4,96,1536]{2,1,0:T(8,128)(2,1)S(1)}, u32[]{:S(2)}, u32[]{:S(2)}) %collective-permute-start.12) | collective-permute-done | bytes 1179680 | tf_op jit(solution)/shard_map/ppermute | solution.py:649
  92.6 8.2 %features.1 = (bf16[1176,768]{1,0:T(8,128)(2,1)}, f32[8,768]{1,0:T(8,128)S(1)}) custom-call(bf16[1176,1152]{1,0:T(8,128)(2,1)} %get-tuple-element.89.joined_ref, bf16[768,1152]{1,0:T(8,128)(2,1)S(1)} %copy-done.2, bf16[1176,768]{1,0:T(8,128)(2,1)S(1)} %copy-done.1, bf16[1176,768]{1,0:T(8,128)(2,1)S(1)} %copy-done), custom_call_target="tpu_custom_call" | custom-call | flops 2100000000 | bytes 1048576 | tf_op jit(solution)/shard_map/features/pallas_call | solution.py:533
  100.8 1.7 collective-permute-start.13
  102.5 68.1 %conditional.1 = (f32[96,768]{1,0:T(8,128)S(1)}, f32[96,768]{1,0:T(8,128)}, f32[48,1152]{1,0:T(8,128)S(1)}, f32[48,384]{1,0:T(8,128)}, f32[1536]{0:T(1024)S(1)}, /*index=5*/bf16[1176,384]{1,0:T(8,128)(2,1)}) conditional(s32[]{:T(128)} %bitcast.9, () %tuple.20, (bf16[4,96,1536]{2,1,0:T(8,128)(2,1)}, bf16[4,96,1536]{2,1,0:T(8,128)(2,1)}, ...), branch_computations={%region_0.0_spmd, %region_1.4_spmd} | conditional | flops 1010197248 | bytes 53773916 | solution.py:787
  102.5 8.5 %weights.1 = (bf16[2,4,48,1536]{3,2,1,0:T(8,128)(2,1)S(1)}, bf16[2,4,48,1536]{3,2,1,0:T(8,128)(2,1)}) custom-call(bf16[768,1280]{1,0:T(8,128)(2,1)} %get-tuple-element.24.normed_t_ref, bf16[768,1280]{1,0:T(8,128)(2,1)} %get-tuple-element.25.dy_t_ref, bf16[1176,1152]{1,0:T(8,128)(2,1)} %get-tuple-element.26.joined_ref, ...), custom_call_target="tpu_custom_call" | custom-call | flops 1000000000 | bytes 1048576 | tf_op jit(solution)/shard_map/cond/branch_1_fun/weights/pallas_call | solution.py:587
  111.6 1.3 add_convert_fusion
  112.9 14.2 %all-to-all-start = ((bf16[4,96,1536]{2,1,0:T(8,128)(2,1)}), bf16[4,96,1536]{2,1,0:T(8,128)(2,1)}, u32[]{:S(2)}, u32[]{:S(2)}) async-start(bf16[4,96,1536]{2,1,0:T(8,128)(2,1)} %add_convert_fusion), calls=%async_computation | async-start | bytes 2359296 | tf_op jit(solution)/shard_map/cond/branch_1_fun/all_to_all | solution.py:703
  127.2 1.7 convert_add_fusion
  129.1 2.6 %add_convert_fusion.1 = bf16[1176,384]{1,0:T(8,128)(2,1)} fusion(f32[1176,384]{1,0:T(8,128)S(1)} %copy-done.10, bf16[1176,384]{1,0:T(8,128)(2,1)} %get-tuple-element.33), kind=kLoop, calls=%fused_computation.2 | loop fusion | flops 1354752 | bytes 3612672 | tf_op jit(solution)/shard_map/cond/branch_1_fun/convert_element_type | solution.py:42
  131.7 1.7 collective-permute-start.3
  133.4 10.7 %collective-permute-done.3 = bf16[896]{0:T(1024)(128)(2,1)S(1)} collective-permute-done((bf16[896]{0:T(1024)(128)(2,1)S(1)}, bf16[896]{0:T(1024)(128)(2,1)S(1)}, u32[]{:S(2)}, u32[]{:S(2)}) %collective-permute-start.3) | collective-permute-done | bytes 1824 | tf_op jit(solution)/shard_map/cond/branch_1_fun/ppermute | solution.py:649
  144.2 1.2 fusion
  145.5 2.7 %collective-permute-start.5 = (bf16[56,1536]{1,0:T(8,128)(2,1)S(1)}, bf16[56,1536]{1,0:T(8,128)(2,1)S(1)}, u32[]{:S(2)}, u32[]{:S(2)}) collective-permute-start(bf16[56,1536]{1,0:T(8,128)(2,1)S(1)} %get-tuple-element.110), channel_id=1, source_target_pairs={{0,16},{4,20},{8,24},{12,28},{16,0},{20,4},{24,8},{28,12},{1,17},{... | collective-permute-start | bytes 516104 | tf_op jit(solution)/shard_map/cond/branch_1_fun/ppermute | solution.py:649
  148.2 3.0 %collective-permute-start.6 = (bf16[56,1536]{1,0:T(8,128)(2,1)S(1)}, bf16[56,1536]{1,0:T(8,128)(2,1)S(1)}, u32[]{:S(2)}, u32[]{:S(2)}) collective-permute-start(bf16[56,1536]{1,0:T(8,128)(2,1)S(1)} %get-tuple-element.111), channel_id=1, source_target_pairs={{0,24},{4,28},{8,16},{12,20},{16,8},{20,12},{24,0},{28,4},{1,25},{... | collective-permute-start | bytes 516104 | tf_op jit(solution)/shard_map/cond/branch_1_fun/ppermute | solution.py:649
  151.2 13.3 %all-to-all-done = bf16[4,96,1536]{2,1,0:T(8,128)(2,1)} async-done(((bf16[4,96,1536]{2,1,0:T(8,128)(2,1)}), bf16[4,96,1536]{2,1,0:T(8,128)(2,1)}, u32[]{:S(2)}, u32[]{:S(2)}) %all-to-all-start) | async-done | bytes 1179680 | tf_op jit(solution)/shard_map/cond/branch_1_fun/all_to_all | solution.py:703
  164.5 2.2 %convert_reduce_fusion = (f32[96,768]{1,0:T(8,128)}, f32[96,768]{1,0:T(8,128)S(1)}) fusion(bf16[4,96,1536]{2,1,0:T(8,128)(2,1)} %all-to-all-done), kind=kLoop, calls=%fused_computation.9 | loop fusion | flops 1032192 | bytes 1769472 | tf_op jit(solution)/shard_map/cond/branch_1_fun/reduce_sum | solution.py:705
  166.7 1.6 collective-permute-done.4
  169.0 0.7 add_add_fusion.1
  169.6 1.0 add_add_fusion
  171.2 1.2 copy-done.3
  172.4 1.2 copy-done.5
  173.5 7.1 %token_rows.1 = bf16[1176,768]{1,0:T(8,128)(2,1)} custom-call(bf16[1176,768]{1,0:T(8,128)(2,1)} %get-tuple-element.98.sent_ref, bf16[1176,768]{1,0:T(8,128)(2,1)} %collective-permute-done.13.came_ref, bf16[1176,768]{1,0:T(8,128)(2,1)S(1)} %copy-done, bf16[1,768]{1,0:T(2,128)(2,1)S(1)} %copy-done.6, bf16[1176,384]{1,0:T(8,128)(2,1)S(1)} %copy-done.3, ...), custom_call_target="tpu_custom_call" | custom-call | flops 2100000000 | bytes 1048576 | tf_op jit(solution)/shard_map/token_rows/pallas_call | solution.py:626
  (72 shorter events, 4.8 us)
Async XLA Ops:
  0.6 24.8 %collective-permute-start.7 = (bf16[1176,384]{1,0:T(8,128)(2,1)}, bf16[1176,384]{1,0:T(8,128)(2,1)S(1)}, u32[]{:S(2)}, u32[]{:S(2)}) collective-permute-start(bf16[1176,384]{1,0:T(8,128)(2,1)} %mine_ref.5), channel_id=1, source_target_pairs={{0,2},{2,0},{1,3},{3,1},{4,6},{6,4},{5,7},{7,5},{8,10},{10,8},{9,1... | collective-permute-start | bytes 2709512 | tf_op jit(solution)/shard_map/ppermute | solution.py:649
  3.6 21.8 %collective-permute-start.8 = (bf16[768,768]{1,0:T(8,128)(2,1)}, bf16[768,768]{1,0:T(8,128)(2,1)S(1)}, u32[]{:S(2)}, u32[]{:S(2)}) collective-permute-start(bf16[768,768]{1,0:T(8,128)(2,1)} %refs_0_.1), channel_id=1, source_target_pairs={{0,1},{1,0},{2,3},{3,2},{4,5},{5,4},{6,7},{7,6},{8,9},{9,8},{10,11... | collective-permute-start | bytes 3538952 | tf_op jit(solution)/shard_map/ppermute | solution.py:649
  3.6 21.9 %collective-permute-start.9 = (bf16[768,768]{1,0:T(8,128)(2,1)}, bf16[768,768]{1,0:T(8,128)(2,1)}, u32[]{:S(2)}, u32[]{:S(2)}) collective-permute-start(bf16[768,768]{1,0:T(8,128)(2,1)} %refs_2_.1), channel_id=1, source_target_pairs={{0,1},{1,0},{2,3},{3,2},{4,5},{5,4},{6,7},{7,6},{8,9},{9,8},{10,11... | collective-permute-start | bytes 3538952 | tf_op jit(solution)/shard_map/ppermute | solution.py:649
  25.5 27.9 %copy-start.13 = (bf16[1176,384]{1,0:T(8,128)(2,1)}, bf16[1176,384]{1,0:T(8,128)(2,1)S(1)}, u32[]{:S(2)}) copy-start(bf16[1176,384]{1,0:T(8,128)(2,1)S(1)} %get-tuple-element.76.att_ref) | copy-start | bytes 2709508
  25.5 1.3 copy-start.17
  53.3 9.2 %collective-permute-start.10 = (bf16[2,4,96,1536]{3,2,1,0:T(8,128)(2,1)}, bf16[2,4,96,1536]{3,2,1,0:T(8,128)(2,1)S(1)}, u32[]{:S(2)}, u32[]{:S(2)}) collective-permute-start(bf16[2,4,96,1536]{3,2,1,0:T(8,128)(2,1)} %get-tuple-element.79), channel_id=1, source_target_pairs={{0,1},{1,0},{2,3},{3,2},{4,5},{5,4},{6,7},{7,6},{8,9},{9,8},{10,11... | collective-permute-start | bytes 7077896 | tf_op jit(solution)/shard_map/ppermute | solution.py:649
  53.4 9.1 %copy-start.9 = (bf16[2,4,96,1536]{3,2,1,0:T(8,128)(2,1)S(1)}, bf16[2,4,96,1536]{3,2,1,0:T(8,128)(2,1)}, u32[]{:S(2)}) copy-start(bf16[2,4,96,1536]{3,2,1,0:T(8,128)(2,1)} %get-tuple-element.78) | copy-start | bytes 7077892
  62.2 22.8 %collective-permute-start.11 = (bf16[1176,384]{1,0:T(8,128)(2,1)}, bf16[1176,384]{1,0:T(8,128)(2,1)}, u32[]{:S(2)}, u32[]{:S(2)}) collective-permute-start(bf16[1176,384]{1,0:T(8,128)(2,1)} %get-tuple-element.87), channel_id=1, source_target_pairs={{0,2},{2,0},{1,3},{3,1},{4,6},{6,4},{5,7},{7,5},{8,10},{10,8},{9,1... | collective-permute-start | bytes 2709512 | tf_op jit(solution)/shard_map/ppermute | solution.py:649
  64.4 28.2 %collective-permute-start.12 = (bf16[4,96,1536]{2,1,0:T(8,128)(2,1)S(1)}, bf16[4,96,1536]{2,1,0:T(8,128)(2,1)S(1)}, u32[]{:S(2)}, u32[]{:S(2)}) collective-permute-start(bf16[4,96,1536]{2,1,0:T(8,128)(2,1)S(1)} %get-tuple-element.114), channel_id=1, source_target_pairs={{0,4},{4,0},{8,12},{12,8},{16,20},{20,16},{24,28},{28,24},{1,5},{5... | collective-permute-start | bytes 3538952 | tf_op jit(solution)/shard_map/ppermute | solution.py:649
  66.2 26.3 %copy-start = (bf16[1176,768]{1,0:T(8,128)(2,1)S(1)}, bf16[1176,768]{1,0:T(8,128)(2,1)}, u32[]{:S(2)}) copy-start(bf16[1176,768]{1,0:T(8,128)(2,1)} %tok_ref.7) | copy-start | bytes 5419012
  66.2 26.3 %copy-start.1 = (bf16[1176,768]{1,0:T(8,128)(2,1)S(1)}, bf16[1176,768]{1,0:T(8,128)(2,1)}, u32[]{:S(2)}) copy-start(bf16[1176,768]{1,0:T(8,128)(2,1)} %get-tuple-element.90.mlp_ref) | copy-start | bytes 5419012
  66.2 26.3 %copy-start.2 = (bf16[768,1152]{1,0:T(8,128)(2,1)S(1)}, bf16[768,1152]{1,0:T(8,128)(2,1)}, u32[]{:S(2)}) copy-start(bf16[768,1152]{1,0:T(8,128)(2,1)} %w_ref.3) | copy-start | bytes 5308420
  92.5 8.2 %copy-start.11 = (bf16[4,96,1536]{2,1,0:T(8,128)(2,1)}, bf16[4,96,1536]{2,1,0:T(8,128)(2,1)S(1)}, u32[]{:S(2)}) copy-start(bf16[4,96,1536]{2,1,0:T(8,128)(2,1)S(1)} %collective-permute-done.12) | copy-start | bytes 3538948
  100.8 69.8 %collective-permute-start.13 = (bf16[1176,768]{1,0:T(8,128)(2,1)}, bf16[1176,768]{1,0:T(8,128)(2,1)}, u32[]{:S(2)}, u32[]{:S(2)}) collective-permute-start(bf16[1176,768]{1,0:T(8,128)(2,1)} %get-tuple-element.98.sent_ref), channel_id=1, source_target_pairs={{0,2},{2,0},{1,3},{3,1},{4,6},{6,4},{5,7},{7,5},{8,10},{10,8},{9,1... | collective-permute-start | bytes 5419016 | tf_op jit(solution)/shard_map/ppermute | solution.py:649
  102.5 68.7 %copy-start.6 = (bf16[1,768]{1,0:T(2,128)(2,1)S(1)}, bf16[1,768]{1,0:T(2,128)(2,1)}, u32[]{:S(2)}) copy-start(bf16[1,768]{1,0:T(2,128)(2,1)} %reshape.50.gain_ref) | copy-start | bytes 4612
  102.5 9.2 %copy-start.8 = (bf16[4,96,1536]{2,1,0:T(8,128)(2,1)S(1)}, bf16[4,96,1536]{2,1,0:T(8,128)(2,1)}, u32[]{:S(2)}) copy-start(bf16[4,96,1536]{2,1,0:T(8,128)(2,1)} %get-tuple-element.20) | copy-start | bytes 3538948 | tf_op jit(solution)/shard_map/cond
  102.5 9.2 %copy-start.12 = (bf16[4,96,1536]{2,1,0:T(8,128)(2,1)S(1)}, bf16[4,96,1536]{2,1,0:T(8,128)(2,1)}, u32[]{:S(2)}) copy-start(bf16[4,96,1536]{2,1,0:T(8,128)(2,1)} %get-tuple-element.21) | copy-start | bytes 3538948 | tf_op jit(solution)/shard_map/cond
  111.0 16.2 %collective-permute-start.1 = (bf16[2,4,48,1536]{3,2,1,0:T(8,128)(2,1)}, bf16[2,4,48,1536]{3,2,1,0:T(8,128)(2,1)}, u32[]{:S(2)}, u32[]{:S(2)}) collective-permute-start(bf16[2,4,48,1536]{3,2,1,0:T(8,128)(2,1)} %get-tuple-element.29), channel_id=1, source_target_pairs={{0,1},{1,0},{2,3},{3,2},{4,5},{5,4},{6,7},{7,6},{8,9},{9,8},{10,11... | collective-permute-start | bytes 3538952 | tf_op jit(solution)/shard_map/cond/branch_1_fun/ppermute | solution.py:649
  111.1 16.0 %collective-permute-start = (f32[896]{0:T(1024)S(1)}, f32[896]{0:T(1024)S(1)}, u32[]{:S(2)}, u32[]{:S(2)}) collective-permute-start(f32[896]{0:T(1024)S(1)} %pad_maximum_fusion), channel_id=1, source_target_pairs={{0,1},{1,0},{2,3},{3,2},{4,5},{5,4},{6,7},{7,6},{8,9},{9,8},{10,11... | collective-permute-start | bytes 10760 | tf_op jit(solution)/shard_map/cond/branch_1_fun/ppermute | solution.py:649
  112.9 51.5 %all-to-all-start = ((bf16[4,96,1536]{2,1,0:T(8,128)(2,1)}), bf16[4,96,1536]{2,1,0:T(8,128)(2,1)}, u32[]{:S(2)}, u32[]{:S(2)}) async-start(bf16[4,96,1536]{2,1,0:T(8,128)(2,1)} %add_convert_fusion), calls=%async_computation | async-start | bytes 2359296 | tf_op jit(solution)/shard_map/cond/branch_1_fun/all_to_all | solution.py:703
  127.2 1.9 %copy-start.10 = (f32[1176,384]{1,0:T(8,128)S(1)}, f32[1176,384]{1,0:T(8,128)}, u32[]{:S(2)}) copy-start(f32[1176,384]{1,0:T(8,128)} %get-tuple-element.32) | copy-start | bytes 5419012 | tf_op jit(solution)/shard_map/cond
  128.9 2.8 %copy-start.7 = (bf16[2,4,48,1536]{3,2,1,0:T(8,128)(2,1)}, bf16[2,4,48,1536]{3,2,1,0:T(8,128)(2,1)S(1)}, u32[]{:S(2)}) copy-start(bf16[2,4,48,1536]{3,2,1,0:T(8,128)(2,1)S(1)} %convert_add_fusion) | copy-start | bytes 3538948 | tf_op jit(solution)/shard_map/cond
  129.0 15.2 %collective-permute-start.2 = (bf16[4,48,1536]{2,1,0:T(8,128)(2,1)S(1)}, bf16[4,48,1536]{2,1,0:T(8,128)(2,1)S(1)}, u32[]{:S(2)}, u32[]{:S(2)}) collective-permute-start(bf16[4,48,1536]{2,1,0:T(8,128)(2,1)S(1)} %slice_bitcast_fusion), channel_id=1, source_target_pairs={{0,4},{4,0},{8,12},{12,8},{16,20},{20,16},{24,28},{28,24},{1,5},{5... | collective-permute-start | bytes 1769480 | tf_op jit(solution)/shard_map/cond/branch_1_fun/ppermute | solution.py:649
  131.7 12.4 %collective-permute-start.3 = (bf16[896]{0:T(1024)(128)(2,1)S(1)}, bf16[896]{0:T(1024)(128)(2,1)S(1)}, u32[]{:S(2)}, u32[]{:S(2)}) collective-permute-start(bf16[896]{0:T(1024)(128)(2,1)S(1)} %add_convert_fusion.3), channel_id=1, source_target_pairs={{0,4},{4,0},{8,12},{12,8},{16,20},{20,16},{24,28},{28,24},{1,5},{5... | collective-permute-start | bytes 5384 | tf_op jit(solution)/shard_map/cond/branch_1_fun/ppermute | solution.py:649
  145.5 22.8 %collective-permute-start.5 = (bf16[56,1536]{1,0:T(8,128)(2,1)S(1)}, bf16[56,1536]{1,0:T(8,128)(2,1)S(1)}, u32[]{:S(2)}, u32[]{:S(2)}) collective-permute-start(bf16[56,1536]{1,0:T(8,128)(2,1)S(1)} %get-tuple-element.110), channel_id=1, source_target_pairs={{0,16},{4,20},{8,24},{12,28},{16,0},{20,4},{24,8},{28,12},{1,17},{... | collective-permute-start | bytes 516104 | tf_op jit(solution)/shard_map/cond/branch_1_fun/ppermute | solution.py:649
  148.2 20.1 %collective-permute-start.6 = (bf16[56,1536]{1,0:T(8,128)(2,1)S(1)}, bf16[56,1536]{1,0:T(8,128)(2,1)S(1)}, u32[]{:S(2)}, u32[]{:S(2)}) collective-permute-start(bf16[56,1536]{1,0:T(8,128)(2,1)S(1)} %get-tuple-element.111), channel_id=1, source_target_pairs={{0,24},{4,28},{8,16},{12,20},{16,8},{20,12},{24,0},{28,4},{1,25},{... | collective-permute-start | bytes 516104 | tf_op jit(solution)/shard_map/cond/branch_1_fun/ppermute | solution.py:649
  151.2 17.1 %collective-permute-start.4 = (bf16[56,1536]{1,0:T(8,128)(2,1)S(1)}, bf16[56,1536]{1,0:T(8,128)(2,1)S(1)}, u32[]{:S(2)}, u32[]{:S(2)}) collective-permute-start(bf16[56,1536]{1,0:T(8,128)(2,1)S(1)} %get-tuple-element.109), channel_id=1, source_target_pairs={{0,8},{4,12},{8,0},{12,4},{16,24},{20,28},{24,16},{28,20},{1,9},{5... | collective-permute-start | bytes 516104 | tf_op jit(solution)/shard_map/cond/branch_1_fun/ppermute | solution.py:649
  170.6 10.1 %copy-start.14 = (f32[96,768]{1,0:T(8,128)}, f32[96,768]{1,0:T(8,128)S(1)}, u32[]{:S(2)}) copy-start(f32[96,768]{1,0:T(8,128)S(1)} %get-tuple-element.72) | copy-start | bytes 884740
  170.6 10.1 %copy-start.15 = (f32[48,1152]{1,0:T(8,128)}, f32[48,1152]{1,0:T(8,128)S(1)}, u32[]{:S(2)}) copy-start(f32[48,1152]{1,0:T(8,128)S(1)} %get-tuple-element.69) | copy-start | bytes 663556
  170.6 10.1 %collective-permute-start.14 = (f32[1536]{0:T(1024)S(1)}, f32[1536]{0:T(1024)S(1)}, u32[]{:S(2)}, u32[]{:S(2)}) collective-permute-start(f32[1536]{0:T(1024)S(1)} %get-tuple-element.101), channel_id=1, source_target_pairs={{0,2},{2,0},{1,3},{3,1},{4,6},{6,4},{5,7},{7,5},{8,10},{10,8},{9,1... | collective-permute-start | bytes 18440 | tf_op jit(solution)/shard_map/ppermute | solution.py:649
  171.2 1.2 copy-start.3
  172.4 1.2 copy-start.5
  (2 other events, 1.6 us)

commit v2 on v1

--- a/solution.py
+++ b/solution.py
@@ -14,6 +14,7 @@
 LANES = 128
 VMEM = pltpu.VMEM
 SCALE = 1.0
+ROOM = dict(forward=40, backward=24, dense=32, outputs=24, features=24, weights=24, token_rows=24)
 
 
 def cost(microseconds):
@@ -213,7 +214,7 @@
         ],
         in_specs=[pl.BlockSpec(memory_space=pltpu.SMEM)] + [whole] * 4,
         out_specs=[whole] * 6,
-        compiler_params=pltpu.CompilerParams(vmem_limit_bytes=56 * 2**20),
+        compiler_params=pltpu.CompilerParams(vmem_limit_bytes=ROOM["forward"] * 2**20),
         cost_estimate=cost(24),
     )(big_images, tokens, norm_gain.reshape(1, -1), w_qkv, qk_gains)
 
@@ -337,12 +338,12 @@
             VMEM((2, rows, LANES), jnp.float32),
             VMEM((2, padded, LANES), jnp.float32),
         ],
-        compiler_params=pltpu.CompilerParams(vmem_limit_bytes=56 * 2**20),
+        compiler_params=pltpu.CompilerParams(vmem_limit_bytes=ROOM["backward"] * 2**20),
         cost_estimate=cost(36),
     )(big_images, q_rows, k_rows, v_rows, do_rows, inverses, qk_gains)
 
 
-FINE = 6 * PATCHES // 7
+FINE = 2 * PATCHES
 
 
 def in_order(mine, other):
@@ -442,7 +443,7 @@
         ],
         scratch_shapes=[VMEM((tiles, tile, width), jnp.bfloat16)] * 2
         + [VMEM((tiles, tile, size), jnp.bfloat16) for size in sizes] * 2,
-        compiler_params=pltpu.CompilerParams(vmem_limit_bytes=60 * 2**20),
+        compiler_params=pltpu.CompilerParams(vmem_limit_bytes=ROOM["dense"] * 2**20),
         cost_estimate=cost(24),
     )(normed, mine, other, *w_in_pieces, *w_back_pieces)
 
@@ -507,7 +508,7 @@
             row_tile(width // 2),
             pl.BlockSpec((heads, padded, LANES), lambda step: (0, 0, 0)),
         ],
-        compiler_params=pltpu.CompilerParams(vmem_limit_bytes=56 * 2**20),
+        compiler_params=pltpu.CompilerParams(vmem_limit_bytes=ROOM["outputs"] * 2**20),
         cost_estimate=cost(6),
     )(part, tokens, attended, mine, other, w_out_t)
 
@@ -548,57 +549,51 @@
             pl.BlockSpec((tile, width), lambda step: (step, 0)),
             pl.BlockSpec((8, width), lambda step: (0, 0)),
         ],
-        compiler_params=pltpu.CompilerParams(vmem_limit_bytes=40 * 2**20),
+        compiler_params=pltpu.CompilerParams(vmem_limit_bytes=ROOM["features"] * 2**20),
         cost_estimate=cost(0.3 * count),
     )(grad_joined, w_qkv, grad_mlp, tokens)
 
 
-def weights_kernel(chunks, normed_t_ref, dy_t_ref, joined_ref, att_ref, keep_ref, send_ref):
-    halves, rows, columns = keep_ref.shape[1:]
-    tokens = att_ref.shape[0]
+def weights_kernel(*refs):
+    keep_ref, send_ref = refs[-2:]
+    halves, rows = keep_ref.shape[1:3]
     odd, side = lax.axis_index("dp") & 1, lax.axis_index("hid")
-
-    def finish(left_ref, right_ref):
+    at = 0
+    for left_ref, right_ref in zip(refs[:-2:2], refs[1:-2:2]):
+        tokens, columns = right_ref.shape
         total = times(left_ref[:, :tokens], right_ref[...])
+        cols = slice(at, at + columns)
+        at += columns
         for half in range(halves):
             for parity in range(2):
                 start = 2 * (2 * half + parity) * rows
                 even, uneven = total[start : start + rows], total[start + rows : start + 2 * rows]
-                keep_ref[odd ^ parity, half] = low(jnp.where(side == 0, even, uneven))
-                send_ref[odd ^ parity, half] = low(jnp.where(side == 0, uneven, even))
-
-    @pl.when(pl.program_id(0) < chunks)
-    def _():
-        finish(normed_t_ref, joined_ref)
-
-    @pl.when(pl.program_id(0) == chunks)
-    def _():
-        finish(dy_t_ref, att_ref)
-
-
-def weights(normed_t, dy_t, grad_joined, attended):
+                keep_ref[odd ^ parity, half, :, cols] = low(jnp.where(side == 0, even, uneven))
+                send_ref[odd ^ parity, half, :, cols] = low(jnp.where(side == 0, uneven, even))
+
+
+def weights(*products):
     groups = lax.axis_size("dp")
-    rows, columns = attended.shape
-    chunks = grad_joined.shape[1] // columns
-    shape = (2, groups // 2, normed_t.shape[0] // (2 * groups), columns)
-    whole = jax.ShapeDtypeStruct(shape[:3] + (columns * (chunks + 1),), jnp.bfloat16)
-    turned = pl.BlockSpec(normed_t.shape, lambda step: (0, 0))
-    out = pl.BlockSpec(shape, lambda step: (0, 0, 0, step))
+    columns = sum(size for _, _, size, _ in products)
+    shape = (2, groups // 2, products[0][0].shape[0] // (2 * groups), columns)
+    whole = lambda shape: pl.BlockSpec(shape, lambda step: (0,) * len(shape))
+    specs, operands = [], []
+    for turned, right, size, place in products:
+        specs += [
+            whole(turned.shape),
+            pl.BlockSpec((right.shape[0], size), lambda step, place=place: (0, place)),
+        ]
+        operands += [turned, right]
     return pl.pallas_call(
-        functools.partial(weights_kernel, chunks),
+        weights_kernel,
         name="weights",
-        grid=(chunks + 1,),
-        out_shape=[whole, whole],
-        in_specs=[
-            turned,
-            turned,
-            pl.BlockSpec((rows, columns), lambda step: (0, jnp.minimum(step, chunks - 1))),
-            pl.BlockSpec((rows, columns), lambda step: (0, 0)),
-        ],
-        out_specs=[out, out],
-        compiler_params=pltpu.CompilerParams(vmem_limit_bytes=48 * 2**20),
-        cost_estimate=cost(1),
-    )(normed_t, dy_t, grad_joined, attended)
+        grid=(1,),
+        out_shape=[jax.ShapeDtypeStruct(shape, jnp.bfloat16)] * 2,
+        in_specs=specs,
+        out_specs=[whole(shape)] * 2,
+        compiler_params=pltpu.CompilerParams(vmem_limit_bytes=ROOM["weights"] * 2**20),
+        cost_estimate=cost(3),
+    )(*operands)
 
 
 def tokens_kernel(sent_ref, came_ref, tok_ref, gain_ref, mine_ref, other_ref, *refs):
@@ -639,7 +634,7 @@
         + [pl.BlockSpec(memory_space=pl.ANY)] * len(more),
         out_specs=far(width),
         input_output_aliases={6: 0} if more else {},
-        compiler_params=pltpu.CompilerParams(vmem_limit_bytes=40 * 2**20),
+        compiler_params=pltpu.CompilerParams(vmem_limit_bytes=ROOM["token_rows"] * 2**20),
         cost_estimate=cost(0.3 * count),
     )(sent, came, tokens, norm_gain.reshape(1, -1), mine, other, *more)
 
@@ -675,14 +670,15 @@
     return pieces[0]
 
 
-def row_blocks(normed_t, dy_t, grad_joined, attended):
+def row_blocks(*products):
     groups, sides = lax.axis_size("dp"), lax.axis_size("hid")
-    width = normed_t.shape[0]
+    width = products[0][0].shape[0]
     if sides == 2 and width % (16 * groups * sides) == 0:
-        keep, send = weights(normed_t, dy_t, grad_joined, attended)
+        keep, send = weights(*products)
         return wide(keep) + wide(swap(send, "hid", 1))
-    tokens = attended.shape[0]
-    parts = [times(normed_t[:, :tokens], grad_joined), times(dy_t[:, :tokens], attended)]
+    parts = []
+    for turned, right, size, place in products:
+        parts.append(times(turned[:, : right.shape[0]], right[:, place * size : place * size + size]))
     shaped = jnp.concatenate(parts, axis=1).reshape(groups // 2, 2, sides, width // (groups * sides), -1)
     odd = lax.axis_index("dp") & 1
     shaped = shaped[:, odd ^ jnp.arange(2)][:, :, lax.axis_index("hid") ^ jnp.arange(sides)]
@@ -705,29 +701,20 @@
     return tuple(jnp.sum(wide(part), axis=0) for part in (total[:, :, :half], total[:, :, half:]))
 
 
-def sum_far(kept, came, extra, extra_came, columns):
-    half, rows, width = kept.shape
-    extra = low(wide(extra) + wide(extra_came))
-    extra = jnp.pad(extra, (0, 8 * width - extra.shape[0])).reshape(1, 8, width)
-    total = low(wide(kept) + wide(came))
-    total = jnp.concatenate([total, jnp.broadcast_to(extra, (half, 8, width))], axis=1)
+def far_terms(total):
     me = lax.axis_index("dp") // 2
     terms = [lax.dynamic_index_in_dim(total, me, keepdims=False)]
-    for step in range(1, half):
+    for step in range(1, total.shape[0]):
         block = lax.dynamic_index_in_dim(total, me ^ step, keepdims=False)
         terms.append(swap(block, "dp", 2 * step))
-
-    def added(part):
-        values = [wide(part(term)) for term in terms]
-        while len(values) > 1:
-            values = [first + second for first, second in zip(values[::2], values[1::2])]
-        return values[0]
-
-    return (
-        added(lambda term: term[:rows, :columns]),
-        added(lambda term: term[:rows, columns:]),
-        added(lambda term: term[rows]),
-    )
+    return terms
+
+
+def added(terms):
+    values = [wide(term) for term in terms]
+    while len(values) > 1:
+        values = [first + second for first, second in zip(values[::2], values[1::2])]
+    return values[0]
 
 
 def sum_everywhere(value, axes):
@@ -756,44 +743,43 @@
     grad_joined, qk_part = backward(big_images, q_rows, k_rows, v_rows, do_rows, inverses, qk_gains)
     grad_joined, out_came, mlp_came = lax.optimization_barrier((grad_joined, out_came, mlp_came))
     mine, gain_part = features(0, tokens.shape[0] // FINE, grad_joined, w_qkv, grad_mlp, tokens)
+    mine, mlp_came = lax.optimization_barrier((mine, mlp_came))
     came = swap(mine, "hg", 1)
-
-    def weight_sums(normed_t, dy_t, grad_joined, attended, mlp_kept, mlp_came, gain_part, qk_part, kept, out_came):
-        blocks = row_blocks(normed_t, dy_t, grad_joined, attended)
-        mlp_grads = sum_rest(mlp_kept, mlp_came)
+    columns = attended.shape[1]
+
+    def weight_sums(normed_t, dy_t, grad_joined, attended, gain_part, qk_part, kept, out_came):
+        first_kept, first_came = halve(row_blocks((normed_t, grad_joined, 2 * columns, 0)))
+        blocks = row_blocks((normed_t, grad_joined, columns, 2), (dy_t, attended, columns, 0))
         small = jnp.concatenate([gain_part[0], qk_part[0, :size], qk_part[0, LANES : LANES + size]])
         small = low(sum_everywhere(small, ("hid",)))
         small, blocks = lax.optimization_barrier((small, blocks))
-        blocks_kept, blocks_came = halve(blocks)
-        sums = sum_far(blocks_kept, blocks_came, small, swap(small, "dp", 1), grad_joined.shape[1])
-        return mlp_grads, sums, low(kept + wide(out_came))
+        second_kept, second_came = halve(blocks)
+        small = low(wide(small) + wide(swap(small, "dp", 1)))
+        small = jnp.pad(small, (0, 8 * 2 * columns - small.shape[0])).reshape(1, 8, -1)
+        first = added(far_terms(low(wide(first_kept) + wide(first_came))))
+        second = low(wide(second_kept) + wide(second_came))
+        small = jnp.broadcast_to(small, second.shape[:1] + small.shape[1:])
+        return first, jnp.concatenate([second, small], axis=1), low(kept + wide(out_came))
 
     def no_sums(*operands):
         return jax.tree.map(lambda kind: jnp.zeros(kind.shape, kind.dtype), kinds)
 
-    operands = (
-        normed_t,
-        dy_t,
-        grad_joined,
-        attended,
-        mlp_kept,
-        mlp_came,
-        gain_part,
-        qk_part,
-        kept,
-        out_came,
-    )
+    operands = (normed_t, dy_t, grad_joined, attended, gain_part, qk_part, kept, out_came)
     kinds = jax.eval_shape(weight_sums, *operands)
-    mlp_grads, sums, output = lax.cond(big_images[0] >= 0, weight_sums, no_sums, *operands)
-    w_in_grad, w_back_grad = mlp_grads
-    w_qkv_grad, w_out_t_grad, small = sums
-    came, small = lax.optimization_barrier((came, small))
+    first, second, output = lax.cond(big_images[0] >= 0, weight_sums, no_sums, *operands)
+    w_in_grad, w_back_grad = sum_rest(mlp_kept, mlp_came)
+    terms = far_terms(second)
+    token_grad = token_rows(0, mine, came, tokens, norm_gain, cotangent, other, None)
+    terms[1], token_grad = lax.optimization_barrier((terms[1], token_grad))
+    rows = first.shape[0]
+    w_qkv_grad = jnp.concatenate([first, added([term[:rows, :columns] for term in terms])], axis=1)
+    w_out_t_grad = added([term[:rows, columns:] for term in terms])
+    small = added([term[rows:] for term in terms]).reshape(-1)
     small = sum_everywhere(small, ("hg",))
     own = lax.axis_index("dp") * lax.axis_size("hid") + lax.axis_index("hid")
     gain_rows = width // (groups * lax.axis_size("hid"))
     norm_gain_grad = lax.dynamic_slice_in_dim(small, own * gain_rows, gain_rows, 0)
     qk_gains_grad = small[width : width + 2 * size].reshape(2, size)
-    token_grad = token_rows(0, mine, came, tokens, norm_gain, cotangent, other, None)
     return (
         output,
         token_grad,

time: 183 us -> 154 us (0.84); the launches traced: 182 us -> 156 us
  waiting for transfers between devices: 33.1 us -> 11.9 us
  starting transfers between devices: 30.2 us -> 24.5 us
  Pallas kernels: 97.3 us -> 93.4 us
  local copies, waits for them, and re-layouts: 8.12 us -> 11.2 us
    all_to_all x1, waiting for transfers between devices: 13.3 us -> 0.01 us  [sum_rest(): lax.all_to_all(total, 'dp', 0, 0, axis_index_groups=groups, tiled=True)]
    pallas_call x1, Pallas kernels: 18.8 us -> 29.4 us  [backward(): pl.pallas_call(backward_kernel, name='backward', grid=(heads // 2,), out_...]
    ppermute x15 -> x20, waiting for transfers between devices: 19.8 us -> 11.9 us  [swap(): lax.ppermute(value, axis, [(place, place ^ bit) for place in range(size)])]
    all_to_all x1, starting transfers between devices: 14.2 us -> 6.57 us  [sum_rest(): lax.all_to_all(total, 'dp', 0, 0, axis_index_groups=groups, tiled=True)]
    pallas_call x1, Pallas kernels: 26.5 us -> 21.7 us  [dense(): pl.pallas_call(functools.partial(dense_kernel, count, tiles), name='dense...]
    pallas_call x1, Pallas kernels: 8.2 us -> 3.76 us  [features(): pl.pallas_call(features_kernel, name='features', grid=(count,), out_shape...]
    pallas_call x1, Pallas kernels: 8.85 us -> 5.8 us  [outputs(): pl.pallas_call(outputs_kernel, name='outputs', grid=(rows // tile,), out_...]
    unnamed x26 -> x32, local copies, waits for them, and re-layouts: 3.72 us -> 6.44 us
  transfers between devices with their start and end apart: 16 -> 21, of which waited for: 4 -> 5; matrix products, arithmetic and copies ran while one was open for 8% -> 9% of each run, Pallas kernels for 34% -> 44%
where the time goes in v2:
time: 154 us; the launch traced here: 156 us
  Pallas kernels  93.4 us (61%)
  starting transfers between devices  24.5 us (16%)
  other arithmetic  13.3 us (9%)
  waiting for transfers between devices  11.9 us (8%)
  local copies, waits for them, and re-layouts  11.2 us (7%)
  between operations  1.54 us (1%)
    pallas_call x1, Pallas kernels, backward(): pl.pallas_call(backward_kernel, name='backward', grid=(heads // 2,), out_...  29.4 us
    pallas_call x1, Pallas kernels, dense(): pl.pallas_call(functools.partial(dense_kernel, count, tiles), name='dense...  21.7 us
    pallas_call x1, Pallas kernels, forward(): pl.pallas_call(forward_kernel, name='forward', out_shape=[jax.ShapeDtypeS...  19.9 us
    ppermute x20, starting transfers between devices, swap(): lax.ppermute(value, axis, [(place, place ^ bit) for place in range(size)])  17.9 us
    ppermute x20, waiting for transfers between devices, swap(): lax.ppermute(value, axis, [(place, place ^ bit) for place in range(size)])  11.9 us
    pallas_call x2, Pallas kernels, weights(): pl.pallas_call(weights_kernel, name='weights', grid=(1,), out_shape=[jax....  7.84 us
    all_to_all x1, starting transfers between devices, sum_rest(): lax.all_to_all(total, 'dp', 0, 0, axis_index_groups=groups, tiled=True)  6.57 us
    unnamed x32, local copies, waits for them, and re-layouts  6.44 us
  transfers between devices with their start and end apart: 21, of which 5 were waited for; matrix products, arithmetic and copies ran while one was open for 9% of the time, Pallas kernels for 44%

profile of v2, /device:TPU:0, one launch (start us, length us, event | category | flops | bytes accessed | tf_op | source)
XLA Modules:
  0.0 155.9 jit_solution(9776853923757004991)
XLA Ops:
  0.6 3.0 %collective-permute-start.9 = (bf16[1176,384]{1,0:T(8,128)(2,1)}, bf16[1176,384]{1,0:T(8,128)(2,1)S(1)}, u32[]{:S(2)}, u32[]{:S(2)}) collective-permute-start(bf16[1176,384]{1,0:T(8,128)(2,1)} %mine_ref.5), channel_id=1, source_target_pairs={{0,2},{2,0},{1,3},{3,1},{4,6},{6,4},{5,7},{7,5},{8,10},{10,8},{9,1... | collective-permute-start | bytes 2709512 | tf_op jit(solution)/shard_map/ppermute | solution.py:644
  5.5 1.5 copy-done
  7.0 1.5 copy-done.4
  9.1 19.9 %forward.1 = (bf16[1176,768]{1,0:T(8,128)(2,1)S(1)}, bf16[6,1280,128]{2,1,0:T(8,128)(2,1)S(1)}, bf16[6,1280,128]{2,1,0:T(8,128)(2,1)S(1)}, bf16[6,1280,128]{2,1,...) custom-call(s32[1]{0:T(128)S(6)} %copy.23.flag_ref, bf16[1176,768]{1,0:T(8,128)(2,1)S(1)} %copy-done, ...), custom_call_target="tpu_custom_call" | custom-call | flops 24000000000 | bytes 1048576 | tf_op jit(solution)/shard_map/forward/pallas_call | solution.py:204
  29.1 21.7 %dense.1 = (f32[1176,768]{1,0:T(8,128)S(1)}, bf16[1176,768]{1,0:T(8,128)(2,1)S(1)}, bf16[768,1280]{1,0:T(8,128)(2,1)}, bf16[768,1280]{1,0:T(8,128)(2,1)}, bf16[2...) custom-call(bf16[1176,768]{1,0:T(8,128)(2,1)S(1)} %get-tuple-element.69.normed_ref, ...), custom_call_target="tpu_custom_call" | custom-call | flops 24000000000 | bytes 1048576 | tf_op jit(solution)/shard_map/dense/pallas_call | solution.py:425
  50.8 5.8 %outputs.1 = (f32[1176,384]{1,0:T(8,128)}, bf16[1176,384]{1,0:T(8,128)(2,1)S(1)}, bf16[6,1280,128]{2,1,0:T(8,128)(2,1)S(1)}) custom-call(f32[1176,768]{1,0:T(8,128)S(1)} %get-tuple-element.74.part_ref, bf16[1176,768]{1,0:T(8,128)(2,1)S(1)} %copy-done.1, bf16[1176,384]{1,0:T(8,128)(2,1)S(1)} %get-tuple-element.75.att_ref, bf16[1176,384]{1,0:T(8,128)(2,1)S(1)} %copy-done.6, ...), custom_call_target="tpu_custom_call" | custom-call | flops 6000000000 | bytes 1048576 | tf_op jit(solution)/shard_map/outputs/pallas_call | solution.py:495
  57.6 29.4 %backward.1 = (bf16[1176,1152]{1,0:T(8,128)(2,1)S(1)}, f32[8,256]{1,0:T(8,128)S(1)}) custom-call(s32[1]{0:T(128)S(6)} %copy.23.flag_ref, bf16[6,1280,128]{2,1,0:T(8,128)(2,1)S(1)} %get-tuple-element.71.q_ref, bf16[6,1280,128]{2,1,0:T(8,128)(2,1)S(1)} %get-tuple-element.72.k_ref, bf16[6,1280,128]{2,1,0:T(8,128)(2,1)S(1)} %get-tuple-element.73.v_ref, ...), custom_call_target="tpu_custom_call" | custom-call | flops 35999997952 | bytes 1048576 | tf_op jit(solution)/shard_map/backward/pallas_call | solution.py:320
  87.1 3.8 %features.1 = (bf16[1176,768]{1,0:T(8,128)(2,1)S(1)}, f32[8,768]{1,0:T(8,128)S(1)}) custom-call(bf16[1176,1152]{1,0:T(8,128)(2,1)S(1)} %get-tuple-element.83.joined_ref, bf16[768,1152]{1,0:T(8,128)(2,1)S(1)} %copy-done.5, bf16[1176,768]{1,0:T(8,128)(2,1)S(1)} %get-tuple-element.84.mlp_ref, bf16[1176,768]{1,0:T(8,128)(2,1)S(1)} %copy-done.1), custom_call_target="tpu_custom_call" | custom-call | flops 900000000 | bytes 1048576 | tf_op jit(solution)/shard_map/features/pallas_call | solution.py:534
  90.9 1.3 copy-done.2
  92.2 1.4 add_convert_fusion.5
  93.5 6.6 %all-to-all-start = ((bf16[4,96,1536]{2,1,0:T(8,128)(2,1)}), bf16[4,96,1536]{2,1,0:T(8,128)(2,1)}, u32[]{:S(2)}, u32[]{:S(2)}) async-start(bf16[4,96,1536]{2,1,0:T(8,128)(2,1)} %add_convert_fusion.5), calls=%async_computation | async-start | bytes 2359296 | tf_op jit(solution)/shard_map/all_to_all | solution.py:699
  100.1 1.5 collective-permute-start.16
  101.6 34.0 %conditional.1 = (f32[48,768]{1,0:T(8,128)S(1)}, bf16[4,56,768]{2,1,0:T(8,128)(2,1)}, bf16[1176,384]{1,0:T(8,128)(2,1)}) conditional(s32[]{:T(128)} %bitcast.13, () %tuple.21, (bf16[768,1280]{1,0:T(8,128)(2,1)}, bf16[1176,1152]{1,0:T(8,128)(2,1)}, f32[8,768]{1,0:T(8,128)S(1)}, f32[8,256]{1,0:T(8,128)S(1)}, bf16[768,1280]{1,0:T(8,128)(2,1)}, ...), branch_computations={%region_0.0_spmd, %region_1.2_spmd} | conditional | flops 6005849088 | bytes 69979888 | solution.py:769
  101.6 4.8 %weights.2 = (bf16[2,4,48,768]{3,2,1,0:T(8,128)(2,1)S(1)}, bf16[2,4,48,768]{3,2,1,0:T(8,128)(2,1)}) custom-call(bf16[768,1280]{1,0:T(8,128)(2,1)} %get-tuple-element.16.refs_0_, bf16[1176,1152]{1,0:T(8,128)(2,1)} %get-tuple-element.17.refs_1_), custom_call_target="tpu_custom_call" | custom-call | flops 3000000000 | bytes 1048576 | tf_op jit(solution)/shard_map/cond/branch_1_fun/weights/pallas_call | solution.py:587
  107.0 3.1 %weights.3 = (bf16[2,4,48,768]{3,2,1,0:T(8,128)(2,1)S(1)}, bf16[2,4,48,768]{3,2,1,0:T(8,128)(2,1)}) custom-call(bf16[768,1280]{1,0:T(8,128)(2,1)S(1)} %copy-done.21, bf16[1176,1152]{1,0:T(8,128)(2,1)S(1)} %copy-done.16, bf16[768,1280]{1,0:T(8,128)(2,1)S(1)} %copy-done.22, bf16[1176,384]{1,0:T(8,128)(2,1)S(1)} %copy-done.24), custom_call_target="tpu_custom_call" | custom-call | flops 3000000000 | bytes 1048576 | tf_op jit(solution)/shard_map/cond/branch_1_fun/weights/pallas_call | solution.py:587
  110.1 1.1 add_convert_fusion
  111.4 1.3 add_convert_fusion.1
  114.0 1.2 convert_add_fusion
  115.2 1.6 %collective-permute-start.8 = (bf16[896]{0:T(1024)(128)(2,1)S(1)}, bf16[896]{0:T(1024)(128)(2,1)S(1)}, u32[]{:S(2)}, u32[]{:S(2)}) collective-permute-start(bf16[896]{0:T(1024)(128)(2,1)S(1)} %add_convert_fusion.3), channel_id=1, source_target_pairs={{0,4},{4,0},{8,12},{12,8},{16,20},{20,16},{24,28},{28,24},{1,5},{5... | collective-permute-start | bytes 5384 | tf_op jit(solution)/shard_map/cond/branch_1_fun/ppermute | solution.py:644
  118.1 5.5 %collective-permute-done.8 = bf16[896]{0:T(1024)(128)(2,1)S(1)} collective-permute-done((bf16[896]{0:T(1024)(128)(2,1)S(1)}, bf16[896]{0:T(1024)(128)(2,1)S(1)}, u32[]{:S(2)}, u32[]{:S(2)}) %collective-permute-start.8) | collective-permute-done | bytes 1824 | tf_op jit(solution)/shard_map/cond/branch_1_fun/ppermute | solution.py:644
  123.7 1.1 fusion.1
  124.8 2.1 %collective-permute-start.2 = (bf16[48,768]{1,0:T(8,128)(2,1)S(1)}, bf16[48,768]{1,0:T(8,128)(2,1)S(1)}, u32[]{:S(2)}, u32[]{:S(2)}) collective-permute-start(bf16[48,768]{1,0:T(8,128)(2,1)S(1)} %get-tuple-element.102), channel_id=1, source_target_pairs={{0,8},{4,12},{8,0},{12,4},{16,24},{20,28},{24,16},{28,20},{1,9},{5... | collective-permute-start | bytes 221192 | tf_op jit(solution)/shard_map/cond/branch_1_fun/ppermute | solution.py:644
  126.9 2.4 %collective-permute-start.3 = (bf16[48,768]{1,0:T(8,128)(2,1)S(1)}, bf16[48,768]{1,0:T(8,128)(2,1)S(1)}, u32[]{:S(2)}, u32[]{:S(2)}) collective-permute-start(bf16[48,768]{1,0:T(8,128)(2,1)S(1)} %get-tuple-element.104), channel_id=1, source_target_pairs={{0,16},{4,20},{8,24},{12,28},{16,0},{20,4},{24,8},{28,12},{1,17},{... | collective-permute-start | bytes 221192 | tf_op jit(solution)/shard_map/cond/branch_1_fun/ppermute | solution.py:644
  129.5 1.0 fusion
  131.3 2.8 %collective-permute-done.3 = bf16[48,768]{1,0:T(8,128)(2,1)S(1)} collective-permute-done((bf16[48,768]{1,0:T(8,128)(2,1)S(1)}, bf16[48,768]{1,0:T(8,128)(2,1)S(1)}, u32[]{:S(2)}, u32[]{:S(2)}) %collective-permute-start.3) | collective-permute-done | bytes 73760 | tf_op jit(solution)/shard_map/cond/branch_1_fun/ppermute | solution.py:644
  134.2 1.4 collective-permute-done.4
  137.5 1.6 %collective-permute-start.17 = (bf16[56,768]{1,0:T(8,128)(2,1)S(1)}, bf16[56,768]{1,0:T(8,128)(2,1)S(1)}, u32[]{:S(2)}, u32[]{:S(2)}) collective-permute-start(bf16[56,768]{1,0:T(8,128)(2,1)S(1)} %get-tuple-element.113), channel_id=1, source_target_pairs={{0,16},{4,20},{8,24},{12,28},{16,0},{20,4},{24,8},{28,12},{1,17},{... | collective-permute-start | bytes 258056 | tf_op jit(solution)/shard_map/ppermute | solution.py:644
  139.1 2.0 %collective-permute-start.18 = (bf16[56,768]{1,0:T(8,128)(2,1)S(1)}, bf16[56,768]{1,0:T(8,128)(2,1)S(1)}, u32[]{:S(2)}, u32[]{:S(2)}) collective-permute-start(bf16[56,768]{1,0:T(8,128)(2,1)S(1)} %get-tuple-element.112), channel_id=1, source_target_pairs={{0,24},{4,28},{8,16},{12,20},{16,8},{20,12},{24,0},{28,4},{1,25},{... | collective-permute-start | bytes 258056 | tf_op jit(solution)/shard_map/ppermute | solution.py:644
  141.1 2.4 %convert_reduce_fusion = (f32[96,768]{1,0:T(8,128)}, f32[96,768]{1,0:T(8,128)}) fusion(bf16[4,96,1536]{2,1,0:T(8,128)(2,1)} %all-to-all-done), kind=kLoop, calls=%fused_computation.27 | loop fusion | flops 1032192 | bytes 1769472 | tf_op jit(solution)/shard_map/reduce_sum | solution.py:701
  143.5 1.5 copy-done.3
  144.9 5.1 %token_rows.1 = bf16[1176,768]{1,0:T(8,128)(2,1)} custom-call(bf16[1176,768]{1,0:T(8,128)(2,1)S(1)} %copy-done.3, bf16[1176,768]{1,0:T(8,128)(2,1)} %collective-permute-done.16.came_ref, bf16[1176,768]{1,0:T(8,128)(2,1)S(1)} %copy-done.1, bf16[1,768]{1,0:T(2,128)(2,1)S(1)} %reshape.53.gain_ref, bf16[1176,384]{1,0:T(8,128)(2,1)S(1)} %copy-done.6, ...), custom_call_target="tpu_custom_call" | custom-call | flops 900000000 | bytes 1048576 | tf_op jit(solution)/shard_map/token_rows/pallas_call | solution.py:621
  152.8 1.9 %collective-permute-done.19 = f32[6144]{0:T(1024)S(1)} collective-permute-done((f32[6144]{0:T(1024)S(1)}, f32[6144]{0:T(1024)S(1)}, u32[]{:S(2)}, u32[]{:S(2)}) %collective-permute-start.19) | collective-permute-done | bytes 24608 | tf_op jit(solution)/shard_map/ppermute | solution.py:644
  (101 shorter events, 13.2 us)
Async XLA Ops:
  0.6 28.4 %collective-permute-start.9 = (bf16[1176,384]{1,0:T(8,128)(2,1)}, bf16[1176,384]{1,0:T(8,128)(2,1)S(1)}, u32[]{:S(2)}, u32[]{:S(2)}) collective-permute-start(bf16[1176,384]{1,0:T(8,128)(2,1)} %mine_ref.5), channel_id=1, source_target_pairs={{0,2},{2,0},{1,3},{3,1},{4,6},{6,4},{5,7},{7,5},{8,10},{10,8},{9,1... | collective-permute-start | bytes 2709512 | tf_op jit(solution)/shard_map/ppermute | solution.py:644
  3.6 25.4 %collective-permute-start.10 = (bf16[768,768]{1,0:T(8,128)(2,1)}, bf16[768,768]{1,0:T(8,128)(2,1)S(1)}, u32[]{:S(2)}, u32[]{:S(2)}) collective-permute-start(bf16[768,768]{1,0:T(8,128)(2,1)} %refs_0_.1), channel_id=1, source_target_pairs={{0,1},{1,0},{2,3},{3,2},{4,5},{5,4},{6,7},{7,6},{8,9},{9,8},{10,11... | collective-permute-start | bytes 3538952 | tf_op jit(solution)/shard_map/ppermute | solution.py:644
  3.6 25.4 %collective-permute-start.11 = (bf16[768,768]{1,0:T(8,128)(2,1)}, bf16[768,768]{1,0:T(8,128)(2,1)S(1)}, u32[]{:S(2)}, u32[]{:S(2)}) collective-permute-start(bf16[768,768]{1,0:T(8,128)(2,1)} %refs_2_.1), channel_id=1, source_target_pairs={{0,1},{1,0},{2,3},{3,2},{4,5},{5,4},{6,7},{7,6},{8,9},{9,8},{10,11... | collective-permute-start | bytes 3538952 | tf_op jit(solution)/shard_map/ppermute | solution.py:644
  9.1 19.9 %copy-start.6 = (bf16[1176,384]{1,0:T(8,128)(2,1)S(1)}, bf16[1176,384]{1,0:T(8,128)(2,1)}, u32[]{:S(2)}) copy-start(bf16[1176,384]{1,0:T(8,128)(2,1)} %mine_ref.5) | copy-start | bytes 2709508
  9.1 19.9 %copy-start.11 = (bf16[768,768]{1,0:T(8,128)(2,1)S(1)}, bf16[768,768]{1,0:T(8,128)(2,1)}, u32[]{:S(2)}) copy-start(bf16[768,768]{1,0:T(8,128)(2,1)} %refs_0_.1) | copy-start | bytes 3538948
  9.1 19.9 %copy-start.12 = (bf16[768,768]{1,0:T(8,128)(2,1)S(1)}, bf16[768,768]{1,0:T(8,128)(2,1)}, u32[]{:S(2)}) copy-start(bf16[768,768]{1,0:T(8,128)(2,1)} %refs_2_.1) | copy-start | bytes 3538948
  29.0 21.8 %copy-start.23 = (bf16[1176,384]{1,0:T(8,128)(2,1)}, bf16[1176,384]{1,0:T(8,128)(2,1)S(1)}, u32[]{:S(2)}) copy-start(bf16[1176,384]{1,0:T(8,128)(2,1)S(1)} %get-tuple-element.75.att_ref) | copy-start | bytes 2709508
  29.0 21.8 %copy-start.7 = (bf16[1176,384]{1,0:T(8,128)(2,1)}, bf16[1176,384]{1,0:T(8,128)(2,1)S(1)}, u32[]{:S(2)}) copy-start(bf16[1176,384]{1,0:T(8,128)(2,1)S(1)} %collective-permute-done.9.other_ref) | copy-start | bytes 2709508
  29.1 21.7 %copy-start.1 = (bf16[1176,768]{1,0:T(8,128)(2,1)S(1)}, bf16[1176,768]{1,0:T(8,128)(2,1)}, u32[]{:S(2)}) copy-start(bf16[1176,768]{1,0:T(8,128)(2,1)} %tok_ref.7) | copy-start | bytes 5419012
  29.1 21.7 %copy-start.13 = (bf16[768,384]{1,0:T(8,128)(2,1)S(1)}, bf16[768,384]{1,0:T(8,128)(2,1)}, u32[]{:S(2)}) copy-start(bf16[768,384]{1,0:T(8,128)(2,1)} %w_out_ref.1) | copy-start | bytes 1769476
  50.8 5.9 %collective-permute-start.12 = (bf16[2,4,96,1536]{3,2,1,0:T(8,128)(2,1)S(1)}, bf16[2,4,96,1536]{3,2,1,0:T(8,128)(2,1)S(1)}, u32[]{:S(2)}, u32[]{:S(2)}) collective-permute-start(bf16[2,4,96,1536]{3,2,1,0:T(8,128)(2,1)S(1)} %get-tuple-element.78), channel_id=1, source_target_pairs={{0,1},{1,0},{2,3},{3,2},{4,5},{5,4},{6,7},{7,6},{8,9},{9,8},{10,11... | collective-permute-start | bytes 7077896 | tf_op jit(solution)/shard_map/ppermute | solution.py:644
  56.6 30.5 %collective-permute-start.13 = (bf16[1176,384]{1,0:T(8,128)(2,1)S(1)}, bf16[1176,384]{1,0:T(8,128)(2,1)S(1)}, u32[]{:S(2)}, u32[]{:S(2)}) collective-permute-start(bf16[1176,384]{1,0:T(8,128)(2,1)S(1)} %get-tuple-element.82), channel_id=1, source_target_pairs={{0,2},{2,0},{1,3},{3,1},{4,6},{6,4},{5,7},{7,5},{8,10},{10,8},{9,1... | collective-permute-start | bytes 2709512 | tf_op jit(solution)/shard_map/ppermute | solution.py:644
  57.5 29.6 %collective-permute-start.14 = (bf16[4,96,1536]{2,1,0:T(8,128)(2,1)S(1)}, bf16[4,96,1536]{2,1,0:T(8,128)(2,1)S(1)}, u32[]{:S(2)}, u32[]{:S(2)}) collective-permute-start(bf16[4,96,1536]{2,1,0:T(8,128)(2,1)S(1)} %get-tuple-element.107), channel_id=1, source_target_pairs={{0,4},{4,0},{8,12},{12,8},{16,20},{20,16},{24,28},{28,24},{1,5},{5... | collective-permute-start | bytes 3538952 | tf_op jit(solution)/shard_map/ppermute | solution.py:644
  57.6 29.5 %copy-start.5 = (bf16[768,1152]{1,0:T(8,128)(2,1)S(1)}, bf16[768,1152]{1,0:T(8,128)(2,1)}, u32[]{:S(2)}) copy-start(bf16[768,1152]{1,0:T(8,128)(2,1)} %w_ref.3) | copy-start | bytes 5308420
  93.5 47.6 %all-to-all-start = ((bf16[4,96,1536]{2,1,0:T(8,128)(2,1)}), bf16[4,96,1536]{2,1,0:T(8,128)(2,1)}, u32[]{:S(2)}, u32[]{:S(2)}) async-start(bf16[4,96,1536]{2,1,0:T(8,128)(2,1)} %add_convert_fusion.5), calls=%async_computation | async-start | bytes 2359296 | tf_op jit(solution)/shard_map/all_to_all | solution.py:699
  100.1 43.3 %collective-permute-start.16 = (bf16[1176,768]{1,0:T(8,128)(2,1)}, bf16[1176,768]{1,0:T(8,128)(2,1)}, u32[]{:S(2)}, u32[]{:S(2)}) collective-permute-start(bf16[1176,768]{1,0:T(8,128)(2,1)} %copy-done.2), channel_id=1, source_target_pairs={{0,2},{2,0},{1,3},{3,1},{4,6},{6,4},{5,7},{7,5},{8,10},{10,8},{9,1... | collective-permute-start | bytes 5419016 | tf_op jit(solution)/shard_map/ppermute | solution.py:644
  101.6 5.4 %copy-start.21 = (bf16[768,1280]{1,0:T(8,128)(2,1)S(1)}, bf16[768,1280]{1,0:T(8,128)(2,1)}, u32[]{:S(2)}) copy-start(bf16[768,1280]{1,0:T(8,128)(2,1)} %get-tuple-element.16.refs_0_) | copy-start | bytes 5898244 | tf_op jit(solution)/shard_map/cond
  101.6 5.4 %copy-start.22 = (bf16[768,1280]{1,0:T(8,128)(2,1)S(1)}, bf16[768,1280]{1,0:T(8,128)(2,1)}, u32[]{:S(2)}) copy-start(bf16[768,1280]{1,0:T(8,128)(2,1)} %get-tuple-element.22.refs_2_) | copy-start | bytes 5898244 | tf_op jit(solution)/shard_map/cond
  101.6 5.4 %copy-start.24 = (bf16[1176,384]{1,0:T(8,128)(2,1)S(1)}, bf16[1176,384]{1,0:T(8,128)(2,1)}, u32[]{:S(2)}) copy-start(bf16[1176,384]{1,0:T(8,128)(2,1)} %get-tuple-element.23.refs_3_) | copy-start | bytes 2709508 | tf_op jit(solution)/shard_map/cond
  106.4 5.0 %collective-permute-start = (bf16[2,4,48,768]{3,2,1,0:T(8,128)(2,1)}, bf16[2,4,48,768]{3,2,1,0:T(8,128)(2,1)}, u32[]{:S(2)}, u32[]{:S(2)}) collective-permute-start(bf16[2,4,48,768]{3,2,1,0:T(8,128)(2,1)} %get-tuple-element.19), channel_id=1, source_target_pairs={{0,1},{1,0},{2,3},{3,2},{4,5},{5,4},{6,7},{7,6},{8,9},{9,8},{10,11... | collective-permute-start | bytes 1769480 | tf_op jit(solution)/shard_map/cond/branch_1_fun/ppermute | solution.py:644
  106.5 4.8 %collective-permute-start.5 = (f32[896]{0:T(1024)S(1)}, f32[896]{0:T(1024)S(1)}, u32[]{:S(2)}, u32[]{:S(2)}) collective-permute-start(f32[896]{0:T(1024)S(1)} %pad_maximum_fusion.1), channel_id=1, source_target_pairs={{0,1},{1,0},{2,3},{3,2},{4,5},{5,4},{6,7},{7,6},{8,9},{9,8},{10,11... | collective-permute-start | bytes 10760 | tf_op jit(solution)/shard_map/cond/branch_1_fun/ppermute | solution.py:644
  110.1 3.9 %collective-permute-start.6 = (bf16[2,4,48,768]{3,2,1,0:T(8,128)(2,1)}, bf16[2,4,48,768]{3,2,1,0:T(8,128)(2,1)}, u32[]{:S(2)}, u32[]{:S(2)}) collective-permute-start(bf16[2,4,48,768]{3,2,1,0:T(8,128)(2,1)} %get-tuple-element.25), channel_id=1, source_target_pairs={{0,1},{1,0},{2,3},{3,2},{4,5},{5,4},{6,7},{7,6},{8,9},{9,8},{10,11... | collective-permute-start | bytes 1769480 | tf_op jit(solution)/shard_map/cond/branch_1_fun/ppermute | solution.py:644
  113.5 10.2 %collective-permute-start.1 = (bf16[4,48,768]{2,1,0:T(8,128)(2,1)}, bf16[4,48,768]{2,1,0:T(8,128)(2,1)}, u32[]{:S(2)}, u32[]{:S(2)}) collective-permute-start(bf16[4,48,768]{2,1,0:T(8,128)(2,1)} %slice_bitcast_fusion.2), channel_id=1, source_target_pairs={{0,4},{4,0},{8,12},{12,8},{16,20},{20,16},{24,28},{28,24},{1,5},{5... | collective-permute-start | bytes 884744 | tf_op jit(solution)/shard_map/cond/branch_1_fun/ppermute | solution.py:644
  115.2 8.4 %collective-permute-start.8 = (bf16[896]{0:T(1024)(128)(2,1)S(1)}, bf16[896]{0:T(1024)(128)(2,1)S(1)}, u32[]{:S(2)}, u32[]{:S(2)}) collective-permute-start(bf16[896]{0:T(1024)(128)(2,1)S(1)} %add_convert_fusion.3), channel_id=1, source_target_pairs={{0,4},{4,0},{8,12},{12,8},{16,20},{20,16},{24,28},{28,24},{1,5},{5... | collective-permute-start | bytes 5384 | tf_op jit(solution)/shard_map/cond/branch_1_fun/ppermute | solution.py:644
  117.6 12.0 %collective-permute-start.7 = (bf16[4,48,768]{2,1,0:T(8,128)(2,1)}, bf16[4,48,768]{2,1,0:T(8,128)(2,1)}, u32[]{:S(2)}, u32[]{:S(2)}) collective-permute-start(bf16[4,48,768]{2,1,0:T(8,128)(2,1)} %slice_bitcast_fusion), channel_id=1, source_target_pairs={{0,4},{4,0},{8,12},{12,8},{16,20},{20,16},{24,28},{28,24},{1,5},{5... | collective-permute-start | bytes 884744 | tf_op jit(solution)/shard_map/cond/branch_1_fun/ppermute | solution.py:644
  124.8 6.5 %collective-permute-start.2 = (bf16[48,768]{1,0:T(8,128)(2,1)S(1)}, bf16[48,768]{1,0:T(8,128)(2,1)S(1)}, u32[]{:S(2)}, u32[]{:S(2)}) collective-permute-start(bf16[48,768]{1,0:T(8,128)(2,1)S(1)} %get-tuple-element.102), channel_id=1, source_target_pairs={{0,8},{4,12},{8,0},{12,4},{16,24},{20,28},{24,16},{28,20},{1,9},{5... | collective-permute-start | bytes 221192 | tf_op jit(solution)/shard_map/cond/branch_1_fun/ppermute | solution.py:644
  126.9 7.2 %collective-permute-start.3 = (bf16[48,768]{1,0:T(8,128)(2,1)S(1)}, bf16[48,768]{1,0:T(8,128)(2,1)S(1)}, u32[]{:S(2)}, u32[]{:S(2)}) collective-permute-start(bf16[48,768]{1,0:T(8,128)(2,1)S(1)} %get-tuple-element.104), channel_id=1, source_target_pairs={{0,16},{4,20},{8,24},{12,28},{16,0},{20,4},{24,8},{28,12},{1,17},{... | collective-permute-start | bytes 221192 | tf_op jit(solution)/shard_map/cond/branch_1_fun/ppermute | solution.py:644
  129.3 6.3 %collective-permute-start.4 = (bf16[48,768]{1,0:T(8,128)(2,1)S(1)}, bf16[48,768]{1,0:T(8,128)(2,1)S(1)}, u32[]{:S(2)}, u32[]{:S(2)}) collective-permute-start(bf16[48,768]{1,0:T(8,128)(2,1)S(1)} %get-tuple-element.103), channel_id=1, source_target_pairs={{0,24},{4,28},{8,16},{12,20},{16,8},{20,12},{24,0},{28,4},{1,25},{... | collective-permute-start | bytes 221192 | tf_op jit(solution)/shard_map/cond/branch_1_fun/ppermute | solution.py:644
  136.6 13.4 %collective-permute-start.15 = (bf16[56,768]{1,0:T(8,128)(2,1)S(1)}, bf16[56,768]{1,0:T(8,128)(2,1)S(1)}, u32[]{:S(2)}, u32[]{:S(2)}) collective-permute-start(bf16[56,768]{1,0:T(8,128)(2,1)S(1)} %get-tuple-element.114), channel_id=1, source_target_pairs={{0,8},{4,12},{8,0},{12,4},{16,24},{20,28},{24,16},{28,20},{1,9},{5... | collective-permute-start | bytes 258056 | tf_op jit(solution)/shard_map/ppermute | solution.py:644
  137.5 12.6 %collective-permute-start.17 = (bf16[56,768]{1,0:T(8,128)(2,1)S(1)}, bf16[56,768]{1,0:T(8,128)(2,1)S(1)}, u32[]{:S(2)}, u32[]{:S(2)}) collective-permute-start(bf16[56,768]{1,0:T(8,128)(2,1)S(1)} %get-tuple-element.113), channel_id=1, source_target_pairs={{0,16},{4,20},{8,24},{12,28},{16,0},{20,4},{24,8},{28,12},{1,17},{... | collective-permute-start | bytes 258056 | tf_op jit(solution)/shard_map/ppermute | solution.py:644
  139.1 11.0 %collective-permute-start.18 = (bf16[56,768]{1,0:T(8,128)(2,1)S(1)}, bf16[56,768]{1,0:T(8,128)(2,1)S(1)}, u32[]{:S(2)}, u32[]{:S(2)}) collective-permute-start(bf16[56,768]{1,0:T(8,128)(2,1)S(1)} %get-tuple-element.112), channel_id=1, source_target_pairs={{0,24},{4,28},{8,16},{12,20},{16,8},{20,12},{24,0},{28,4},{1,25},{... | collective-permute-start | bytes 258056 | tf_op jit(solution)/shard_map/ppermute | solution.py:644
  150.8 3.9 %collective-permute-start.19 = (f32[6144]{0:T(1024)S(1)}, f32[6144]{0:T(1024)S(1)}, u32[]{:S(2)}, u32[]{:S(2)}) collective-permute-start(f32[6144]{0:T(1024)S(1)} %reshape.54), channel_id=1, source_target_pairs={{0,2},{2,0},{1,3},{3,1},{4,6},{6,4},{5,7},{7,5},{8,10},{10,8},{9,1... | collective-permute-start | bytes 73736 | tf_op jit(solution)/shard_map/ppermute | solution.py:644
  (14 other events, 34.5 us)

commit v3 on v2

--- a/solution.py
+++ b/solution.py
@@ -13,6 +13,12 @@
 LOG2E = math.log2(math.e)
 LANES = 128
 VMEM = pltpu.VMEM
+
+
+def pinned(value):
+    return pltpu.with_memory_space_constraint(value, pltpu.HBM)
+
+
 SCALE = 1.0
 ROOM = dict(forward=40, backward=24, dense=32, outputs=24, features=24, weights=24, token_rows=24)
 
@@ -89,14 +95,31 @@
 
 
 def forward_kernel(
-    flag_ref, tok_ref, gain_ref, w_ref, qk_ref, normed_ref, q_ref, k_ref, v_ref, att_ref, inv_ref
+    flag_ref,
+    tok_hbm,
+    gain_ref,
+    w_hbm,
+    qk_ref,
+    normed_ref,
+    q_hbm,
+    k_hbm,
+    v_hbm,
+    att_ref,
+    inv_ref,
+    tok_ref,
+    w_ref,
+    q_ref,
+    k_ref,
+    v_ref,
+    in_sems,
+    out_sems,
 ):
     rows = tok_ref.shape[0]
     heads, padded, _ = q_ref.shape
     tile = 2 * PATCHES
     size = qk_ref.shape[1]
     columns = w_ref.shape[1]
-    gain = wide(gain_ref[...])
+    gain = wide(gain_ref[...]).reshape(1, -1)
     q_gain = wide(qk_ref[0:1, :]) * (size**-0.5 * LOG2E)
     k_gain = wide(qk_ref[1:2, :])
     ones = jnp.ones_like(k_gain)
@@ -107,9 +130,22 @@
     mean_of = low(jnp.where(group_a == group_b, 1.0 / size, 0.0))
     stride = rows // (3 * LANES) and 3 * LANES
     strip = rows - (rows // stride - 1) * stride
+    strips = rows // stride
+    edges = [0] + [stride * step + 32 for step in range(1, strips)] + [rows]
+    token_copies = []
+    for step in range(strips):
+        part = pl.ds(edges[step], edges[step + 1] - edges[step])
+        token_copies.append(pltpu.make_async_copy(tok_hbm.at[part], tok_ref.at[part], in_sems.at[step]))
+    w_copy = pltpu.make_async_copy(w_hbm, w_ref, in_sems.at[strips])
+    token_copies[0].start()
+    w_copy.start()
+    for copy in token_copies[1:]:
+        copy.start()
     lane = lane_of((strip, LANES))
 
     def project(step, _):
+        for place, copy in enumerate(token_copies):
+            pl.when(step == place)(copy.wait)
         here = pl.ds(pl.multiple_of(step * stride, LANES), strip)
         x = wide(tok_ref[here, :])
         x = x - jnp.mean(x, axis=1, keepdims=True)
@@ -150,10 +186,19 @@
         inv_ref[here, :] = lax.rsqrt(compact + EPSILON)
         return 0
 
-    lax.fori_loop(0, rows // stride, project, 0)
+    w_copy.wait()
+    lax.fori_loop(0, strips, project, 0)
     lane = lane_of((tile, LANES))
     for ref in (q_ref, k_ref, v_ref):
         ref[:, rows:, :] = jnp.zeros((heads, padded - rows, LANES), jnp.bfloat16)
+    key_copy = pltpu.make_async_copy(k_ref, k_hbm, out_sems.at[0])
+    value_copy = pltpu.make_async_copy(v_ref, v_hbm, out_sems.at[1])
+    key_copy.start()
+    value_copy.start()
+
+    def query_copy(pair):
+        part = pl.ds(2 * pair, 2)
+        return pltpu.make_async_copy(q_ref.at[part], q_hbm.at[part], out_sems.at[2 + pair])
 
     def attend(pair, _, big):
         for start in range(0, rows, tile):
@@ -183,6 +228,7 @@
             att_ref[here, pl.ds(pl.multiple_of(pair * LANES, LANES), LANES)] = low(
                 jnp.where(lane < 64, found[0], other_half(found[1]))
             )
+        query_copy(pair).start()
         return 0
 
     @pl.when(flag_ref[0] > 0)
@@ -192,6 +238,11 @@
     @pl.when(flag_ref[0] <= 0)
     def _():
         lax.fori_loop(0, heads // 2, functools.partial(attend, big=False), 0)
+
+    key_copy.wait()
+    value_copy.wait()
+    for pair in range(heads // 2):
+        query_copy(pair).wait()
 
 
 def forward(big_images, tokens, norm_gain, w_qkv, qk_gains):
@@ -200,7 +251,9 @@
     heads = w_qkv.shape[1] // (3 * size)
     padded = -(-rows // 256) * 256
     whole = pl.BlockSpec(memory_space=VMEM)
-    head_rows = jax.ShapeDtypeStruct((heads, padded, LANES), jnp.bfloat16)
+    hbm = pl.BlockSpec(memory_space=pltpu.HBM)
+    held = VMEM((heads, padded, LANES), jnp.bfloat16)
+    head_rows = pltpu.HBM((heads, padded, LANES), jnp.bfloat16)
     return pl.pallas_call(
         forward_kernel,
         name="forward",
@@ -212,11 +265,20 @@
             jax.ShapeDtypeStruct((rows, heads * size), jnp.bfloat16),
             jax.ShapeDtypeStruct((rows, LANES), jnp.float32),
         ],
-        in_specs=[pl.BlockSpec(memory_space=pltpu.SMEM)] + [whole] * 4,
-        out_specs=[whole] * 6,
+        in_specs=[pl.BlockSpec(memory_space=pltpu.SMEM), hbm, whole, hbm, whole],
+        out_specs=[whole, hbm, hbm, hbm, whole, whole],
+        scratch_shapes=[
+            VMEM((rows, width), jnp.bfloat16),
+            VMEM(w_qkv.shape, jnp.bfloat16),
+            held,
+            held,
+            held,
+            pltpu.SemaphoreType.DMA((rows // (3 * LANES) + 1,)),
+            pltpu.SemaphoreType.DMA((2 + heads // 2,)),
+        ],
         compiler_params=pltpu.CompilerParams(vmem_limit_bytes=ROOM["forward"] * 2**20),
         cost_estimate=cost(24),
-    )(big_images, tokens, norm_gain.reshape(1, -1), w_qkv, qk_gains)
+    )(big_images, pinned(tokens), norm_gain, pinned(w_qkv), qk_gains)
 
 
 def backward_kernel(
@@ -340,7 +402,7 @@
         ],
         compiler_params=pltpu.CompilerParams(vmem_limit_bytes=ROOM["backward"] * 2**20),
         cost_estimate=cost(36),
-    )(big_images, q_rows, k_rows, v_rows, do_rows, inverses, qk_gains)
+    )(big_images, pinned(q_rows), pinned(k_rows), pinned(v_rows), do_rows, inverses, qk_gains)
 
 
 FINE = 2 * PATCHES
@@ -599,7 +661,7 @@
 def tokens_kernel(sent_ref, came_ref, tok_ref, gain_ref, mine_ref, other_ref, *refs):
     out_ref = refs[-1]
     half = mine_ref.shape[1]
-    grad = (wide(sent_ref[...]) + wide(came_ref[...])) * wide(gain_ref[...])
+    grad = (wide(sent_ref[...]) + wide(came_ref[...])) * wide(gain_ref[...]).reshape(1, -1)
     x = wide(tok_ref[...])
     x = x - jnp.mean(x, axis=1, keepdims=True)
     inverse = lax.rsqrt(jnp.mean(x * x, axis=1, keepdims=True) + EPSILON)
@@ -627,7 +689,7 @@
             near(width),
             near(width),
             far(width),
-            pl.BlockSpec((1, width), lambda step: (0, 0)),
+            pl.BlockSpec((width,), lambda step: (0,)),
             far(width // 2),
             far(width // 2),
         ]
@@ -636,7 +698,7 @@
         input_output_aliases={6: 0} if more else {},
         compiler_params=pltpu.CompilerParams(vmem_limit_bytes=ROOM["token_rows"] * 2**20),
         cost_estimate=cost(0.3 * count),
-    )(sent, came, tokens, norm_gain.reshape(1, -1), mine, other, *more)
+    )(sent, came, tokens, norm_gain, mine, other, *more)
 
 
 def swap(value, axis, bit):
@@ -692,13 +754,11 @@
     return low(shaped[0]), swap(low(shaped[1]), "dp", 1)
 
 
-def sum_rest(kept, came):
+def rest_terms(kept, came):
     count = lax.axis_size("dp")
     groups = [list(range(odd, count, 2)) for odd in (0, 1)]
     total = low(wide(kept) + wide(came))
-    total = lax.all_to_all(total, "dp", 0, 0, axis_index_groups=groups, tiled=True)
-    half = total.shape[2] // 2
-    return tuple(jnp.sum(wide(part), axis=0) for part in (total[:, :, :half], total[:, :, half:]))
+    return lax.all_to_all(total, "dp", 0, 0, axis_index_groups=groups, tiled=True)
 
 
 def far_terms(total):
@@ -748,33 +808,38 @@
     columns = attended.shape[1]
 
     def weight_sums(normed_t, dy_t, grad_joined, attended, gain_part, qk_part, kept, out_came):
-        first_kept, first_came = halve(row_blocks((normed_t, grad_joined, 2 * columns, 0)))
+        first_blocks = row_blocks((normed_t, grad_joined, 2 * columns, 0))
         blocks = row_blocks((normed_t, grad_joined, columns, 2), (dy_t, attended, columns, 0))
         small = jnp.concatenate([gain_part[0], qk_part[0, :size], qk_part[0, LANES : LANES + size]])
         small = low(sum_everywhere(small, ("hid",)))
-        small, blocks = lax.optimization_barrier((small, blocks))
+        small, first_blocks = lax.optimization_barrier((small, first_blocks))
+        first_kept, first_came = halve(first_blocks)
         second_kept, second_came = halve(blocks)
         small = low(wide(small) + wide(swap(small, "dp", 1)))
-        small = jnp.pad(small, (0, 8 * 2 * columns - small.shape[0])).reshape(1, 8, -1)
-        first = added(far_terms(low(wide(first_kept) + wide(first_came))))
+        small = jnp.pad(small, (0, 8 * 4 * columns - small.shape[0])).reshape(1, 8, -1)
+        first = low(wide(first_kept) + wide(first_came))
         second = low(wide(second_kept) + wide(second_came))
-        small = jnp.broadcast_to(small, second.shape[:1] + small.shape[1:])
-        return first, jnp.concatenate([second, small], axis=1), low(kept + wide(out_came))
+        small = jnp.broadcast_to(small, first.shape[:1] + small.shape[1:])
+        sums = jnp.concatenate([jnp.concatenate([first, second], axis=2), small], axis=1)
+        return sums, low(kept + wide(out_came))
 
     def no_sums(*operands):
         return jax.tree.map(lambda kind: jnp.zeros(kind.shape, kind.dtype), kinds)
 
     operands = (normed_t, dy_t, grad_joined, attended, gain_part, qk_part, kept, out_came)
     kinds = jax.eval_shape(weight_sums, *operands)
-    first, second, output = lax.cond(big_images[0] >= 0, weight_sums, no_sums, *operands)
-    w_in_grad, w_back_grad = sum_rest(mlp_kept, mlp_came)
-    terms = far_terms(second)
+    sums, output = lax.cond(big_images[0] >= 0, weight_sums, no_sums, *operands)
+    mlp_terms = rest_terms(mlp_kept, mlp_came)
+    hidden = mlp_terms.shape[2] // 2
+    w_in_grad = jnp.sum(wide(mlp_terms[:, :, :hidden]), axis=0)
+    w_back_grad = jnp.sum(wide(mlp_terms[:, :, hidden:]), axis=0)
+    terms = far_terms(sums)
     token_grad = token_rows(0, mine, came, tokens, norm_gain, cotangent, other, None)
     terms[1], token_grad = lax.optimization_barrier((terms[1], token_grad))
-    rows = first.shape[0]
-    w_qkv_grad = jnp.concatenate([first, added([term[:rows, :columns] for term in terms])], axis=1)
-    w_out_t_grad = added([term[:rows, columns:] for term in terms])
-    small = added([term[rows:] for term in terms]).reshape(-1)
+    rows = sums.shape[1] - 8
+    w_qkv_grad = added([term[:rows, : 3 * columns] for term in terms])
+    w_out_t_grad = added([term[:rows, 3 * columns :] for term in terms])
+    small = added([term[rows : rows + 1] for term in terms]).reshape(-1)
     small = sum_everywhere(small, ("hg",))
     own = lax.axis_index("dp") * lax.axis_size("hid") + lax.axis_index("hid")
     gain_rows = width // (groups * lax.axis_size("hid"))

time: 154 us -> 153 us (level); the launches traced: 156 us -> 151 us
  Pallas kernels: 93.4 us -> 76.3 us
  waiting for transfers between devices: 11.9 us -> 24.3 us
  starting transfers between devices: 24.5 us -> 28 us
  local copies, waits for them, and re-layouts: 11.2 us -> 9.09 us
    ppermute x20 -> x17, waiting for transfers between devices: 11.9 us -> 24.3 us  [swap(): lax.ppermute(value, axis, [(place, place ^ bit) for place in range(size)])]
    pallas_call x1, Pallas kernels: 29.4 us -> 17.2 us  [backward(): pl.pallas_call(backward_kernel, name='backward', grid=(heads // 2,), out_...]
    pallas_call x1, Pallas kernels: 19.9 us -> 16.4 us  [forward(): pl.pallas_call(forward_kernel, name='forward', out_shape=[jax.ShapeDtypeS...]
    ppermute x20 -> x17, starting transfers between devices: 17.9 us -> 21.2 us  [swap(): lax.ppermute(value, axis, [(place, place ^ bit) for place in range(size)])]
    add x3, other arithmetic: 1.43 us -> 4.01 us  [added(): first + second]
    unnamed x32 -> x36, local copies, waits for them, and re-layouts: 6.44 us -> 4.18 us
    pallas_call x2, Pallas kernels: 7.84 us -> 6.16 us  [weights(): pl.pallas_call(weights_kernel, name='weights', grid=(1,), out_shape=[jax....]
  transfers between devices with their start and end apart: 21 -> 18, of which waited for: 5 -> 7; matrix products, arithmetic and copies ran while one was open for 9% -> 8% of each run, Pallas kernels for 44% -> 34%
where the time goes in v3:
time: 153 us; the launch traced here: 151 us
  Pallas kernels  76.3 us (50%)
  starting transfers between devices  28 us (18%)
  waiting for transfers between devices  24.3 us (16%)
  other arithmetic  12.2 us (8%)
  local copies, waits for them, and re-layouts  9.09 us (6%)
    ppermute x17, waiting for transfers between devices, swap(): lax.ppermute(value, axis, [(place, place ^ bit) for place in range(size)])  24.3 us
    pallas_call x1, Pallas kernels, dense(): pl.pallas_call(functools.partial(dense_kernel, count, tiles), name='dense...  21.7 us
    ppermute x17, starting transfers between devices, swap(): lax.ppermute(value, axis, [(place, place ^ bit) for place in range(size)])  21.2 us
    pallas_call x1, Pallas kernels, backward(): pl.pallas_call(backward_kernel, name='backward', grid=(heads // 2,), out_...  17.2 us
    pallas_call x1, Pallas kernels, forward(): pl.pallas_call(forward_kernel, name='forward', out_shape=[jax.ShapeDtypeS...  16.4 us
    all_to_all x1, starting transfers between devices, rest_terms(): lax.all_to_all(total, 'dp', 0, 0, axis_index_groups=groups, tiled=True)  6.77 us
    pallas_call x2, Pallas kernels, weights(): pl.pallas_call(weights_kernel, name='weights', grid=(1,), out_shape=[jax....  6.16 us
    pallas_call x1, Pallas kernels, outputs(): pl.pallas_call(outputs_kernel, name='outputs', grid=(rows // tile,), out_...  5.85 us
  transfers between devices with their start and end apart: 18, of which 7 were waited for; matrix products, arithmetic and copies ran while one was open for 8% of the time, Pallas kernels for 34%

profile of v3, /device:TPU:0, one launch (start us, length us, event | category | flops | bytes accessed | tf_op | source)
XLA Modules:
  0.0 151.4 jit_solution(301167034975069552)
XLA Ops:
  0.6 3.0 %collective-permute-start.6 = (bf16[1176,384]{1,0:T(8,128)(2,1)}, bf16[1176,384]{1,0:T(8,128)(2,1)S(1)}, u32[]{:S(2)}, u32[]{:S(2)}) collective-permute-start(bf16[1176,384]{1,0:T(8,128)(2,1)} %mine_ref.5), channel_id=1, source_target_pairs={{0,2},{2,0},{1,3},{3,1},{4,6},{6,4},{5,7},{7,5},{8,10},{10,8},{9,1... | collective-permute-start | bytes 2709512 | tf_op jit(solution)/shard_map/ppermute | solution.py:706
  6.1 16.4 %forward.1 = (bf16[1176,768]{1,0:T(8,128)(2,1)S(1)}, bf16[6,1280,128]{2,1,0:T(8,128)(2,1)}, bf16[6,1280,128]{2,1,0:T(8,128)(2,1)}, bf16[6,1280,128]{2,1,0:T(8,12...) custom-call(s32[1]{0:T(128)S(6)} %copy.21.flag_ref, bf16[1176,768]{1,0:T(8,128)(2,1)} %tok_ref.5, ...), custom_call_target="tpu_custom_call" | custom-call | flops 24000000000 | bytes 1048576 | tf_op jit(solution)/shard_map/forward/pallas_call | solution.py:257
  22.6 1.3 collective-permute-done.6.other_ref
  24.0 21.7 %dense.1 = (f32[1176,768]{1,0:T(8,128)S(1)}, bf16[1176,768]{1,0:T(8,128)(2,1)S(1)}, bf16[768,1280]{1,0:T(8,128)(2,1)}, bf16[768,1280]{1,0:T(8,128)(2,1)}, bf16[2...) custom-call(bf16[1176,768]{1,0:T(8,128)(2,1)S(1)} %get-tuple-element.71.normed_ref, ...), custom_call_target="tpu_custom_call" | custom-call | flops 24000000000 | bytes 1048576 | tf_op jit(solution)/shard_map/dense/pallas_call | solution.py:487
  45.7 5.9 %outputs.1 = (f32[1176,384]{1,0:T(8,128)}, bf16[1176,384]{1,0:T(8,128)(2,1)S(1)}, bf16[6,1280,128]{2,1,0:T(8,128)(2,1)S(1)}) custom-call(f32[1176,768]{1,0:T(8,128)S(1)} %get-tuple-element.72.part_ref, bf16[1176,768]{1,0:T(8,128)(2,1)S(1)} %copy-done, bf16[1176,384]{1,0:T(8,128)(2,1)S(1)} %get-tuple-element.73.att_ref, bf16[1176,384]{1,0:T(8,128)(2,1)S(1)} %copy-done.4, ...), custom_call_target="tpu_custom_call" | custom-call | flops 6000000000 | bytes 1048576 | tf_op jit(solution)/shard_map/outputs/pallas_call | solution.py:557
  51.6 1.7 %collective-permute-start.10 = (bf16[1176,384]{1,0:T(8,128)(2,1)S(1)}, bf16[1176,384]{1,0:T(8,128)(2,1)S(1)}, u32[]{:S(2)}, u32[]{:S(2)}) collective-permute-start(bf16[1176,384]{1,0:T(8,128)(2,1)S(1)} %get-tuple-element.80), channel_id=1, source_target_pairs={{0,2},{2,0},{1,3},{3,1},{4,6},{6,4},{5,7},{7,5},{8,10},{10,8},{9,1... | collective-permute-start | bytes 2709512 | tf_op jit(solution)/shard_map/ppermute | solution.py:706
  54.2 1.6 %collective-permute-start.11 = (bf16[4,96,1536]{2,1,0:T(8,128)(2,1)S(1)}, bf16[4,96,1536]{2,1,0:T(8,128)(2,1)S(1)}, u32[]{:S(2)}, u32[]{:S(2)}) collective-permute-start(bf16[4,96,1536]{2,1,0:T(8,128)(2,1)S(1)} %get-tuple-element.102), channel_id=1, source_target_pairs={{0,4},{4,0},{8,12},{12,8},{16,20},{20,16},{24,28},{28,24},{1,5},{5... | collective-permute-start | bytes 3538952 | tf_op jit(solution)/shard_map/ppermute | solution.py:706
  55.8 17.2 %backward.1 = (bf16[1176,1152]{1,0:T(8,128)(2,1)S(1)}, f32[8,256]{1,0:T(8,128)S(1)}) custom-call(s32[1]{0:T(128)S(6)} %copy.21.flag_ref, bf16[6,1280,128]{2,1,0:T(8,128)(2,1)} %get-tuple-element.68.q_ref, bf16[6,1280,128]{2,1,0:T(8,128)(2,1)} %get-tuple-element.69.k_ref, bf16[6,1280,128]{2,1,0:T(8,128)(2,1)} %get-tuple-element.70.v_ref, ...), custom_call_target="tpu_custom_call" | custom-call | flops 35999997952 | bytes 1048576 | tf_op jit(solution)/shard_map/backward/pallas_call | solution.py:382
  74.0 8.3 %collective-permute-done.11 = bf16[4,96,1536]{2,1,0:T(8,128)(2,1)S(1)} collective-permute-done((bf16[4,96,1536]{2,1,0:T(8,128)(2,1)S(1)}, bf16[4,96,1536]{2,1,0:T(8,128)(2,1)S(1)}, u32[]{:S(2)}, u32[]{:S(2)}) %collective-permute-start.11) | collective-permute-done | bytes 1179680 | tf_op jit(solution)/shard_map/ppermute | solution.py:706
  82.3 3.8 %features.1 = (bf16[1176,768]{1,0:T(8,128)(2,1)S(1)}, f32[8,768]{1,0:T(8,128)S(1)}) custom-call(bf16[1176,1152]{1,0:T(8,128)(2,1)S(1)} %get-tuple-element.81.joined_ref, bf16[768,1152]{1,0:T(8,128)(2,1)S(1)} %copy-done.3, bf16[1176,768]{1,0:T(8,128)(2,1)S(1)} %get-tuple-element.82.mlp_ref, bf16[1176,768]{1,0:T(8,128)(2,1)S(1)} %copy-done), custom_call_target="tpu_custom_call" | custom-call | flops 900000000 | bytes 1048576 | tf_op jit(solution)/shard_map/features/pallas_call | solution.py:596
  86.1 1.3 copy-done.1
  87.4 1.4 add_convert_fusion.5
  88.8 6.8 %all-to-all-start = ((bf16[4,96,1536]{2,1,0:T(8,128)(2,1)}), bf16[4,96,1536]{2,1,0:T(8,128)(2,1)}, u32[]{:S(2)}, u32[]{:S(2)}) async-start(bf16[4,96,1536]{2,1,0:T(8,128)(2,1)} %add_convert_fusion.5), calls=%async_computation | async-start | bytes 2359296 | tf_op jit(solution)/shard_map/all_to_all | solution.py:761
  95.6 1.5 collective-permute-start.13
  97.1 29.0 %conditional.1 = (bf16[4,56,1536]{2,1,0:T(8,128)(2,1)S(1)}, bf16[1176,384]{1,0:T(8,128)(2,1)}) conditional(s32[]{:T(128)} %bitcast.8, () %tuple.21, (f32[8,768]{1,0:T(8,128)S(1)}, f32[8,256]{1,0:T(8,128)S(1)}, bf16[768,1280]{1,0:T(8,128)(2,1)}, bf16[1176,1152]{1,0:T(8,128)(2,1)}, bf16[768,1280]{1,0:T(8,128)(2,1)}, ...), branch_computations={%region_0.0_spmd, %region_1.2_spmd} | conditional | flops 6006967296 | bytes 64277700 | solution.py:831
  97.2 2.9 %collective-permute-start = (f32[896]{0:T(1024)S(1)}, f32[896]{0:T(1024)S(1)}, u32[]{:S(2)}, u32[]{:S(2)}) collective-permute-start(f32[896]{0:T(1024)S(1)} %pad_maximum_fusion.1), channel_id=1, source_target_pairs={{0,1},{1,0},{2,3},{3,2},{4,5},{5,4},{6,7},{7,6},{8,9},{9,8},{10,11... | collective-permute-start | bytes 10760 | tf_op jit(solution)/shard_map/cond/branch_1_fun/ppermute | solution.py:706
  100.1 3.9 %weights.2 = (bf16[2,4,48,768]{3,2,1,0:T(8,128)(2,1)S(1)}, bf16[2,4,48,768]{3,2,1,0:T(8,128)(2,1)S(1)}) custom-call(bf16[768,1280]{1,0:T(8,128)(2,1)} %get-tuple-element.18.refs_0_, bf16[1176,1152]{1,0:T(8,128)(2,1)} %get-tuple-element.19.refs_1_), custom_call_target="tpu_custom_call" | custom-call | flops 3000000000 | bytes 1048576 | tf_op jit(solution)/shard_map/cond/branch_1_fun/weights/pallas_call | solution.py:649
  104.4 2.2 %weights.3 = (bf16[2,4,48,768]{3,2,1,0:T(8,128)(2,1)S(1)}, bf16[2,4,48,768]{3,2,1,0:T(8,128)(2,1)S(1)}) custom-call(bf16[768,1280]{1,0:T(8,128)(2,1)S(1)} %copy-done.21, bf16[1176,1152]{1,0:T(8,128)(2,1)S(1)} %copy-done.15, bf16[768,1280]{1,0:T(8,128)(2,1)S(1)} %copy-done.22, bf16[1176,384]{1,0:T(8,128)(2,1)S(1)} %copy-done.24), custom_call_target="tpu_custom_call" | custom-call | flops 3000000000 | bytes 1048576 | tf_op jit(solution)/shard_map/cond/branch_1_fun/weights/pallas_call | solution.py:649
  107.0 1.2 add_convert_fusion
  109.1 1.6 %collective-permute-start.2 = (bf16[4,48,768]{2,1,0:T(8,128)(2,1)}, bf16[4,48,768]{2,1,0:T(8,128)(2,1)}, u32[]{:S(2)}, u32[]{:S(2)}) collective-permute-start(bf16[4,48,768]{2,1,0:T(8,128)(2,1)} %slice_bitcast_fusion.2), channel_id=1, source_target_pairs={{0,4},{4,0},{8,12},{12,8},{16,20},{20,16},{24,28},{28,24},{1,5},{5... | collective-permute-start | bytes 884744 | tf_op jit(solution)/shard_map/cond/branch_1_fun/ppermute | solution.py:706
  112.8 1.6 %collective-permute-start.4 = (bf16[4,48,768]{2,1,0:T(8,128)(2,1)}, bf16[4,48,768]{2,1,0:T(8,128)(2,1)}, u32[]{:S(2)}, u32[]{:S(2)}) collective-permute-start(bf16[4,48,768]{2,1,0:T(8,128)(2,1)} %slice_bitcast_fusion), channel_id=1, source_target_pairs={{0,4},{4,0},{8,12},{12,8},{16,20},{20,16},{24,28},{28,24},{1,5},{5... | collective-permute-start | bytes 884744 | tf_op jit(solution)/shard_map/cond/branch_1_fun/ppermute | solution.py:706
  114.4 4.8 %collective-permute-done.5 = bf16[896]{0:T(1024)(128)(2,1)S(1)} collective-permute-done((bf16[896]{0:T(1024)(128)(2,1)S(1)}, bf16[896]{0:T(1024)(128)(2,1)S(1)}, u32[]{:S(2)}, u32[]{:S(2)}) %collective-permute-start.5) | collective-permute-done | bytes 1824 | tf_op jit(solution)/shard_map/cond/branch_1_fun/ppermute | solution.py:706
  120.4 4.5 %collective-permute-done.4 = bf16[4,48,768]{2,1,0:T(8,128)(2,1)} collective-permute-done((bf16[4,48,768]{2,1,0:T(8,128)(2,1)}, bf16[4,48,768]{2,1,0:T(8,128)(2,1)}, u32[]{:S(2)}, u32[]{:S(2)}) %collective-permute-start.4) | collective-permute-done | bytes 294944 | tf_op jit(solution)/shard_map/cond/branch_1_fun/ppermute | solution.py:706
  127.0 2.9 %collective-permute-start.12 = (bf16[56,1536]{1,0:T(8,128)(2,1)}, bf16[56,1536]{1,0:T(8,128)(2,1)}, u32[]{:S(2)}, u32[]{:S(2)}) collective-permute-start(bf16[56,1536]{1,0:T(8,128)(2,1)} %get-tuple-element.107), channel_id=1, source_target_pairs={{0,8},{4,12},{8,0},{12,4},{16,24},{20,28},{24,16},{28,20},{1,9},{5... | collective-permute-start | bytes 516104 | tf_op jit(solution)/shard_map/ppermute | solution.py:706
  129.9 1.3 collective-permute-start.14
  132.3 2.4 %convert_reduce_fusion = (f32[96,768]{1,0:T(8,128)}, f32[96,768]{1,0:T(8,128)}) fusion(bf16[4,96,1536]{2,1,0:T(8,128)(2,1)} %all-to-all-done), kind=kLoop, calls=%fused_computation.22 | loop fusion | flops 1032192 | bytes 1769472 | tf_op jit(solution)/shard_map/reduce_sum | solution.py:835
  134.7 1.2 collective-permute-done.13.came_ref
  135.9 1.5 copy-done.2
  137.4 5.1 %token_rows.1 = bf16[1176,768]{1,0:T(8,128)(2,1)} custom-call(bf16[1176,768]{1,0:T(8,128)(2,1)S(1)} %copy-done.2, bf16[1176,768]{1,0:T(8,128)(2,1)} %collective-permute-done.13.came_ref, bf16[1176,768]{1,0:T(8,128)(2,1)S(1)} %copy-done, bf16[768]{0:T(1024)(128)(2,1)S(1)} %copy-done.8, bf16[1176,384]{1,0:T(8,128)(2,1)S(1)} %copy-done.4, ...), custom_call_target="tpu_custom_call" | custom-call | flops 900000000 | bytes 1048576 | tf_op jit(solution)/shard_map/token_rows/pallas_call | solution.py:683
  142.5 3.1 %collective-permute-done.14 = bf16[56,1536]{1,0:T(8,128)(2,1)} collective-permute-done((bf16[56,1536]{1,0:T(8,128)(2,1)}, bf16[56,1536]{1,0:T(8,128)(2,1)}, u32[]{:S(2)}, u32[]{:S(2)}) %collective-permute-start.14) | collective-permute-done | bytes 172064 | tf_op jit(solution)/shard_map/ppermute | solution.py:706
  147.0 1.7 %add_add_fusion = f32[48,1152]{1,0:T(8,128)} fusion(bf16[56,1536]{1,0:T(8,128)(2,1)} %collective-permute-done.15, bf16[56,1536]{1,0:T(8,128)(2,1)} %collective-permute-done.14, bf16[56,1536]{1,0:T(8,128)(2,1)S(1)} %copy-done.20, bf16[56,1536]{1,0:T(8,128)(2,1)} %collective-permute-done.12), kind=kLoop, calls=%fused_computation.24 | loop fusion | flops 387072 | bytes 663552 | tf_op jit(solution)/shard_map/add | solution.py:776
  148.7 1.5 add_add_fusion.1
  (91 shorter events, 14.6 us)
Async XLA Ops:
  0.6 23.3 %collective-permute-start.6 = (bf16[1176,384]{1,0:T(8,128)(2,1)}, bf16[1176,384]{1,0:T(8,128)(2,1)S(1)}, u32[]{:S(2)}, u32[]{:S(2)}) collective-permute-start(bf16[1176,384]{1,0:T(8,128)(2,1)} %mine_ref.5), channel_id=1, source_target_pairs={{0,2},{2,0},{1,3},{3,1},{4,6},{6,4},{5,7},{7,5},{8,10},{10,8},{9,1... | collective-permute-start | bytes 2709512 | tf_op jit(solution)/shard_map/ppermute | solution.py:706
  3.6 20.3 %collective-permute-start.7 = (bf16[768,768]{1,0:T(8,128)(2,1)}, bf16[768,768]{1,0:T(8,128)(2,1)S(1)}, u32[]{:S(2)}, u32[]{:S(2)}) collective-permute-start(bf16[768,768]{1,0:T(8,128)(2,1)} %refs_0_.1), channel_id=1, source_target_pairs={{0,1},{1,0},{2,3},{3,2},{4,5},{5,4},{6,7},{7,6},{8,9},{9,8},{10,11... | collective-permute-start | bytes 3538952 | tf_op jit(solution)/shard_map/ppermute | solution.py:706
  3.6 20.3 %collective-permute-start.8 = (bf16[768,768]{1,0:T(8,128)(2,1)}, bf16[768,768]{1,0:T(8,128)(2,1)S(1)}, u32[]{:S(2)}, u32[]{:S(2)}) collective-permute-start(bf16[768,768]{1,0:T(8,128)(2,1)} %refs_2_.1), channel_id=1, source_target_pairs={{0,1},{1,0},{2,3},{3,2},{4,5},{5,4},{6,7},{7,6},{8,9},{9,8},{10,11... | collective-permute-start | bytes 3538952 | tf_op jit(solution)/shard_map/ppermute | solution.py:706
  6.1 17.8 %copy-start.4 = (bf16[1176,384]{1,0:T(8,128)(2,1)S(1)}, bf16[1176,384]{1,0:T(8,128)(2,1)}, u32[]{:S(2)}) copy-start(bf16[1176,384]{1,0:T(8,128)(2,1)} %mine_ref.5) | copy-start | bytes 2709508
  6.1 17.8 %copy-start.9 = (bf16[768,768]{1,0:T(8,128)(2,1)S(1)}, bf16[768,768]{1,0:T(8,128)(2,1)}, u32[]{:S(2)}) copy-start(bf16[768,768]{1,0:T(8,128)(2,1)} %refs_0_.1) | copy-start | bytes 3538948
  6.1 17.8 %copy-start.10 = (bf16[768,768]{1,0:T(8,128)(2,1)S(1)}, bf16[768,768]{1,0:T(8,128)(2,1)}, u32[]{:S(2)}) copy-start(bf16[768,768]{1,0:T(8,128)(2,1)} %refs_2_.1) | copy-start | bytes 3538948
  22.6 23.1 %copy-start.23 = (bf16[1176,384]{1,0:T(8,128)(2,1)}, bf16[1176,384]{1,0:T(8,128)(2,1)S(1)}, u32[]{:S(2)}) copy-start(bf16[1176,384]{1,0:T(8,128)(2,1)S(1)} %get-tuple-element.73.att_ref) | copy-start | bytes 2709508
  23.9 21.8 %copy-start.5 = (bf16[1176,384]{1,0:T(8,128)(2,1)}, bf16[1176,384]{1,0:T(8,128)(2,1)S(1)}, u32[]{:S(2)}) copy-start(bf16[1176,384]{1,0:T(8,128)(2,1)S(1)} %collective-permute-done.6.other_ref) | copy-start | bytes 2709508
  23.9 21.8 %copy-start = (bf16[1176,768]{1,0:T(8,128)(2,1)S(1)}, bf16[1176,768]{1,0:T(8,128)(2,1)}, u32[]{:S(2)}) copy-start(bf16[1176,768]{1,0:T(8,128)(2,1)} %tok_ref.5) | copy-start | bytes 5419012
  23.9 21.8 %copy-start.11 = (bf16[768,384]{1,0:T(8,128)(2,1)S(1)}, bf16[768,384]{1,0:T(8,128)(2,1)}, u32[]{:S(2)}) copy-start(bf16[768,384]{1,0:T(8,128)(2,1)} %w_out_ref.1) | copy-start | bytes 1769476
  45.7 7.6 %collective-permute-start.9 = (bf16[2,4,96,1536]{3,2,1,0:T(8,128)(2,1)S(1)}, bf16[2,4,96,1536]{3,2,1,0:T(8,128)(2,1)S(1)}, u32[]{:S(2)}, u32[]{:S(2)}) collective-permute-start(bf16[2,4,96,1536]{3,2,1,0:T(8,128)(2,1)S(1)} %get-tuple-element.76), channel_id=1, source_target_pairs={{0,1},{1,0},{2,3},{3,2},{4,5},{5,4},{6,7},{7,6},{8,9},{9,8},{10,11... | collective-permute-start | bytes 7077896 | tf_op jit(solution)/shard_map/ppermute | solution.py:706
  51.6 22.4 %collective-permute-start.10 = (bf16[1176,384]{1,0:T(8,128)(2,1)S(1)}, bf16[1176,384]{1,0:T(8,128)(2,1)S(1)}, u32[]{:S(2)}, u32[]{:S(2)}) collective-permute-start(bf16[1176,384]{1,0:T(8,128)(2,1)S(1)} %get-tuple-element.80), channel_id=1, source_target_pairs={{0,2},{2,0},{1,3},{3,1},{4,6},{6,4},{5,7},{7,5},{8,10},{10,8},{9,1... | collective-permute-start | bytes 2709512 | tf_op jit(solution)/shard_map/ppermute | solution.py:706
  54.2 28.2 %collective-permute-start.11 = (bf16[4,96,1536]{2,1,0:T(8,128)(2,1)S(1)}, bf16[4,96,1536]{2,1,0:T(8,128)(2,1)S(1)}, u32[]{:S(2)}, u32[]{:S(2)}) collective-permute-start(bf16[4,96,1536]{2,1,0:T(8,128)(2,1)S(1)} %get-tuple-element.102), channel_id=1, source_target_pairs={{0,4},{4,0},{8,12},{12,8},{16,20},{20,16},{24,28},{28,24},{1,5},{5... | collective-permute-start | bytes 3538952 | tf_op jit(solution)/shard_map/ppermute | solution.py:706
  55.8 26.6 %copy-start.3 = (bf16[768,1152]{1,0:T(8,128)(2,1)S(1)}, bf16[768,1152]{1,0:T(8,128)(2,1)}, u32[]{:S(2)}) copy-start(bf16[768,1152]{1,0:T(8,128)(2,1)} %w_ref.1) | copy-start | bytes 5308420
  73.0 13.1 %copy-start.14 = (bf16[1176,1152]{1,0:T(8,128)(2,1)}, bf16[1176,1152]{1,0:T(8,128)(2,1)S(1)}, u32[]{:S(2)}) copy-start(bf16[1176,1152]{1,0:T(8,128)(2,1)S(1)} %get-tuple-element.81.joined_ref) | copy-start | bytes 8128516
  74.0 12.1 %copy-start.18 = (bf16[1176,384]{1,0:T(8,128)(2,1)}, bf16[1176,384]{1,0:T(8,128)(2,1)S(1)}, u32[]{:S(2)}) copy-start(bf16[1176,384]{1,0:T(8,128)(2,1)S(1)} %collective-permute-done.10) | copy-start | bytes 2709508
  88.8 43.5 %all-to-all-start = ((bf16[4,96,1536]{2,1,0:T(8,128)(2,1)}), bf16[4,96,1536]{2,1,0:T(8,128)(2,1)}, u32[]{:S(2)}, u32[]{:S(2)}) async-start(bf16[4,96,1536]{2,1,0:T(8,128)(2,1)} %add_convert_fusion.5), calls=%async_computation | async-start | bytes 2359296 | tf_op jit(solution)/shard_map/all_to_all | solution.py:761
  95.6 40.3 %collective-permute-start.13 = (bf16[1176,768]{1,0:T(8,128)(2,1)}, bf16[1176,768]{1,0:T(8,128)(2,1)}, u32[]{:S(2)}, u32[]{:S(2)}) collective-permute-start(bf16[1176,768]{1,0:T(8,128)(2,1)} %copy-done.1), channel_id=1, source_target_pairs={{0,2},{2,0},{1,3},{3,1},{4,6},{6,4},{5,7},{7,5},{8,10},{10,8},{9,1... | collective-permute-start | bytes 5419016 | tf_op jit(solution)/shard_map/ppermute | solution.py:706
  97.2 11.0 %collective-permute-start = (f32[896]{0:T(1024)S(1)}, f32[896]{0:T(1024)S(1)}, u32[]{:S(2)}, u32[]{:S(2)}) collective-permute-start(f32[896]{0:T(1024)S(1)} %pad_maximum_fusion.1), channel_id=1, source_target_pairs={{0,1},{1,0},{2,3},{3,2},{4,5},{5,4},{6,7},{7,6},{8,9},{9,8},{10,11... | collective-permute-start | bytes 10760 | tf_op jit(solution)/shard_map/cond/branch_1_fun/ppermute | solution.py:706
  100.1 4.1 %copy-start.22 = (bf16[768,1280]{1,0:T(8,128)(2,1)S(1)}, bf16[768,1280]{1,0:T(8,128)(2,1)}, u32[]{:S(2)}) copy-start(bf16[768,1280]{1,0:T(8,128)(2,1)} %get-tuple-element.23.refs_2_) | copy-start | bytes 5898244 | tf_op jit(solution)/shard_map/cond
  100.1 4.3 %copy-start.24 = (bf16[1176,384]{1,0:T(8,128)(2,1)S(1)}, bf16[1176,384]{1,0:T(8,128)(2,1)}, u32[]{:S(2)}) copy-start(bf16[1176,384]{1,0:T(8,128)(2,1)} %get-tuple-element.24.refs_3_) | copy-start | bytes 2709508 | tf_op jit(solution)/shard_map/cond
  104.0 4.2 %collective-permute-start.1 = (bf16[2,4,48,768]{3,2,1,0:T(8,128)(2,1)S(1)}, bf16[2,4,48,768]{3,2,1,0:T(8,128)(2,1)S(1)}, u32[]{:S(2)}, u32[]{:S(2)}) collective-permute-start(bf16[2,4,48,768]{3,2,1,0:T(8,128)(2,1)S(1)} %get-tuple-element.21), channel_id=1, source_target_pairs={{0,1},{1,0},{2,3},{3,2},{4,5},{5,4},{6,7},{7,6},{8,9},{9,8},{10,11... | collective-permute-start | bytes 1769480 | tf_op jit(solution)/shard_map/cond/branch_1_fun/ppermute | solution.py:706
  106.6 4.5 %collective-permute-start.3 = (bf16[2,4,48,768]{3,2,1,0:T(8,128)(2,1)S(1)}, bf16[2,4,48,768]{3,2,1,0:T(8,128)(2,1)S(1)}, u32[]{:S(2)}, u32[]{:S(2)}) collective-permute-start(bf16[2,4,48,768]{3,2,1,0:T(8,128)(2,1)S(1)} %get-tuple-element.26), channel_id=1, source_target_pairs={{0,1},{1,0},{2,3},{3,2},{4,5},{5,4},{6,7},{7,6},{8,9},{9,8},{10,11... | collective-permute-start | bytes 1769480 | tf_op jit(solution)/shard_map/cond/branch_1_fun/ppermute | solution.py:706
  109.1 10.2 %collective-permute-start.2 = (bf16[4,48,768]{2,1,0:T(8,128)(2,1)}, bf16[4,48,768]{2,1,0:T(8,128)(2,1)}, u32[]{:S(2)}, u32[]{:S(2)}) collective-permute-start(bf16[4,48,768]{2,1,0:T(8,128)(2,1)} %slice_bitcast_fusion.2), channel_id=1, source_target_pairs={{0,4},{4,0},{8,12},{12,8},{16,20},{20,16},{24,28},{28,24},{1,5},{5... | collective-permute-start | bytes 884744 | tf_op jit(solution)/shard_map/cond/branch_1_fun/ppermute | solution.py:706
  110.7 8.6 %collective-permute-start.5 = (bf16[896]{0:T(1024)(128)(2,1)S(1)}, bf16[896]{0:T(1024)(128)(2,1)S(1)}, u32[]{:S(2)}, u32[]{:S(2)}) collective-permute-start(bf16[896]{0:T(1024)(128)(2,1)S(1)} %add_convert_fusion.3), channel_id=1, source_target_pairs={{0,4},{4,0},{8,12},{12,8},{16,20},{20,16},{24,28},{28,24},{1,5},{5... | collective-permute-start | bytes 5384 | tf_op jit(solution)/shard_map/cond/branch_1_fun/ppermute | solution.py:706
  112.8 12.1 %collective-permute-start.4 = (bf16[4,48,768]{2,1,0:T(8,128)(2,1)}, bf16[4,48,768]{2,1,0:T(8,128)(2,1)}, u32[]{:S(2)}, u32[]{:S(2)}) collective-permute-start(bf16[4,48,768]{2,1,0:T(8,128)(2,1)} %slice_bitcast_fusion), channel_id=1, source_target_pairs={{0,4},{4,0},{8,12},{12,8},{16,20},{20,16},{24,28},{28,24},{1,5},{5... | collective-permute-start | bytes 884744 | tf_op jit(solution)/shard_map/cond/branch_1_fun/ppermute | solution.py:706
  126.1 9.8 %copy-start.8 = (bf16[768]{0:T(1024)(128)(2,1)S(1)}, bf16[768]{0:T(1024)(128)(2,1)}, u32[]{:S(2)}) copy-start(bf16[768]{0:T(1024)(128)(2,1)} %gain_ref.3) | copy-start | bytes 4612
  127.0 15.5 %collective-permute-start.12 = (bf16[56,1536]{1,0:T(8,128)(2,1)}, bf16[56,1536]{1,0:T(8,128)(2,1)}, u32[]{:S(2)}, u32[]{:S(2)}) collective-permute-start(bf16[56,1536]{1,0:T(8,128)(2,1)} %get-tuple-element.107), channel_id=1, source_target_pairs={{0,8},{4,12},{8,0},{12,4},{16,24},{20,28},{24,16},{28,20},{1,9},{5... | collective-permute-start | bytes 516104 | tf_op jit(solution)/shard_map/ppermute | solution.py:706
  129.9 15.6 %collective-permute-start.14 = (bf16[56,1536]{1,0:T(8,128)(2,1)}, bf16[56,1536]{1,0:T(8,128)(2,1)}, u32[]{:S(2)}, u32[]{:S(2)}) collective-permute-start(bf16[56,1536]{1,0:T(8,128)(2,1)} %get-tuple-element.106), channel_id=1, source_target_pairs={{0,16},{4,20},{8,24},{12,28},{16,0},{20,4},{24,8},{28,12},{1,17},{... | collective-permute-start | bytes 516104 | tf_op jit(solution)/shard_map/ppermute | solution.py:706
  131.3 14.3 %collective-permute-start.15 = (bf16[56,1536]{1,0:T(8,128)(2,1)}, bf16[56,1536]{1,0:T(8,128)(2,1)}, u32[]{:S(2)}, u32[]{:S(2)}) collective-permute-start(bf16[56,1536]{1,0:T(8,128)(2,1)} %get-tuple-element.105), channel_id=1, source_target_pairs={{0,24},{4,28},{8,16},{12,20},{16,8},{20,12},{24,0},{28,4},{1,25},{... | collective-permute-start | bytes 516104 | tf_op jit(solution)/shard_map/ppermute | solution.py:706
  137.4 9.6 %copy-start.20 = (bf16[56,1536]{1,0:T(8,128)(2,1)S(1)}, bf16[56,1536]{1,0:T(8,128)(2,1)}, u32[]{:S(2)}) copy-start(bf16[56,1536]{1,0:T(8,128)(2,1)} %get-tuple-element.104) | copy-start | bytes 516100
  146.4 3.8 %collective-permute-start.16 = (f32[1536]{0:T(1024)S(1)}, f32[1536]{0:T(1024)S(1)}, u32[]{:S(2)}, u32[]{:S(2)}) collective-permute-start(f32[1536]{0:T(1024)S(1)} %fusion.6), channel_id=1, source_target_pairs={{0,2},{2,0},{1,3},{3,1},{4,6},{6,4},{5,7},{7,5},{8,10},{10,8},{9,1... | collective-permute-start | bytes 18440 | tf_op jit(solution)/shard_map/ppermute | solution.py:706
  (11 other events, 23.6 us)

commit v4 on v3

--- a/solution.py
+++ b/solution.py
@@ -97,9 +97,9 @@
 def forward_kernel(
     flag_ref,
     tok_hbm,
-    gain_ref,
+    gain_hbm,
     w_hbm,
-    qk_ref,
+    qk_hbm,
     normed_ref,
     q_hbm,
     k_hbm,
@@ -107,7 +107,9 @@
     att_ref,
     inv_ref,
     tok_ref,
+    gain_ref,
     w_ref,
+    qk_ref,
     q_ref,
     k_ref,
     v_ref,
@@ -118,13 +120,6 @@
     heads, padded, _ = q_ref.shape
     tile = 2 * PATCHES
     size = qk_ref.shape[1]
-    columns = w_ref.shape[1]
-    gain = wide(gain_ref[...]).reshape(1, -1)
-    q_gain = wide(qk_ref[0:1, :]) * (size**-0.5 * LOG2E)
-    k_gain = wide(qk_ref[1:2, :])
-    ones = jnp.ones_like(k_gain)
-    gains = jnp.concatenate([q_gain, k_gain, ones, q_gain, k_gain, ones], axis=1)
-    is_value = jnp.concatenate([0 * ones, 0 * ones, ones, 0 * ones, 0 * ones, ones], axis=1)
     group_a = row_of((256, 256)) // size
     group_b = lane_of((256, 256)) // size
     mean_of = low(jnp.where(group_a == group_b, 1.0 / size, 0.0))
@@ -137,11 +132,26 @@
         part = pl.ds(edges[step], edges[step + 1] - edges[step])
         token_copies.append(pltpu.make_async_copy(tok_hbm.at[part], tok_ref.at[part], in_sems.at[step]))
     w_copy = pltpu.make_async_copy(w_hbm, w_ref, in_sems.at[strips])
+    small_copies = [
+        pltpu.make_async_copy(source, target, in_sems.at[strips + 1 + place])
+        for place, (source, target) in enumerate(((gain_hbm, gain_ref), (qk_hbm, qk_ref)))
+    ]
+    for copy in small_copies:
+        copy.start()
     token_copies[0].start()
     w_copy.start()
     for copy in token_copies[1:]:
         copy.start()
     lane = lane_of((strip, LANES))
+
+    for copy in small_copies:
+        copy.wait()
+    gain = wide(gain_ref[...]).reshape(1, -1)
+    q_gain = wide(qk_ref[0:1, :]) * (size**-0.5 * LOG2E)
+    k_gain = wide(qk_ref[1:2, :])
+    ones = jnp.ones_like(k_gain)
+    gains = jnp.concatenate([q_gain, k_gain, ones, q_gain, k_gain, ones], axis=1)
+    is_value = jnp.concatenate([0 * ones, 0 * ones, ones, 0 * ones, 0 * ones, ones], axis=1)
 
     def project(step, _):
         for place, copy in enumerate(token_copies):
@@ -152,9 +162,9 @@
         x = x * lax.rsqrt(jnp.mean(x * x, axis=1, keepdims=True) + EPSILON)
         normed = low(x * gain)
         normed_ref[here, :] = normed
-        compact = jnp.zeros((strip, LANES), jnp.float32)
+        every = times(normed, w_ref[...])
         for pair in range(heads // 2):
-            joined = times(normed, w_ref[:, 384 * pair : 384 * pair + 384])
+            joined = every[:, 384 * pair : 384 * pair + 384]
             parts = []
             for at in (0, 256):
                 wid = min(256, 384 - at)
@@ -163,14 +173,9 @@
                 centred = block - times(low(block), means)
                 squares = low(centred * centred)
                 variance = times(squares, means)
-                place = 6 * pair + at // size
-                pick = low(
-                    jnp.where(
-                        row_of((wid, LANES)) // size + place == lane_of((wid, LANES)), 1.0 / size, 0.0
-                    )
-                )
-                compact = compact + times(squares, pick)
-                hat = centred * lax.rsqrt(variance + EPSILON)
+                inverse = lax.rsqrt(variance + EPSILON)
+                inv_ref[here, 384 * pair + at : 384 * pair + at + wid] = low(inverse)
+                hat = centred * inverse
                 parts.append(
                     jnp.where(is_value[:, at : at + wid] > 0, block, hat * gains[:, at : at + wid])
                 )
@@ -183,7 +188,6 @@
             q_ref[2 * pair + 1, here, :] = low(jnp.where(first, other_half(b1), 0.0))
             k_ref[2 * pair + 1, here, :] = low(jnp.where(first, b2, unit))
             v_ref[2 * pair + 1, here, :] = low(jnp.where(first, other_half(b2), unit))
-        inv_ref[here, :] = lax.rsqrt(compact + EPSILON)
         return 0
 
     w_copy.wait()
@@ -263,22 +267,24 @@
             head_rows,
             head_rows,
             jax.ShapeDtypeStruct((rows, heads * size), jnp.bfloat16),
-            jax.ShapeDtypeStruct((rows, LANES), jnp.float32),
-        ],
-        in_specs=[pl.BlockSpec(memory_space=pltpu.SMEM), hbm, whole, hbm, whole],
+            pltpu.HBM((rows, w_qkv.shape[1]), jnp.bfloat16),
+        ],
+        in_specs=[pl.BlockSpec(memory_space=pltpu.SMEM)] + [hbm] * 4,
         out_specs=[whole, hbm, hbm, hbm, whole, whole],
         scratch_shapes=[
             VMEM((rows, width), jnp.bfloat16),
+            VMEM(norm_gain.shape, jnp.bfloat16),
             VMEM(w_qkv.shape, jnp.bfloat16),
+            VMEM(qk_gains.shape, jnp.bfloat16),
             held,
             held,
             held,
-            pltpu.SemaphoreType.DMA((rows // (3 * LANES) + 1,)),
+            pltpu.SemaphoreType.DMA((rows // (3 * LANES) + 3,)),
             pltpu.SemaphoreType.DMA((2 + heads // 2,)),
         ],
         compiler_params=pltpu.CompilerParams(vmem_limit_bytes=ROOM["forward"] * 2**20),
         cost_estimate=cost(24),
-    )(big_images, pinned(tokens), norm_gain, pinned(w_qkv), qk_gains)
+    )(big_images, pinned(tokens), pinned(norm_gain), pinned(w_qkv), pinned(qk_gains))
 
 
 def backward_kernel(
@@ -354,13 +360,11 @@
         turned_ref[side] = dq_ref[side].T
     for start in range(0, rows, tile):
         here = slice(start, start + tile)
-        inverse_first, inverse_second = two_terms(inv_ref[here, :])
+        inv0, inv1, inv2 = (wide(inv_ref[here, at : at + LANES]) for at in range(0, 3 * LANES, LANES))
+        inverses = (inv0, other_half(inv0)), (other_half(inv1), inv2)
         blocks = []
         for side in range(2):
-            shape = (LANES, 2 * LANES)
-            source = 6 * pair + 3 * side + lane_of(shape) // LANES
-            pick = low(jnp.where(row_of(shape) == source, 1.0, 0.0))
-            inverse = times(inverse_first, pick) + times(inverse_second, pick)
+            inverse = jnp.concatenate(inverses[side], axis=1)
             hat = jnp.concatenate([q_ref[side, here, :], k_ref[side, here, :]], axis=1)
             hat = wide(hat) * backs
             grad = jnp.concatenate([turned_ref[side, here, :], dk_ref[side, here, :]], axis=1)
@@ -389,7 +393,7 @@
         ],
         in_specs=[pl.BlockSpec(memory_space=pltpu.SMEM)]
         + [pair_spec] * 4
-        + [pl.BlockSpec((rows, LANES), lambda pair: (0, 0)), pl.BlockSpec(qk_gains.shape, lambda pair: (0, 0))],
+        + [pl.BlockSpec((rows, 3 * LANES), lambda pair: (0, pair)), pl.BlockSpec(qk_gains.shape, lambda pair: (0, 0))],
         out_specs=[
             pl.BlockSpec((rows, 3 * LANES), lambda pair: (0, pair)),
             pl.BlockSpec((8, 2 * LANES), lambda pair: (0, 0)),
@@ -402,7 +406,7 @@
         ],
         compiler_params=pltpu.CompilerParams(vmem_limit_bytes=ROOM["backward"] * 2**20),
         cost_estimate=cost(36),
-    )(big_images, pinned(q_rows), pinned(k_rows), pinned(v_rows), do_rows, inverses, qk_gains)
+    )(big_images, pinned(q_rows), pinned(k_rows), pinned(v_rows), do_rows, pinned(inverses), qk_gains)
 
 
 FINE = 2 * PATCHES
@@ -598,7 +602,7 @@
         name="features",
         grid=(count,),
         out_shape=[
-            jax.ShapeDtypeStruct((tile * count, width), jnp.bfloat16),
+            pltpu.HBM((tile * count, width), jnp.bfloat16),
             jax.ShapeDtypeStruct((8, width), jnp.float32),
         ],
         in_specs=[
@@ -619,7 +623,7 @@
 def weights_kernel(*refs):
     keep_ref, send_ref = refs[-2:]
     halves, rows = keep_ref.shape[1:3]
-    odd, side = lax.axis_index("dp") & 1, lax.axis_index("hid")
+    odd, far, side = lax.axis_index("dp") & 1, lax.axis_index("dp") // 2, lax.axis_index("hid")
     at = 0
     for left_ref, right_ref in zip(refs[:-2:2], refs[1:-2:2]):
         tokens, columns = right_ref.shape
@@ -630,8 +634,8 @@
             for parity in range(2):
                 start = 2 * (2 * half + parity) * rows
                 even, uneven = total[start : start + rows], total[start + rows : start + 2 * rows]
-                keep_ref[odd ^ parity, half, :, cols] = low(jnp.where(side == 0, even, uneven))
-                send_ref[odd ^ parity, half, :, cols] = low(jnp.where(side == 0, uneven, even))
+                keep_ref[odd ^ parity, far ^ half, :, cols] = low(jnp.where(side == 0, even, uneven))
+                send_ref[odd ^ parity, far ^ half, :, cols] = low(jnp.where(side == 0, uneven, even))
 
 
 def weights(*products):
@@ -698,7 +702,36 @@
         input_output_aliases={6: 0} if more else {},
         compiler_params=pltpu.CompilerParams(vmem_limit_bytes=ROOM["token_rows"] * 2**20),
         cost_estimate=cost(0.3 * count),
-    )(sent, came, tokens, norm_gain, mine, other, *more)
+    )(pinned(sent), came, tokens, norm_gain, mine, other, *more)
+
+
+def finish_kernel(columns, *refs):
+    first_ref, second_ref, small_ref = refs[-3:]
+    rows = first_ref.shape[0]
+    values = [wide(ref[...]) for ref in refs[:-3]]
+    while len(values) > 1:
+        values = [first + second for first, second in zip(values[::2], values[1::2])]
+    first_ref[...] = values[0][:rows, :columns]
+    second_ref[...] = values[0][:rows, columns:]
+    small_ref[...] = values[0][rows:]
+
+
+def finish(terms, columns):
+    rows, whole = terms[0].shape[0] - 8, terms[0].shape[1]
+    spec = pl.BlockSpec(memory_space=VMEM)
+    return pl.pallas_call(
+        functools.partial(finish_kernel, columns),
+        name="finish",
+        out_shape=[
+            jax.ShapeDtypeStruct((rows, columns), jnp.float32),
+            jax.ShapeDtypeStruct((rows, whole - columns), jnp.float32),
+            jax.ShapeDtypeStruct((8, whole), jnp.float32),
+        ],
+        in_specs=[spec] * len(terms),
+        out_specs=[spec] * 3,
+        compiler_params=pltpu.CompilerParams(vmem_limit_bytes=16 * 2**20),
+        cost_estimate=cost(1),
+    )(*terms)
 
 
 def swap(value, axis, bit):
@@ -743,6 +776,7 @@
         parts.append(times(turned[:, : right.shape[0]], right[:, place * size : place * size + size]))
     shaped = jnp.concatenate(parts, axis=1).reshape(groups // 2, 2, sides, width // (groups * sides), -1)
     odd = lax.axis_index("dp") & 1
+    shaped = shaped[(lax.axis_index("dp") // 2) ^ jnp.arange(groups // 2)]
     shaped = shaped[:, odd ^ jnp.arange(2)][:, :, lax.axis_index("hid") ^ jnp.arange(sides)]
     shaped = shaped.transpose(1, 0, 2, 3, 4)
     for bit in reversed(bits_of("hid")):
@@ -761,20 +795,8 @@
     return lax.all_to_all(total, "dp", 0, 0, axis_index_groups=groups, tiled=True)
 
 
-def far_terms(total):
-    me = lax.axis_index("dp") // 2
-    terms = [lax.dynamic_index_in_dim(total, me, keepdims=False)]
-    for step in range(1, total.shape[0]):
-        block = lax.dynamic_index_in_dim(total, me ^ step, keepdims=False)
-        terms.append(swap(block, "dp", 2 * step))
-    return terms
-
-
-def added(terms):
-    values = [wide(term) for term in terms]
-    while len(values) > 1:
-        values = [first + second for first, second in zip(values[::2], values[1::2])]
-    return values[0]
+def far_terms(blocks):
+    return [blocks[0]] + [swap(block, "dp", 2 * step) for step, block in enumerate(blocks) if step > 0]
 
 
 def sum_everywhere(value, axes):
@@ -821,7 +843,7 @@
         second = low(wide(second_kept) + wide(second_came))
         small = jnp.broadcast_to(small, first.shape[:1] + small.shape[1:])
         sums = jnp.concatenate([jnp.concatenate([first, second], axis=2), small], axis=1)
-        return sums, low(kept + wide(out_came))
+        return [sums[step] for step in range(sums.shape[0])], low(kept + wide(out_came))
 
     def no_sums(*operands):
         return jax.tree.map(lambda kind: jnp.zeros(kind.shape, kind.dtype), kinds)
@@ -836,10 +858,9 @@
     terms = far_terms(sums)
     token_grad = token_rows(0, mine, came, tokens, norm_gain, cotangent, other, None)
     terms[1], token_grad = lax.optimization_barrier((terms[1], token_grad))
-    rows = sums.shape[1] - 8
-    w_qkv_grad = added([term[:rows, : 3 * columns] for term in terms])
-    w_out_t_grad = added([term[:rows, 3 * columns :] for term in terms])
-    small = added([term[rows : rows + 1] for term in terms]).reshape(-1)
+    terms[-1], w_in_grad, w_back_grad = lax.optimization_barrier((terms[-1], w_in_grad, w_back_grad))
+    w_qkv_grad, w_out_t_grad, small = finish(terms, 3 * columns)
+    small = small[0]
     small = sum_everywhere(small, ("hg",))
     own = lax.axis_index("dp") * lax.axis_size("hid") + lax.axis_index("hid")
     gain_rows = width // (groups * lax.axis_size("hid"))

time: 153 us -> 150 us (0.980)
  waiting for transfers between devices: 24.3 us -> 31.1 us
  other arithmetic: 12.2 us -> 8.21 us
  local copies, waits for them, and re-layouts: 9.09 us -> 5.44 us
  starting transfers between devices: 28 us -> 25.9 us
    ppermute x17, waiting for transfers between devices: 24.3 us -> 31.1 us  [swap(): lax.ppermute(value, axis, [(place, place ^ bit) for place in range(size)])]
    add x3 -> x0, other arithmetic: 4.01 us -> none  [added(): first + second]
    unnamed x36 -> x30, local copies, waits for them, and re-layouts: 4.18 us -> 0.73 us
  transfers between devices with their start and end apart: 18 -> 18, of which waited for: 7 -> 9; matrix products, arithmetic and copies ran while one was open for 8% -> 6% of each run, Pallas kernels for 34% -> 34%
where the time goes in v4:
time: 150 us; the launch traced here: 149 us
  Pallas kernels  77.1 us (51%)
  waiting for transfers between devices  31.1 us (21%)
  starting transfers between devices  25.9 us (17%)
  other arithmetic  8.21 us (5%)
  local copies, waits for them, and re-layouts  5.44 us (4%)
    ppermute x17, waiting for transfers between devices, swap(): lax.ppermute(value, axis, [(place, place ^ bit) for place in range(size)])  31.1 us
    pallas_call x1, Pallas kernels, dense(): pl.pallas_call(functools.partial(dense_kernel, count, tiles), name='dense...  21.7 us
    ppermute x17, starting transfers between devices, swap(): lax.ppermute(value, axis, [(place, place ^ bit) for place in range(size)])  20.2 us
    pallas_call x1, Pallas kernels, backward(): pl.pallas_call(backward_kernel, name='backward', grid=(heads // 2,), out_...  16.7 us
    pallas_call x1, Pallas kernels, forward(): pl.pallas_call(forward_kernel, name='forward', out_shape=[jax.ShapeDtypeS...  15.9 us
    pallas_call x2, Pallas kernels, weights(): pl.pallas_call(weights_kernel, name='weights', grid=(1,), out_shape=[jax....  6.16 us
    pallas_call x1, Pallas kernels, outputs(): pl.pallas_call(outputs_kernel, name='outputs', grid=(rows // tile,), out_...  5.86 us
    all_to_all x1, starting transfers between devices, rest_terms(): lax.all_to_all(total, 'dp', 0, 0, axis_index_groups=groups, tiled=True)  5.74 us
  transfers between devices with their start and end apart: 18, of which 9 were waited for; matrix products, arithmetic and copies ran while one was open for 6% of the time, Pallas kernels for 34%

profile of v4, /device:TPU:0, one launch (start us, length us, event | category | flops | bytes accessed | tf_op | source)
XLA Modules:
  0.0 149.3 jit_solution(4387926320387855373)
XLA Ops:
  0.6 3.0 %collective-permute-start.6 = (bf16[1176,384]{1,0:T(8,128)(2,1)}, bf16[1176,384]{1,0:T(8,128)(2,1)S(1)}, u32[]{:S(2)}, u32[]{:S(2)}) collective-permute-start(bf16[1176,384]{1,0:T(8,128)(2,1)} %mine_ref.5), channel_id=1, source_target_pairs={{0,2},{2,0},{1,3},{3,1},{4,6},{6,4},{5,7},{7,5},{8,10},{10,8},{9,1... | collective-permute-start | bytes 2709512 | tf_op jit(solution)/shard_map/ppermute | solution.py:739
  4.8 15.9 %forward.1 = (bf16[1176,768]{1,0:T(8,128)(2,1)S(1)}, bf16[6,1280,128]{2,1,0:T(8,128)(2,1)}, bf16[6,1280,128]{2,1,0:T(8,128)(2,1)}, bf16[6,1280,128]{2,1,0:T(8,12...) custom-call(s32[1]{0:T(128)S(6)} %copy.27.flag_ref, bf16[1176,768]{1,0:T(8,128)(2,1)} %tok_ref.5, ...), custom_call_target="tpu_custom_call" | custom-call | flops 24000000000 | bytes 1048576 | tf_op jit(solution)/shard_map/forward/pallas_call | solution.py:261
  20.8 3.1 %collective-permute-done.6.other_ref = bf16[1176,384]{1,0:T(8,128)(2,1)S(1)} collective-permute-done((bf16[1176,384]{1,0:T(8,128)(2,1)}, bf16[1176,384]{1,0:T(8,128)(2,1)S(1)}, u32[]{:S(2)}, u32[]{:S(2)}) %collective-permute-start.6) | collective-permute-done | bytes 903200 | tf_op jit(solution)/shard_map/ppermute | solution.py:739
  24.0 21.7 %dense.1 = (f32[1176,768]{1,0:T(8,128)S(1)}, bf16[1176,768]{1,0:T(8,128)(2,1)S(1)}, bf16[768,1280]{1,0:T(8,128)(2,1)}, bf16[768,1280]{1,0:T(8,128)(2,1)}, bf16[2...) custom-call(bf16[1176,768]{1,0:T(8,128)(2,1)S(1)} %get-tuple-element.80.normed_ref, ...), custom_call_target="tpu_custom_call" | custom-call | flops 24000000000 | bytes 1048576 | tf_op jit(solution)/shard_map/dense/pallas_call | solution.py:491
  45.7 5.9 %outputs.1 = (f32[1176,384]{1,0:T(8,128)}, bf16[1176,384]{1,0:T(8,128)(2,1)S(1)}, bf16[6,1280,128]{2,1,0:T(8,128)(2,1)S(1)}) custom-call(f32[1176,768]{1,0:T(8,128)S(1)} %get-tuple-element.81.part_ref, bf16[1176,768]{1,0:T(8,128)(2,1)S(1)} %copy-done, bf16[1176,384]{1,0:T(8,128)(2,1)S(1)} %get-tuple-element.82.att_ref, bf16[1176,384]{1,0:T(8,128)(2,1)S(1)} %copy-done.2, ...), custom_call_target="tpu_custom_call" | custom-call | flops 6000000000 | bytes 1048576 | tf_op jit(solution)/shard_map/outputs/pallas_call | solution.py:561
  51.6 1.8 %collective-permute-start.10 = (bf16[1176,384]{1,0:T(8,128)(2,1)S(1)}, bf16[1176,384]{1,0:T(8,128)(2,1)S(1)}, u32[]{:S(2)}, u32[]{:S(2)}) collective-permute-start(bf16[1176,384]{1,0:T(8,128)(2,1)S(1)} %get-tuple-element.89), channel_id=1, source_target_pairs={{0,2},{2,0},{1,3},{3,1},{4,6},{6,4},{5,7},{7,5},{8,10},{10,8},{9,1... | collective-permute-start | bytes 2709512 | tf_op jit(solution)/shard_map/ppermute | solution.py:739
  54.2 1.6 %collective-permute-start.11 = (bf16[4,96,1536]{2,1,0:T(8,128)(2,1)S(1)}, bf16[4,96,1536]{2,1,0:T(8,128)(2,1)S(1)}, u32[]{:S(2)}, u32[]{:S(2)}) collective-permute-start(bf16[4,96,1536]{2,1,0:T(8,128)(2,1)S(1)} %get-tuple-element.124), channel_id=1, source_target_pairs={{0,4},{4,0},{8,12},{12,8},{16,20},{20,16},{24,28},{28,24},{1,5},{5... | collective-permute-start | bytes 3538952 | tf_op jit(solution)/shard_map/ppermute | solution.py:739
  55.8 16.7 %backward.1 = (bf16[1176,1152]{1,0:T(8,128)(2,1)S(1)}, f32[8,256]{1,0:T(8,128)S(1)}) custom-call(s32[1]{0:T(128)S(6)} %copy.27.flag_ref, bf16[6,1280,128]{2,1,0:T(8,128)(2,1)} %get-tuple-element.77.q_ref, bf16[6,1280,128]{2,1,0:T(8,128)(2,1)} %get-tuple-element.78.k_ref, bf16[6,1280,128]{2,1,0:T(8,128)(2,1)} %get-tuple-element.79.v_ref, ...), custom_call_target="tpu_custom_call" | custom-call | flops 35999997952 | bytes 1048576 | tf_op jit(solution)/shard_map/backward/pallas_call | solution.py:386
  72.5 1.5 %collective-permute-done.10 = bf16[1176,384]{1,0:T(8,128)(2,1)S(1)} collective-permute-done((bf16[1176,384]{1,0:T(8,128)(2,1)S(1)}, bf16[1176,384]{1,0:T(8,128)(2,1)S(1)}, u32[]{:S(2)}, u32[]{:S(2)}) %collective-permute-start.10) | collective-permute-done | bytes 903200 | tf_op jit(solution)/shard_map/ppermute | solution.py:739
  74.0 8.3 %collective-permute-done.11 = bf16[4,96,1536]{2,1,0:T(8,128)(2,1)S(1)} collective-permute-done((bf16[4,96,1536]{2,1,0:T(8,128)(2,1)S(1)}, bf16[4,96,1536]{2,1,0:T(8,128)(2,1)S(1)}, u32[]{:S(2)}, u32[]{:S(2)}) %collective-permute-start.11) | collective-permute-done | bytes 1179680 | tf_op jit(solution)/shard_map/ppermute | solution.py:739
  82.4 4.4 %features.1 = (bf16[1176,768]{1,0:T(8,128)(2,1)}, f32[8,768]{1,0:T(8,128)S(1)}) custom-call(bf16[1176,1152]{1,0:T(8,128)(2,1)S(1)} %get-tuple-element.90.joined_ref, bf16[768,1152]{1,0:T(8,128)(2,1)S(1)} %copy-done.1, bf16[1176,768]{1,0:T(8,128)(2,1)S(1)} %get-tuple-element.91.mlp_ref, bf16[1176,768]{1,0:T(8,128)(2,1)S(1)} %copy-done), custom_call_target="tpu_custom_call" | custom-call | flops 900000000 | bytes 1048576 | tf_op jit(solution)/shard_map/features/pallas_call | solution.py:600
  86.8 1.4 add_convert_fusion.5
  88.2 5.7 %all-to-all-start = ((bf16[4,96,1536]{2,1,0:T(8,128)(2,1)}), bf16[4,96,1536]{2,1,0:T(8,128)(2,1)}, u32[]{:S(2)}, u32[]{:S(2)}) async-start(bf16[4,96,1536]{2,1,0:T(8,128)(2,1)} %add_convert_fusion.5), calls=%async_computation | async-start | bytes 2359296 | tf_op jit(solution)/shard_map/all_to_all | solution.py:795
  93.9 1.5 collective-permute-start.13
  95.4 29.1 %conditional.1 = (bf16[56,1536]{1,0:T(8,128)(2,1)S(1)}, bf16[56,1536]{1,0:T(8,128)(2,1)S(1)}, bf16[56,1536]{1,0:T(8,128)(2,1)S(1)}, bf16[56,1536]{1,0:T(8,128)(2,1)}, bf16[1176,384]{1,0:T(8,128)(2,1)}) conditional(s32[]{:T(128)} %bitcast.12, () %tuple.22, (f32[8,768]{1,0:T(8,128)S(1)}, f32[8,256]{1,0:T(8,128)S(1)}, bf16[768,1280]{1,0:T(8,128)(2,1)}, ...), branch_computations={%region_0.0_spmd, %region_1.2_spmd} | conditional | flops 6006967296 | bytes 65653980 | solution.py:853
  96.0 3.9 %weights.2 = (bf16[2,4,48,768]{3,2,1,0:T(8,128)(2,1)S(1)}, bf16[2,4,48,768]{3,2,1,0:T(8,128)(2,1)S(1)}) custom-call(bf16[768,1280]{1,0:T(8,128)(2,1)} %get-tuple-element.18.refs_0_, bf16[1176,1152]{1,0:T(8,128)(2,1)} %get-tuple-element.19.refs_1_), custom_call_target="tpu_custom_call" | custom-call | flops 3000000000 | bytes 1048576 | tf_op jit(solution)/shard_map/cond/branch_1_fun/weights/pallas_call | solution.py:653
  100.2 2.2 %weights.3 = (bf16[2,4,48,768]{3,2,1,0:T(8,128)(2,1)S(1)}, bf16[2,4,48,768]{3,2,1,0:T(8,128)(2,1)S(1)}) custom-call(bf16[768,1280]{1,0:T(8,128)(2,1)S(1)} %copy-done.18, bf16[1176,1152]{1,0:T(8,128)(2,1)S(1)} %copy-done.11, bf16[768,1280]{1,0:T(8,128)(2,1)S(1)} %copy-done.19, bf16[1176,384]{1,0:T(8,128)(2,1)S(1)} %copy-done.21), custom_call_target="tpu_custom_call" | custom-call | flops 3000000000 | bytes 1048576 | tf_op jit(solution)/shard_map/cond/branch_1_fun/weights/pallas_call | solution.py:653
  102.8 1.2 add_convert_fusion
  104.9 3.5 %collective-permute-start.2 = (bf16[4,48,768]{2,1,0:T(8,128)(2,1)}, bf16[4,48,768]{2,1,0:T(8,128)(2,1)}, u32[]{:S(2)}, u32[]{:S(2)}) collective-permute-start(bf16[4,48,768]{2,1,0:T(8,128)(2,1)} %slice_bitcast_fusion.2), channel_id=1, source_target_pairs={{0,4},{4,0},{8,12},{12,8},{16,20},{20,16},{24,28},{28,24},{1,5},{5... | collective-permute-start | bytes 884744 | tf_op jit(solution)/shard_map/cond/branch_1_fun/ppermute | solution.py:739
  110.2 2.0 %collective-permute-start.4 = (bf16[4,48,768]{2,1,0:T(8,128)(2,1)}, bf16[4,48,768]{2,1,0:T(8,128)(2,1)}, u32[]{:S(2)}, u32[]{:S(2)}) collective-permute-start(bf16[4,48,768]{2,1,0:T(8,128)(2,1)} %slice_bitcast_fusion), channel_id=1, source_target_pairs={{0,4},{4,0},{8,12},{12,8},{16,20},{20,16},{24,28},{28,24},{1,5},{5... | collective-permute-start | bytes 884744 | tf_op jit(solution)/shard_map/cond/branch_1_fun/ppermute | solution.py:739
  112.2 4.3 %collective-permute-done.5 = bf16[896]{0:T(1024)(128)(2,1)S(1)} collective-permute-done((bf16[896]{0:T(1024)(128)(2,1)S(1)}, bf16[896]{0:T(1024)(128)(2,1)S(1)}, u32[]{:S(2)}, u32[]{:S(2)}) %collective-permute-start.5) | collective-permute-done | bytes 1824 | tf_op jit(solution)/shard_map/cond/branch_1_fun/ppermute | solution.py:739
  116.7 1.0 fusion.1
  117.7 4.9 %collective-permute-done.4 = bf16[4,48,768]{2,1,0:T(8,128)(2,1)} collective-permute-done((bf16[4,48,768]{2,1,0:T(8,128)(2,1)}, bf16[4,48,768]{2,1,0:T(8,128)(2,1)}, u32[]{:S(2)}, u32[]{:S(2)}) %collective-permute-start.4) | collective-permute-done | bytes 294944 | tf_op jit(solution)/shard_map/cond/branch_1_fun/ppermute | solution.py:739
  122.6 1.1 fusion
  125.1 3.5 %collective-permute-start.15 = (bf16[56,1536]{1,0:T(8,128)(2,1)}, bf16[56,1536]{1,0:T(8,128)(2,1)S(1)}, u32[]{:S(2)}, u32[]{:S(2)}) collective-permute-start(bf16[56,1536]{1,0:T(8,128)(2,1)} %get-tuple-element.107), channel_id=1, source_target_pairs={{0,24},{4,28},{8,16},{12,20},{16,8},{20,12},{24,0},{28,4},{1,25},{... | collective-permute-start | bytes 516104 | tf_op jit(solution)/shard_map/ppermute | solution.py:739
  128.7 1.2 collective-permute-start.14
  129.9 2.4 %convert_reduce_fusion = (f32[96,768]{1,0:T(8,128)}, f32[96,768]{1,0:T(8,128)}) fusion(bf16[4,96,1536]{2,1,0:T(8,128)(2,1)} %all-to-all-done), kind=kLoop, calls=%fused_computation.26 | loop fusion | flops 1032192 | bytes 1769472 | tf_op jit(solution)/shard_map/reduce_sum | solution.py:857
  132.3 2.2 %collective-permute-done.15.refs_3_ = bf16[56,1536]{1,0:T(8,128)(2,1)S(1)} collective-permute-done((bf16[56,1536]{1,0:T(8,128)(2,1)}, bf16[56,1536]{1,0:T(8,128)(2,1)S(1)}, u32[]{:S(2)}, u32[]{:S(2)}) %collective-permute-start.15) | collective-permute-done | bytes 172064 | tf_op jit(solution)/shard_map/ppermute | solution.py:739
  134.4 1.8 %collective-permute-done.13.came_ref = bf16[1176,768]{1,0:T(8,128)(2,1)} collective-permute-done((bf16[1176,768]{1,0:T(8,128)(2,1)}, bf16[1176,768]{1,0:T(8,128)(2,1)}, u32[]{:S(2)}, u32[]{:S(2)}) %collective-permute-start.13) | collective-permute-done | bytes 1806368 | tf_op jit(solution)/shard_map/ppermute | solution.py:739
  136.2 5.5 %token_rows.1 = bf16[1176,768]{1,0:T(8,128)(2,1)} custom-call(bf16[1176,768]{1,0:T(8,128)(2,1)} %get-tuple-element.102.sent_ref, bf16[1176,768]{1,0:T(8,128)(2,1)} %collective-permute-done.13.came_ref, bf16[1176,768]{1,0:T(8,128)(2,1)S(1)} %copy-done, bf16[768]{0:T(1024)(128)(2,1)S(1)} %copy-done.5, bf16[1176,384]{1,0:T(8,128)(2,1)S(1)} %copy-done.2, ...), custom_call_target="tpu_custom_call" | custom-call | flops 900000000 | bytes 1048576 | tf_op jit(solution)/shard_map/token_rows/pallas_call | solution.py:687
  141.7 1.8 %collective-permute-done.14.refs_2_ = bf16[56,1536]{1,0:T(8,128)(2,1)S(1)} collective-permute-done((bf16[56,1536]{1,0:T(8,128)(2,1)}, bf16[56,1536]{1,0:T(8,128)(2,1)S(1)}, u32[]{:S(2)}, u32[]{:S(2)}) %collective-permute-start.14) | collective-permute-done | bytes 172064 | tf_op jit(solution)/shard_map/ppermute | solution.py:739
  144.9 3.1 %collective-permute-done.16 = f32[1536]{0:T(1024)S(1)} collective-permute-done((f32[1536]{0:T(1024)S(1)}, f32[1536]{0:T(1024)S(1)}, u32[]{:S(2)}, u32[]{:S(2)}) %collective-permute-start.16) | collective-permute-done | bytes 6176 | tf_op jit(solution)/shard_map/ppermute | solution.py:739
  (84 shorter events, 9.5 us)
Async XLA Ops:
  0.6 23.3 %collective-permute-start.6 = (bf16[1176,384]{1,0:T(8,128)(2,1)}, bf16[1176,384]{1,0:T(8,128)(2,1)S(1)}, u32[]{:S(2)}, u32[]{:S(2)}) collective-permute-start(bf16[1176,384]{1,0:T(8,128)(2,1)} %mine_ref.5), channel_id=1, source_target_pairs={{0,2},{2,0},{1,3},{3,1},{4,6},{6,4},{5,7},{7,5},{8,10},{10,8},{9,1... | collective-permute-start | bytes 2709512 | tf_op jit(solution)/shard_map/ppermute | solution.py:739
  3.6 20.3 %collective-permute-start.7 = (bf16[768,768]{1,0:T(8,128)(2,1)}, bf16[768,768]{1,0:T(8,128)(2,1)S(1)}, u32[]{:S(2)}, u32[]{:S(2)}) collective-permute-start(bf16[768,768]{1,0:T(8,128)(2,1)} %refs_0_.1), channel_id=1, source_target_pairs={{0,1},{1,0},{2,3},{3,2},{4,5},{5,4},{6,7},{7,6},{8,9},{9,8},{10,11... | collective-permute-start | bytes 3538952 | tf_op jit(solution)/shard_map/ppermute | solution.py:739
  3.6 20.3 %collective-permute-start.8 = (bf16[768,768]{1,0:T(8,128)(2,1)}, bf16[768,768]{1,0:T(8,128)(2,1)S(1)}, u32[]{:S(2)}, u32[]{:S(2)}) collective-permute-start(bf16[768,768]{1,0:T(8,128)(2,1)} %refs_2_.1), channel_id=1, source_target_pairs={{0,1},{1,0},{2,3},{3,2},{4,5},{5,4},{6,7},{7,6},{8,9},{9,8},{10,11... | collective-permute-start | bytes 3538952 | tf_op jit(solution)/shard_map/ppermute | solution.py:739
  4.8 19.1 %copy-start.2 = (bf16[1176,384]{1,0:T(8,128)(2,1)S(1)}, bf16[1176,384]{1,0:T(8,128)(2,1)}, u32[]{:S(2)}) copy-start(bf16[1176,384]{1,0:T(8,128)(2,1)} %mine_ref.5) | copy-start | bytes 2709508
  4.8 19.1 %copy-start.6 = (bf16[768,768]{1,0:T(8,128)(2,1)S(1)}, bf16[768,768]{1,0:T(8,128)(2,1)}, u32[]{:S(2)}) copy-start(bf16[768,768]{1,0:T(8,128)(2,1)} %refs_0_.1) | copy-start | bytes 3538948
  4.8 19.1 %copy-start.7 = (bf16[768,768]{1,0:T(8,128)(2,1)S(1)}, bf16[768,768]{1,0:T(8,128)(2,1)}, u32[]{:S(2)}) copy-start(bf16[768,768]{1,0:T(8,128)(2,1)} %refs_2_.1) | copy-start | bytes 3538948
  20.8 24.9 %copy-start.20 = (bf16[1176,384]{1,0:T(8,128)(2,1)}, bf16[1176,384]{1,0:T(8,128)(2,1)S(1)}, u32[]{:S(2)}) copy-start(bf16[1176,384]{1,0:T(8,128)(2,1)S(1)} %get-tuple-element.82.att_ref) | copy-start | bytes 2709508
  23.9 21.8 %copy-start.3 = (bf16[1176,384]{1,0:T(8,128)(2,1)}, bf16[1176,384]{1,0:T(8,128)(2,1)S(1)}, u32[]{:S(2)}) copy-start(bf16[1176,384]{1,0:T(8,128)(2,1)S(1)} %collective-permute-done.6.other_ref) | copy-start | bytes 2709508
  23.9 21.8 %copy-start = (bf16[1176,768]{1,0:T(8,128)(2,1)S(1)}, bf16[1176,768]{1,0:T(8,128)(2,1)}, u32[]{:S(2)}) copy-start(bf16[1176,768]{1,0:T(8,128)(2,1)} %tok_ref.5) | copy-start | bytes 5419012
  23.9 21.8 %copy-start.8 = (bf16[768,384]{1,0:T(8,128)(2,1)S(1)}, bf16[768,384]{1,0:T(8,128)(2,1)}, u32[]{:S(2)}) copy-start(bf16[768,384]{1,0:T(8,128)(2,1)} %w_out_ref.1) | copy-start | bytes 1769476
  45.7 7.7 %collective-permute-start.9 = (bf16[2,4,96,1536]{3,2,1,0:T(8,128)(2,1)S(1)}, bf16[2,4,96,1536]{3,2,1,0:T(8,128)(2,1)S(1)}, u32[]{:S(2)}, u32[]{:S(2)}) collective-permute-start(bf16[2,4,96,1536]{3,2,1,0:T(8,128)(2,1)S(1)} %get-tuple-element.85), channel_id=1, source_target_pairs={{0,1},{1,0},{2,3},{3,2},{4,5},{5,4},{6,7},{7,6},{8,9},{9,8},{10,11... | collective-permute-start | bytes 7077896 | tf_op jit(solution)/shard_map/ppermute | solution.py:739
  51.6 22.5 %collective-permute-start.10 = (bf16[1176,384]{1,0:T(8,128)(2,1)S(1)}, bf16[1176,384]{1,0:T(8,128)(2,1)S(1)}, u32[]{:S(2)}, u32[]{:S(2)}) collective-permute-start(bf16[1176,384]{1,0:T(8,128)(2,1)S(1)} %get-tuple-element.89), channel_id=1, source_target_pairs={{0,2},{2,0},{1,3},{3,1},{4,6},{6,4},{5,7},{7,5},{8,10},{10,8},{9,1... | collective-permute-start | bytes 2709512 | tf_op jit(solution)/shard_map/ppermute | solution.py:739
  54.2 28.2 %collective-permute-start.11 = (bf16[4,96,1536]{2,1,0:T(8,128)(2,1)S(1)}, bf16[4,96,1536]{2,1,0:T(8,128)(2,1)S(1)}, u32[]{:S(2)}, u32[]{:S(2)}) collective-permute-start(bf16[4,96,1536]{2,1,0:T(8,128)(2,1)S(1)} %get-tuple-element.124), channel_id=1, source_target_pairs={{0,4},{4,0},{8,12},{12,8},{16,20},{20,16},{24,28},{28,24},{1,5},{5... | collective-permute-start | bytes 3538952 | tf_op jit(solution)/shard_map/ppermute | solution.py:739
  55.8 26.6 %copy-start.1 = (bf16[768,1152]{1,0:T(8,128)(2,1)S(1)}, bf16[768,1152]{1,0:T(8,128)(2,1)}, u32[]{:S(2)}) copy-start(bf16[768,1152]{1,0:T(8,128)(2,1)} %w_ref.1) | copy-start | bytes 5308420
  72.5 14.3 %copy-start.10 = (bf16[1176,1152]{1,0:T(8,128)(2,1)}, bf16[1176,1152]{1,0:T(8,128)(2,1)S(1)}, u32[]{:S(2)}) copy-start(bf16[1176,1152]{1,0:T(8,128)(2,1)S(1)} %get-tuple-element.90.joined_ref) | copy-start | bytes 8128516
  74.0 12.8 %copy-start.14 = (bf16[1176,384]{1,0:T(8,128)(2,1)}, bf16[1176,384]{1,0:T(8,128)(2,1)S(1)}, u32[]{:S(2)}) copy-start(bf16[1176,384]{1,0:T(8,128)(2,1)S(1)} %collective-permute-done.10) | copy-start | bytes 2709508
  88.2 41.7 %all-to-all-start = ((bf16[4,96,1536]{2,1,0:T(8,128)(2,1)}), bf16[4,96,1536]{2,1,0:T(8,128)(2,1)}, u32[]{:S(2)}, u32[]{:S(2)}) async-start(bf16[4,96,1536]{2,1,0:T(8,128)(2,1)} %add_convert_fusion.5), calls=%async_computation | async-start | bytes 2359296 | tf_op jit(solution)/shard_map/all_to_all | solution.py:795
  93.9 42.3 %collective-permute-start.13 = (bf16[1176,768]{1,0:T(8,128)(2,1)}, bf16[1176,768]{1,0:T(8,128)(2,1)}, u32[]{:S(2)}, u32[]{:S(2)}) collective-permute-start(bf16[1176,768]{1,0:T(8,128)(2,1)} %get-tuple-element.102.sent_ref), channel_id=1, source_target_pairs={{0,2},{2,0},{1,3},{3,1},{4,6},{6,4},{5,7},{7,5},{8,10},{10,8},{9,1... | collective-permute-start | bytes 5419016 | tf_op jit(solution)/shard_map/ppermute | solution.py:739
  95.4 40.8 %copy-start.5 = (bf16[768]{0:T(1024)(128)(2,1)S(1)}, bf16[768]{0:T(1024)(128)(2,1)}, u32[]{:S(2)}) copy-start(bf16[768]{0:T(1024)(128)(2,1)} %gain_ref.1) | copy-start | bytes 4612
  95.5 8.5 %collective-permute-start = (f32[896]{0:T(1024)S(1)}, f32[896]{0:T(1024)S(1)}, u32[]{:S(2)}, u32[]{:S(2)}) collective-permute-start(f32[896]{0:T(1024)S(1)} %pad_maximum_fusion.1), channel_id=1, source_target_pairs={{0,1},{1,0},{2,3},{3,2},{4,5},{5,4},{6,7},{7,6},{8,9},{9,8},{10,11... | collective-permute-start | bytes 10760 | tf_op jit(solution)/shard_map/cond/branch_1_fun/ppermute | solution.py:739
  96.0 4.1 %copy-start.19 = (bf16[768,1280]{1,0:T(8,128)(2,1)S(1)}, bf16[768,1280]{1,0:T(8,128)(2,1)}, u32[]{:S(2)}) copy-start(bf16[768,1280]{1,0:T(8,128)(2,1)} %get-tuple-element.23.refs_2_) | copy-start | bytes 5898244 | tf_op jit(solution)/shard_map/cond
  96.0 4.3 %copy-start.21 = (bf16[1176,384]{1,0:T(8,128)(2,1)S(1)}, bf16[1176,384]{1,0:T(8,128)(2,1)}, u32[]{:S(2)}) copy-start(bf16[1176,384]{1,0:T(8,128)(2,1)} %get-tuple-element.24.refs_3_) | copy-start | bytes 2709508 | tf_op jit(solution)/shard_map/cond
  99.9 4.2 %collective-permute-start.1 = (bf16[2,4,48,768]{3,2,1,0:T(8,128)(2,1)S(1)}, bf16[2,4,48,768]{3,2,1,0:T(8,128)(2,1)S(1)}, u32[]{:S(2)}, u32[]{:S(2)}) collective-permute-start(bf16[2,4,48,768]{3,2,1,0:T(8,128)(2,1)S(1)} %get-tuple-element.21), channel_id=1, source_target_pairs={{0,1},{1,0},{2,3},{3,2},{4,5},{5,4},{6,7},{7,6},{8,9},{9,8},{10,11... | collective-permute-start | bytes 1769480 | tf_op jit(solution)/shard_map/cond/branch_1_fun/ppermute | solution.py:739
  102.5 6.0 %collective-permute-start.3 = (bf16[2,4,48,768]{3,2,1,0:T(8,128)(2,1)S(1)}, bf16[2,4,48,768]{3,2,1,0:T(8,128)(2,1)S(1)}, u32[]{:S(2)}, u32[]{:S(2)}) collective-permute-start(bf16[2,4,48,768]{3,2,1,0:T(8,128)(2,1)S(1)} %get-tuple-element.26), channel_id=1, source_target_pairs={{0,1},{1,0},{2,3},{3,2},{4,5},{5,4},{6,7},{7,6},{8,9},{9,8},{10,11... | collective-permute-start | bytes 1769480 | tf_op jit(solution)/shard_map/cond/branch_1_fun/ppermute | solution.py:739
  104.9 11.7 %collective-permute-start.2 = (bf16[4,48,768]{2,1,0:T(8,128)(2,1)}, bf16[4,48,768]{2,1,0:T(8,128)(2,1)}, u32[]{:S(2)}, u32[]{:S(2)}) collective-permute-start(bf16[4,48,768]{2,1,0:T(8,128)(2,1)} %slice_bitcast_fusion.2), channel_id=1, source_target_pairs={{0,4},{4,0},{8,12},{12,8},{16,20},{20,16},{24,28},{28,24},{1,5},{5... | collective-permute-start | bytes 884744 | tf_op jit(solution)/shard_map/cond/branch_1_fun/ppermute | solution.py:739
  108.5 8.1 %collective-permute-start.5 = (bf16[896]{0:T(1024)(128)(2,1)S(1)}, bf16[896]{0:T(1024)(128)(2,1)S(1)}, u32[]{:S(2)}, u32[]{:S(2)}) collective-permute-start(bf16[896]{0:T(1024)(128)(2,1)S(1)} %add_convert_fusion.3), channel_id=1, source_target_pairs={{0,4},{4,0},{8,12},{12,8},{16,20},{20,16},{24,28},{28,24},{1,5},{5... | collective-permute-start | bytes 5384 | tf_op jit(solution)/shard_map/cond/branch_1_fun/ppermute | solution.py:739
  110.2 12.3 %collective-permute-start.4 = (bf16[4,48,768]{2,1,0:T(8,128)(2,1)}, bf16[4,48,768]{2,1,0:T(8,128)(2,1)}, u32[]{:S(2)}, u32[]{:S(2)}) collective-permute-start(bf16[4,48,768]{2,1,0:T(8,128)(2,1)} %slice_bitcast_fusion), channel_id=1, source_target_pairs={{0,4},{4,0},{8,12},{12,8},{16,20},{20,16},{24,28},{28,24},{1,5},{5... | collective-permute-start | bytes 884744 | tf_op jit(solution)/shard_map/cond/branch_1_fun/ppermute | solution.py:739
  125.1 9.3 %collective-permute-start.15 = (bf16[56,1536]{1,0:T(8,128)(2,1)}, bf16[56,1536]{1,0:T(8,128)(2,1)S(1)}, u32[]{:S(2)}, u32[]{:S(2)}) collective-permute-start(bf16[56,1536]{1,0:T(8,128)(2,1)} %get-tuple-element.107), channel_id=1, source_target_pairs={{0,24},{4,28},{8,16},{12,20},{16,8},{20,12},{24,0},{28,4},{1,25},{... | collective-permute-start | bytes 516104 | tf_op jit(solution)/shard_map/ppermute | solution.py:739
  128.7 13.0 %collective-permute-start.12 = (bf16[56,1536]{1,0:T(8,128)(2,1)}, bf16[56,1536]{1,0:T(8,128)(2,1)S(1)}, u32[]{:S(2)}, u32[]{:S(2)}) collective-permute-start(bf16[56,1536]{1,0:T(8,128)(2,1)} %copy-done.16), channel_id=1, source_target_pairs={{0,8},{4,12},{8,0},{12,4},{16,24},{20,28},{24,16},{28,20},{1,9},{5... | collective-permute-start | bytes 516104 | tf_op jit(solution)/shard_map/ppermute | solution.py:739
  128.7 14.8 %collective-permute-start.14 = (bf16[56,1536]{1,0:T(8,128)(2,1)}, bf16[56,1536]{1,0:T(8,128)(2,1)S(1)}, u32[]{:S(2)}, u32[]{:S(2)}) collective-permute-start(bf16[56,1536]{1,0:T(8,128)(2,1)} %copy-done.17), channel_id=1, source_target_pairs={{0,16},{4,20},{8,24},{12,28},{16,0},{20,4},{24,8},{28,12},{1,17},{... | collective-permute-start | bytes 516104 | tf_op jit(solution)/shard_map/ppermute | solution.py:739
  129.9 6.3 %copy-start.4 = (bf16[1176,384]{1,0:T(8,128)(2,1)S(1)}, bf16[1176,384]{1,0:T(8,128)(2,1)}, u32[]{:S(2)}) copy-start(bf16[1176,384]{1,0:T(8,128)(2,1)} %copy-done.3) | copy-start | bytes 2709508
  144.3 3.7 %collective-permute-start.16 = (f32[1536]{0:T(1024)S(1)}, f32[1536]{0:T(1024)S(1)}, u32[]{:S(2)}, u32[]{:S(2)}) collective-permute-start(f32[1536]{0:T(1024)S(1)} %slice_reduce_fusion.1), channel_id=1, source_target_pairs={{0,2},{2,0},{1,3},{3,1},{4,6},{6,4},{5,7},{7,5},{8,10},{10,8},{9,1... | collective-permute-start | bytes 18440 | tf_op jit(solution)/shard_map/ppermute | solution.py:739
  (8 other events, 20.2 us)

commit v5 on v4

--- a/solution.py
+++ b/solution.py
@@ -305,8 +305,8 @@
     k_gain = jnp.concatenate([k_gain, zeros], axis=1)
 
     def attend(side, _, big):
-        for start in range(0, rows, tile):
-            here = slice(start, start + tile)
+        for start in range(0, rows, rows if big else tile):
+            here = slice(start, start + (rows if big else tile))
             if big:
                 over = slice(0, padded)
             else:
@@ -857,8 +857,8 @@
     w_back_grad = jnp.sum(wide(mlp_terms[:, :, hidden:]), axis=0)
     terms = far_terms(sums)
     token_grad = token_rows(0, mine, came, tokens, norm_gain, cotangent, other, None)
-    terms[1], token_grad = lax.optimization_barrier((terms[1], token_grad))
-    terms[-1], w_in_grad, w_back_grad = lax.optimization_barrier((terms[-1], w_in_grad, w_back_grad))
+    held = (terms[1], token_grad, w_in_grad, w_back_grad)
+    terms[1], token_grad, w_in_grad, w_back_grad = lax.optimization_barrier(held)
     w_qkv_grad, w_out_t_grad, small = finish(terms, 3 * columns)
     small = small[0]
     small = sum_everywhere(small, ("hg",))

time: 150 us -> 149 us (level)
    all_to_all x1, starting transfers between devices: 5.74 us -> 7.47 us  [rest_terms(): lax.all_to_all(total, 'dp', 0, 0, axis_index_groups=groups, tiled=True)]
    ppermute x17, starting transfers between devices: 20.2 us -> 18.6 us  [swap(): lax.ppermute(value, axis, [(place, place ^ bit) for place in range(size)])]
  transfers between devices with their start and end apart: 18 -> 18, of which waited for: 9 -> 7; matrix products, arithmetic and copies ran while one was open for 6% -> 6% of each run, Pallas kernels for 34% -> 34%
where the time goes in v5:
time: 149 us
  Pallas kernels  77 us (52%)
  waiting for transfers between devices  31.1 us (21%)
  starting transfers between devices  26.1 us (18%)
  other arithmetic  8.22 us (6%)
  local copies, waits for them, and re-layouts  4.62 us (3%)
    ppermute x17, waiting for transfers between devices, swap(): lax.ppermute(value, axis, [(place, place ^ bit) for place in range(size)])  31.1 us
    pallas_call x1, Pallas kernels, dense(): pl.pallas_call(functools.partial(dense_kernel, count, tiles), name='dense...  21.7 us
    ppermute x17, starting transfers between devices, swap(): lax.ppermute(value, axis, [(place, place ^ bit) for place in range(size)])  18.6 us
    pallas_call x1, Pallas kernels, backward(): pl.pallas_call(backward_kernel, name='backward', grid=(heads // 2,), out_...  16.7 us
    pallas_call x1, Pallas kernels, forward(): pl.pallas_call(forward_kernel, name='forward', out_shape=[jax.ShapeDtypeS...  15.9 us
    all_to_all x1, starting transfers between devices, rest_terms(): lax.all_to_all(total, 'dp', 0, 0, axis_index_groups=groups, tiled=True)  7.47 us
    pallas_call x2, Pallas kernels, weights(): pl.pallas_call(weights_kernel, name='weights', grid=(1,), out_shape=[jax....  6.16 us
    pallas_call x1, Pallas kernels, outputs(): pl.pallas_call(outputs_kernel, name='outputs', grid=(rows // tile,), out_...  5.86 us
  transfers between devices with their start and end apart: 18, of which 7 were waited for; matrix products, arithmetic and copies ran while one was open for 6% of the time, Pallas kernels for 34%

profile of v5, /device:TPU:0, one launch (start us, length us, event | category | flops | bytes accessed | tf_op | source)
XLA Modules:
  0.0 148.7 jit_solution(723853523290551642)
XLA Ops:
  0.6 3.0 %collective-permute-start.6 = (bf16[1176,384]{1,0:T(8,128)(2,1)}, bf16[1176,384]{1,0:T(8,128)(2,1)S(1)}, u32[]{:S(2)}, u32[]{:S(2)}) collective-permute-start(bf16[1176,384]{1,0:T(8,128)(2,1)} %mine_ref.5), channel_id=1, source_target_pairs={{0,2},{2,0},{1,3},{3,1},{4,6},{6,4},{5,7},{7,5},{8,10},{10,8},{9,1... | collective-permute-start | bytes 2709512 | tf_op jit(solution)/shard_map/ppermute | solution.py:739
  4.8 15.9 %forward.1 = (bf16[1176,768]{1,0:T(8,128)(2,1)S(1)}, bf16[6,1280,128]{2,1,0:T(8,128)(2,1)}, bf16[6,1280,128]{2,1,0:T(8,128)(2,1)}, bf16[6,1280,128]{2,1,0:T(8,12...) custom-call(s32[1]{0:T(128)S(6)} %copy.27.flag_ref, bf16[1176,768]{1,0:T(8,128)(2,1)} %tok_ref.5, ...), custom_call_target="tpu_custom_call" | custom-call | flops 24000000000 | bytes 1048576 | tf_op jit(solution)/shard_map/forward/pallas_call | solution.py:261
  20.8 3.1 %collective-permute-done.6.other_ref = bf16[1176,384]{1,0:T(8,128)(2,1)S(1)} collective-permute-done((bf16[1176,384]{1,0:T(8,128)(2,1)}, bf16[1176,384]{1,0:T(8,128)(2,1)S(1)}, u32[]{:S(2)}, u32[]{:S(2)}) %collective-permute-start.6) | collective-permute-done | bytes 903200 | tf_op jit(solution)/shard_map/ppermute | solution.py:739
  24.0 21.7 %dense.1 = (f32[1176,768]{1,0:T(8,128)S(1)}, bf16[1176,768]{1,0:T(8,128)(2,1)S(1)}, bf16[768,1280]{1,0:T(8,128)(2,1)}, bf16[768,1280]{1,0:T(8,128)(2,1)}, bf16[2...) custom-call(bf16[1176,768]{1,0:T(8,128)(2,1)S(1)} %get-tuple-element.79.normed_ref, ...), custom_call_target="tpu_custom_call" | custom-call | flops 24000000000 | bytes 1048576 | tf_op jit(solution)/shard_map/dense/pallas_call | solution.py:491
  45.7 5.9 %outputs.1 = (f32[1176,384]{1,0:T(8,128)}, bf16[1176,384]{1,0:T(8,128)(2,1)S(1)}, bf16[6,1280,128]{2,1,0:T(8,128)(2,1)S(1)}) custom-call(f32[1176,768]{1,0:T(8,128)S(1)} %get-tuple-element.80.part_ref, bf16[1176,768]{1,0:T(8,128)(2,1)S(1)} %copy-done, bf16[1176,384]{1,0:T(8,128)(2,1)S(1)} %get-tuple-element.81.att_ref, bf16[1176,384]{1,0:T(8,128)(2,1)S(1)} %copy-done.2, ...), custom_call_target="tpu_custom_call" | custom-call | flops 6000000000 | bytes 1048576 | tf_op jit(solution)/shard_map/outputs/pallas_call | solution.py:561
  51.6 1.8 %collective-permute-start.10 = (bf16[1176,384]{1,0:T(8,128)(2,1)S(1)}, bf16[1176,384]{1,0:T(8,128)(2,1)S(1)}, u32[]{:S(2)}, u32[]{:S(2)}) collective-permute-start(bf16[1176,384]{1,0:T(8,128)(2,1)S(1)} %get-tuple-element.88), channel_id=1, source_target_pairs={{0,2},{2,0},{1,3},{3,1},{4,6},{6,4},{5,7},{7,5},{8,10},{10,8},{9,1... | collective-permute-start | bytes 2709512 | tf_op jit(solution)/shard_map/ppermute | solution.py:739
  54.2 3.1 %collective-permute-start.11 = (bf16[4,96,1536]{2,1,0:T(8,128)(2,1)S(1)}, bf16[4,96,1536]{2,1,0:T(8,128)(2,1)S(1)}, u32[]{:S(2)}, u32[]{:S(2)}) collective-permute-start(bf16[4,96,1536]{2,1,0:T(8,128)(2,1)S(1)} %get-tuple-element.122), channel_id=1, source_target_pairs={{0,4},{4,0},{8,12},{12,8},{16,20},{20,16},{24,28},{28,24},{1,5},{5... | collective-permute-start | bytes 3538952 | tf_op jit(solution)/shard_map/ppermute | solution.py:739
  57.3 16.7 %backward.1 = (bf16[1176,1152]{1,0:T(8,128)(2,1)S(1)}, f32[8,256]{1,0:T(8,128)S(1)}) custom-call(s32[1]{0:T(128)S(6)} %copy.27.flag_ref, bf16[6,1280,128]{2,1,0:T(8,128)(2,1)} %get-tuple-element.76.q_ref, bf16[6,1280,128]{2,1,0:T(8,128)(2,1)} %get-tuple-element.77.k_ref, bf16[6,1280,128]{2,1,0:T(8,128)(2,1)} %get-tuple-element.78.v_ref, ...), custom_call_target="tpu_custom_call" | custom-call | flops 35999997952 | bytes 1048576 | tf_op jit(solution)/shard_map/backward/pallas_call | solution.py:386
  74.1 9.1 %collective-permute-done.11 = bf16[4,96,1536]{2,1,0:T(8,128)(2,1)S(1)} collective-permute-done((bf16[4,96,1536]{2,1,0:T(8,128)(2,1)S(1)}, bf16[4,96,1536]{2,1,0:T(8,128)(2,1)S(1)}, u32[]{:S(2)}, u32[]{:S(2)}) %collective-permute-start.11) | collective-permute-done | bytes 1179680 | tf_op jit(solution)/shard_map/ppermute | solution.py:739
  83.2 4.4 %features.1 = (bf16[1176,768]{1,0:T(8,128)(2,1)}, f32[8,768]{1,0:T(8,128)S(1)}) custom-call(bf16[1176,1152]{1,0:T(8,128)(2,1)S(1)} %get-tuple-element.89.joined_ref, bf16[768,1152]{1,0:T(8,128)(2,1)S(1)} %copy-done.1, bf16[1176,768]{1,0:T(8,128)(2,1)S(1)} %get-tuple-element.90.mlp_ref, bf16[1176,768]{1,0:T(8,128)(2,1)S(1)} %copy-done), custom_call_target="tpu_custom_call" | custom-call | flops 900000000 | bytes 1048576 | tf_op jit(solution)/shard_map/features/pallas_call | solution.py:600
  87.7 1.4 add_convert_fusion.5
  89.0 7.5 %all-to-all-start = ((bf16[4,96,1536]{2,1,0:T(8,128)(2,1)}), bf16[4,96,1536]{2,1,0:T(8,128)(2,1)}, u32[]{:S(2)}, u32[]{:S(2)}) async-start(bf16[4,96,1536]{2,1,0:T(8,128)(2,1)} %add_convert_fusion.5), calls=%async_computation | async-start | bytes 2359296 | tf_op jit(solution)/shard_map/all_to_all | solution.py:795
  96.5 1.5 %collective-permute-start.13 = (bf16[1176,768]{1,0:T(8,128)(2,1)}, bf16[1176,768]{1,0:T(8,128)(2,1)}, u32[]{:S(2)}, u32[]{:S(2)}) collective-permute-start(bf16[1176,768]{1,0:T(8,128)(2,1)} %get-tuple-element.101.sent_ref), channel_id=1, source_target_pairs={{0,2},{2,0},{1,3},{3,1},{4,6},{6,4},{5,7},{7,5},{8,10},{10,8},{9,1... | collective-permute-start | bytes 5419016 | tf_op jit(solution)/shard_map/ppermute | solution.py:739
  98.0 26.4 %conditional.1 = (bf16[56,1536]{1,0:T(8,128)(2,1)S(1)}, bf16[56,1536]{1,0:T(8,128)(2,1)S(1)}, bf16[56,1536]{1,0:T(8,128)(2,1)S(1)}, bf16[56,1536]{1,0:T(8,128)(2,1)S(1)}, bf16[1176,384]{1,0:T(8,128)(2,1)}) conditional(s32[]{:T(128)} %bitcast.12, () %tuple.21, (f32[8,768]{1,0:T(8,128)S(1)}, f32[8,256]{1,0:T(8,128)S(1)}, bf16[768,1280]{1,0:T(8,128)(2,1)}, ...), branch_computations={%region_0.0_spmd, %region_1.2_spmd} | conditional | flops 6006967296 | bytes 65653980 | solution.py:853
  98.1 3.9 %weights.2 = (bf16[2,4,48,768]{3,2,1,0:T(8,128)(2,1)S(1)}, bf16[2,4,48,768]{3,2,1,0:T(8,128)(2,1)S(1)}) custom-call(bf16[768,1280]{1,0:T(8,128)(2,1)} %get-tuple-element.18.refs_0_, bf16[1176,1152]{1,0:T(8,128)(2,1)} %get-tuple-element.19.refs_1_), custom_call_target="tpu_custom_call" | custom-call | flops 3000000000 | bytes 1048576 | tf_op jit(solution)/shard_map/cond/branch_1_fun/weights/pallas_call | solution.py:653
  102.6 2.2 %weights.3 = (bf16[2,4,48,768]{3,2,1,0:T(8,128)(2,1)S(1)}, bf16[2,4,48,768]{3,2,1,0:T(8,128)(2,1)S(1)}) custom-call(bf16[768,1280]{1,0:T(8,128)(2,1)S(1)} %copy-done.19, bf16[1176,1152]{1,0:T(8,128)(2,1)S(1)} %copy-done.11, bf16[768,1280]{1,0:T(8,128)(2,1)S(1)} %copy-done.20, bf16[1176,384]{1,0:T(8,128)(2,1)S(1)} %copy-done.22), custom_call_target="tpu_custom_call" | custom-call | flops 3000000000 | bytes 1048576 | tf_op jit(solution)/shard_map/cond/branch_1_fun/weights/pallas_call | solution.py:653
  105.2 1.2 add_convert_fusion
  106.6 0.7 slice_bitcast_fusion.2
  107.5 1.8 %collective-permute-start.5 = (bf16[896]{0:T(1024)(128)(2,1)S(1)}, bf16[896]{0:T(1024)(128)(2,1)S(1)}, u32[]{:S(2)}, u32[]{:S(2)}) collective-permute-start(bf16[896]{0:T(1024)(128)(2,1)S(1)} %add_convert_fusion.3), channel_id=1, source_target_pairs={{0,4},{4,0},{8,12},{12,8},{16,20},{20,16},{24,28},{28,24},{1,5},{5... | collective-permute-start | bytes 5384 | tf_op jit(solution)/shard_map/cond/branch_1_fun/ppermute | solution.py:739
  109.5 0.8 copy-done.12
  111.3 6.2 %collective-permute-done.5 = bf16[896]{0:T(1024)(128)(2,1)S(1)} collective-permute-done((bf16[896]{0:T(1024)(128)(2,1)S(1)}, bf16[896]{0:T(1024)(128)(2,1)S(1)}, u32[]{:S(2)}, u32[]{:S(2)}) %collective-permute-start.5) | collective-permute-done | bytes 1824 | tf_op jit(solution)/shard_map/cond/branch_1_fun/ppermute | solution.py:739
  117.6 1.0 fusion.1
  118.6 4.6 %collective-permute-done.4 = bf16[4,48,768]{2,1,0:T(8,128)(2,1)} collective-permute-done((bf16[4,48,768]{2,1,0:T(8,128)(2,1)}, bf16[4,48,768]{2,1,0:T(8,128)(2,1)}, u32[]{:S(2)}, u32[]{:S(2)}) %collective-permute-start.4) | collective-permute-done | bytes 294944 | tf_op jit(solution)/shard_map/cond/branch_1_fun/ppermute | solution.py:739
  123.2 1.1 fusion
  125.1 2.0 %collective-permute-start.12 = (bf16[56,1536]{1,0:T(8,128)(2,1)}, bf16[56,1536]{1,0:T(8,128)(2,1)S(1)}, u32[]{:S(2)}, u32[]{:S(2)}) collective-permute-start(bf16[56,1536]{1,0:T(8,128)(2,1)} %copy-done.16), channel_id=1, source_target_pairs={{0,8},{4,12},{8,0},{12,4},{16,24},{20,28},{24,16},{28,20},{1,9},{5... | collective-permute-start | bytes 516104 | tf_op jit(solution)/shard_map/ppermute | solution.py:739
  127.1 2.4 %collective-permute-start.14 = (bf16[56,1536]{1,0:T(8,128)(2,1)}, bf16[56,1536]{1,0:T(8,128)(2,1)S(1)}, u32[]{:S(2)}, u32[]{:S(2)}) collective-permute-start(bf16[56,1536]{1,0:T(8,128)(2,1)} %copy-done.17), channel_id=1, source_target_pairs={{0,16},{4,20},{8,24},{12,28},{16,0},{20,4},{24,8},{28,12},{1,17},{... | collective-permute-start | bytes 516104 | tf_op jit(solution)/shard_map/ppermute | solution.py:739
  130.2 2.4 %convert_reduce_fusion = (f32[96,768]{1,0:T(8,128)}, f32[96,768]{1,0:T(8,128)}) fusion(bf16[4,96,1536]{2,1,0:T(8,128)(2,1)} %all-to-all-done), kind=kLoop, calls=%fused_computation.26 | loop fusion | flops 1032192 | bytes 1769472 | tf_op jit(solution)/shard_map/reduce_sum | solution.py:857
  132.5 2.8 %collective-permute-done.13.came_ref = bf16[1176,768]{1,0:T(8,128)(2,1)} collective-permute-done((bf16[1176,768]{1,0:T(8,128)(2,1)}, bf16[1176,768]{1,0:T(8,128)(2,1)}, u32[]{:S(2)}, u32[]{:S(2)}) %collective-permute-start.13) | collective-permute-done | bytes 1806368 | tf_op jit(solution)/shard_map/ppermute | solution.py:739
  135.3 5.5 %token_rows.1 = bf16[1176,768]{1,0:T(8,128)(2,1)} custom-call(bf16[1176,768]{1,0:T(8,128)(2,1)} %get-tuple-element.101.sent_ref, bf16[1176,768]{1,0:T(8,128)(2,1)} %collective-permute-done.13.came_ref, bf16[1176,768]{1,0:T(8,128)(2,1)S(1)} %copy-done, bf16[768]{0:T(1024)(128)(2,1)S(1)} %copy-done.5, bf16[1176,384]{1,0:T(8,128)(2,1)S(1)} %copy-done.2, ...), custom_call_target="tpu_custom_call" | custom-call | flops 900000000 | bytes 1048576 | tf_op jit(solution)/shard_map/token_rows/pallas_call | solution.py:687
  140.8 2.2 %collective-permute-done.14.refs_2_ = bf16[56,1536]{1,0:T(8,128)(2,1)S(1)} collective-permute-done((bf16[56,1536]{1,0:T(8,128)(2,1)}, bf16[56,1536]{1,0:T(8,128)(2,1)S(1)}, u32[]{:S(2)}, u32[]{:S(2)}) %collective-permute-start.14) | collective-permute-done | bytes 172064 | tf_op jit(solution)/shard_map/ppermute | solution.py:739
  142.9 0.8 finish.1
  144.3 3.1 %collective-permute-done.16 = f32[1536]{0:T(1024)S(1)} collective-permute-done((f32[1536]{0:T(1024)S(1)}, f32[1536]{0:T(1024)S(1)}, u32[]{:S(2)}, u32[]{:S(2)}) %collective-permute-start.16) | collective-permute-done | bytes 6176 | tf_op jit(solution)/shard_map/ppermute | solution.py:739
  (86 shorter events, 7.3 us)
Async XLA Ops:
  0.6 23.3 %collective-permute-start.6 = (bf16[1176,384]{1,0:T(8,128)(2,1)}, bf16[1176,384]{1,0:T(8,128)(2,1)S(1)}, u32[]{:S(2)}, u32[]{:S(2)}) collective-permute-start(bf16[1176,384]{1,0:T(8,128)(2,1)} %mine_ref.5), channel_id=1, source_target_pairs={{0,2},{2,0},{1,3},{3,1},{4,6},{6,4},{5,7},{7,5},{8,10},{10,8},{9,1... | collective-permute-start | bytes 2709512 | tf_op jit(solution)/shard_map/ppermute | solution.py:739
  3.6 20.3 %collective-permute-start.7 = (bf16[768,768]{1,0:T(8,128)(2,1)}, bf16[768,768]{1,0:T(8,128)(2,1)S(1)}, u32[]{:S(2)}, u32[]{:S(2)}) collective-permute-start(bf16[768,768]{1,0:T(8,128)(2,1)} %refs_0_.1), channel_id=1, source_target_pairs={{0,1},{1,0},{2,3},{3,2},{4,5},{5,4},{6,7},{7,6},{8,9},{9,8},{10,11... | collective-permute-start | bytes 3538952 | tf_op jit(solution)/shard_map/ppermute | solution.py:739
  3.6 20.3 %collective-permute-start.8 = (bf16[768,768]{1,0:T(8,128)(2,1)}, bf16[768,768]{1,0:T(8,128)(2,1)S(1)}, u32[]{:S(2)}, u32[]{:S(2)}) collective-permute-start(bf16[768,768]{1,0:T(8,128)(2,1)} %refs_2_.1), channel_id=1, source_target_pairs={{0,1},{1,0},{2,3},{3,2},{4,5},{5,4},{6,7},{7,6},{8,9},{9,8},{10,11... | collective-permute-start | bytes 3538952 | tf_op jit(solution)/shard_map/ppermute | solution.py:739
  4.8 19.1 %copy-start.2 = (bf16[1176,384]{1,0:T(8,128)(2,1)S(1)}, bf16[1176,384]{1,0:T(8,128)(2,1)}, u32[]{:S(2)}) copy-start(bf16[1176,384]{1,0:T(8,128)(2,1)} %mine_ref.5) | copy-start | bytes 2709508
  4.8 19.1 %copy-start.6 = (bf16[768,768]{1,0:T(8,128)(2,1)S(1)}, bf16[768,768]{1,0:T(8,128)(2,1)}, u32[]{:S(2)}) copy-start(bf16[768,768]{1,0:T(8,128)(2,1)} %refs_0_.1) | copy-start | bytes 3538948
  4.8 19.1 %copy-start.7 = (bf16[768,768]{1,0:T(8,128)(2,1)S(1)}, bf16[768,768]{1,0:T(8,128)(2,1)}, u32[]{:S(2)}) copy-start(bf16[768,768]{1,0:T(8,128)(2,1)} %refs_2_.1) | copy-start | bytes 3538948
  20.8 24.9 %copy-start.21 = (bf16[1176,384]{1,0:T(8,128)(2,1)}, bf16[1176,384]{1,0:T(8,128)(2,1)S(1)}, u32[]{:S(2)}) copy-start(bf16[1176,384]{1,0:T(8,128)(2,1)S(1)} %get-tuple-element.81.att_ref) | copy-start | bytes 2709508
  23.9 21.8 %copy-start.3 = (bf16[1176,384]{1,0:T(8,128)(2,1)}, bf16[1176,384]{1,0:T(8,128)(2,1)S(1)}, u32[]{:S(2)}) copy-start(bf16[1176,384]{1,0:T(8,128)(2,1)S(1)} %collective-permute-done.6.other_ref) | copy-start | bytes 2709508
  23.9 21.8 %copy-start = (bf16[1176,768]{1,0:T(8,128)(2,1)S(1)}, bf16[1176,768]{1,0:T(8,128)(2,1)}, u32[]{:S(2)}) copy-start(bf16[1176,768]{1,0:T(8,128)(2,1)} %tok_ref.5) | copy-start | bytes 5419012
  23.9 21.8 %copy-start.8 = (bf16[768,384]{1,0:T(8,128)(2,1)S(1)}, bf16[768,384]{1,0:T(8,128)(2,1)}, u32[]{:S(2)}) copy-start(bf16[768,384]{1,0:T(8,128)(2,1)} %w_out_ref.1) | copy-start | bytes 1769476
  45.7 7.7 %collective-permute-start.9 = (bf16[2,4,96,1536]{3,2,1,0:T(8,128)(2,1)S(1)}, bf16[2,4,96,1536]{3,2,1,0:T(8,128)(2,1)S(1)}, u32[]{:S(2)}, u32[]{:S(2)}) collective-permute-start(bf16[2,4,96,1536]{3,2,1,0:T(8,128)(2,1)S(1)} %get-tuple-element.84), channel_id=1, source_target_pairs={{0,1},{1,0},{2,3},{3,2},{4,5},{5,4},{6,7},{7,6},{8,9},{9,8},{10,11... | collective-permute-start | bytes 7077896 | tf_op jit(solution)/shard_map/ppermute | solution.py:739
  51.6 22.5 %collective-permute-start.10 = (bf16[1176,384]{1,0:T(8,128)(2,1)S(1)}, bf16[1176,384]{1,0:T(8,128)(2,1)S(1)}, u32[]{:S(2)}, u32[]{:S(2)}) collective-permute-start(bf16[1176,384]{1,0:T(8,128)(2,1)S(1)} %get-tuple-element.88), channel_id=1, source_target_pairs={{0,2},{2,0},{1,3},{3,1},{4,6},{6,4},{5,7},{7,5},{8,10},{10,8},{9,1... | collective-permute-start | bytes 2709512 | tf_op jit(solution)/shard_map/ppermute | solution.py:739
  54.2 29.0 %collective-permute-start.11 = (bf16[4,96,1536]{2,1,0:T(8,128)(2,1)S(1)}, bf16[4,96,1536]{2,1,0:T(8,128)(2,1)S(1)}, u32[]{:S(2)}, u32[]{:S(2)}) collective-permute-start(bf16[4,96,1536]{2,1,0:T(8,128)(2,1)S(1)} %get-tuple-element.122), channel_id=1, source_target_pairs={{0,4},{4,0},{8,12},{12,8},{16,20},{20,16},{24,28},{28,24},{1,5},{5... | collective-permute-start | bytes 3538952 | tf_op jit(solution)/shard_map/ppermute | solution.py:739
  57.3 25.9 %copy-start.1 = (bf16[768,1152]{1,0:T(8,128)(2,1)S(1)}, bf16[768,1152]{1,0:T(8,128)(2,1)}, u32[]{:S(2)}) copy-start(bf16[768,1152]{1,0:T(8,128)(2,1)} %w_ref.1) | copy-start | bytes 5308420
  74.1 13.6 %copy-start.10 = (bf16[1176,1152]{1,0:T(8,128)(2,1)}, bf16[1176,1152]{1,0:T(8,128)(2,1)S(1)}, u32[]{:S(2)}) copy-start(bf16[1176,1152]{1,0:T(8,128)(2,1)S(1)} %get-tuple-element.89.joined_ref) | copy-start | bytes 8128516
  74.1 13.6 %copy-start.14 = (bf16[1176,384]{1,0:T(8,128)(2,1)}, bf16[1176,384]{1,0:T(8,128)(2,1)S(1)}, u32[]{:S(2)}) copy-start(bf16[1176,384]{1,0:T(8,128)(2,1)S(1)} %collective-permute-done.10) | copy-start | bytes 2709508
  89.0 41.2 %all-to-all-start = ((bf16[4,96,1536]{2,1,0:T(8,128)(2,1)}), bf16[4,96,1536]{2,1,0:T(8,128)(2,1)}, u32[]{:S(2)}, u32[]{:S(2)}) async-start(bf16[4,96,1536]{2,1,0:T(8,128)(2,1)} %add_convert_fusion.5), calls=%async_computation | async-start | bytes 2359296 | tf_op jit(solution)/shard_map/all_to_all | solution.py:795
  96.5 38.8 %collective-permute-start.13 = (bf16[1176,768]{1,0:T(8,128)(2,1)}, bf16[1176,768]{1,0:T(8,128)(2,1)}, u32[]{:S(2)}, u32[]{:S(2)}) collective-permute-start(bf16[1176,768]{1,0:T(8,128)(2,1)} %get-tuple-element.101.sent_ref), channel_id=1, source_target_pairs={{0,2},{2,0},{1,3},{3,1},{4,6},{6,4},{5,7},{7,5},{8,10},{10,8},{9,1... | collective-permute-start | bytes 5419016 | tf_op jit(solution)/shard_map/ppermute | solution.py:739
  98.0 37.3 %copy-start.5 = (bf16[768]{0:T(1024)(128)(2,1)S(1)}, bf16[768]{0:T(1024)(128)(2,1)}, u32[]{:S(2)}) copy-start(bf16[768]{0:T(1024)(128)(2,1)} %gain_ref.1) | copy-start | bytes 4612
  98.1 8.3 %collective-permute-start = (f32[896]{0:T(1024)S(1)}, f32[896]{0:T(1024)S(1)}, u32[]{:S(2)}, u32[]{:S(2)}) collective-permute-start(f32[896]{0:T(1024)S(1)} %pad_maximum_fusion.1), channel_id=1, source_target_pairs={{0,1},{1,0},{2,3},{3,2},{4,5},{5,4},{6,7},{7,6},{8,9},{9,8},{10,11... | collective-permute-start | bytes 10760 | tf_op jit(solution)/shard_map/cond/branch_1_fun/ppermute | solution.py:739
  98.1 4.5 %copy-start.11 = (bf16[1176,1152]{1,0:T(8,128)(2,1)S(1)}, bf16[1176,1152]{1,0:T(8,128)(2,1)}, u32[]{:S(2)}) copy-start(bf16[1176,1152]{1,0:T(8,128)(2,1)} %get-tuple-element.19.refs_1_) | copy-start | bytes 8128516 | tf_op jit(solution)/shard_map/cond
  98.1 4.5 %copy-start.19 = (bf16[768,1280]{1,0:T(8,128)(2,1)S(1)}, bf16[768,1280]{1,0:T(8,128)(2,1)}, u32[]{:S(2)}) copy-start(bf16[768,1280]{1,0:T(8,128)(2,1)} %get-tuple-element.18.refs_0_) | copy-start | bytes 5898244 | tf_op jit(solution)/shard_map/cond
  102.1 4.4 %collective-permute-start.1 = (bf16[2,4,48,768]{3,2,1,0:T(8,128)(2,1)S(1)}, bf16[2,4,48,768]{3,2,1,0:T(8,128)(2,1)S(1)}, u32[]{:S(2)}, u32[]{:S(2)}) collective-permute-start(bf16[2,4,48,768]{3,2,1,0:T(8,128)(2,1)S(1)} %get-tuple-element.21), channel_id=1, source_target_pairs={{0,1},{1,0},{2,3},{3,2},{4,5},{5,4},{6,7},{7,6},{8,9},{9,8},{10,11... | collective-permute-start | bytes 1769480 | tf_op jit(solution)/shard_map/cond/branch_1_fun/ppermute | solution.py:739
  104.9 4.5 %collective-permute-start.3 = (bf16[2,4,48,768]{3,2,1,0:T(8,128)(2,1)S(1)}, bf16[2,4,48,768]{3,2,1,0:T(8,128)(2,1)S(1)}, u32[]{:S(2)}, u32[]{:S(2)}) collective-permute-start(bf16[2,4,48,768]{3,2,1,0:T(8,128)(2,1)S(1)} %get-tuple-element.26), channel_id=1, source_target_pairs={{0,1},{1,0},{2,3},{3,2},{4,5},{5,4},{6,7},{7,6},{8,9},{9,8},{10,11... | collective-permute-start | bytes 1769480 | tf_op jit(solution)/shard_map/cond/branch_1_fun/ppermute | solution.py:739
  107.3 10.2 %collective-permute-start.2 = (bf16[4,48,768]{2,1,0:T(8,128)(2,1)}, bf16[4,48,768]{2,1,0:T(8,128)(2,1)}, u32[]{:S(2)}, u32[]{:S(2)}) collective-permute-start(bf16[4,48,768]{2,1,0:T(8,128)(2,1)} %slice_bitcast_fusion.2), channel_id=1, source_target_pairs={{0,4},{4,0},{8,12},{12,8},{16,20},{20,16},{24,28},{28,24},{1,5},{5... | collective-permute-start | bytes 884744 | tf_op jit(solution)/shard_map/cond/branch_1_fun/ppermute | solution.py:739
  107.5 9.9 %collective-permute-start.5 = (bf16[896]{0:T(1024)(128)(2,1)S(1)}, bf16[896]{0:T(1024)(128)(2,1)S(1)}, u32[]{:S(2)}, u32[]{:S(2)}) collective-permute-start(bf16[896]{0:T(1024)(128)(2,1)S(1)} %add_convert_fusion.3), channel_id=1, source_target_pairs={{0,4},{4,0},{8,12},{12,8},{16,20},{20,16},{24,28},{28,24},{1,5},{5... | collective-permute-start | bytes 5384 | tf_op jit(solution)/shard_map/cond/branch_1_fun/ppermute | solution.py:739
  111.1 12.1 %collective-permute-start.4 = (bf16[4,48,768]{2,1,0:T(8,128)(2,1)}, bf16[4,48,768]{2,1,0:T(8,128)(2,1)}, u32[]{:S(2)}, u32[]{:S(2)}) collective-permute-start(bf16[4,48,768]{2,1,0:T(8,128)(2,1)} %slice_bitcast_fusion), channel_id=1, source_target_pairs={{0,4},{4,0},{8,12},{12,8},{16,20},{20,16},{24,28},{28,24},{1,5},{5... | collective-permute-start | bytes 884744 | tf_op jit(solution)/shard_map/cond/branch_1_fun/ppermute | solution.py:739
  125.1 15.7 %collective-permute-start.12 = (bf16[56,1536]{1,0:T(8,128)(2,1)}, bf16[56,1536]{1,0:T(8,128)(2,1)S(1)}, u32[]{:S(2)}, u32[]{:S(2)}) collective-permute-start(bf16[56,1536]{1,0:T(8,128)(2,1)} %copy-done.16), channel_id=1, source_target_pairs={{0,8},{4,12},{8,0},{12,4},{16,24},{20,28},{24,16},{28,20},{1,9},{5... | collective-permute-start | bytes 516104 | tf_op jit(solution)/shard_map/ppermute | solution.py:739
  127.1 15.8 %collective-permute-start.14 = (bf16[56,1536]{1,0:T(8,128)(2,1)}, bf16[56,1536]{1,0:T(8,128)(2,1)S(1)}, u32[]{:S(2)}, u32[]{:S(2)}) collective-permute-start(bf16[56,1536]{1,0:T(8,128)(2,1)} %copy-done.17), channel_id=1, source_target_pairs={{0,16},{4,20},{8,24},{12,28},{16,0},{20,4},{24,8},{28,12},{1,17},{... | collective-permute-start | bytes 516104 | tf_op jit(solution)/shard_map/ppermute | solution.py:739
  129.5 13.4 %collective-permute-start.15 = (bf16[56,1536]{1,0:T(8,128)(2,1)}, bf16[56,1536]{1,0:T(8,128)(2,1)S(1)}, u32[]{:S(2)}, u32[]{:S(2)}) collective-permute-start(bf16[56,1536]{1,0:T(8,128)(2,1)} %copy-done.18), channel_id=1, source_target_pairs={{0,24},{4,28},{8,16},{12,20},{16,8},{20,12},{24,0},{28,4},{1,25},{... | collective-permute-start | bytes 516104 | tf_op jit(solution)/shard_map/ppermute | solution.py:739
  130.2 5.2 %copy-start.4 = (bf16[1176,384]{1,0:T(8,128)(2,1)S(1)}, bf16[1176,384]{1,0:T(8,128)(2,1)}, u32[]{:S(2)}) copy-start(bf16[1176,384]{1,0:T(8,128)(2,1)} %copy-done.3) | copy-start | bytes 2709508
  143.7 3.7 %collective-permute-start.16 = (f32[1536]{0:T(1024)S(1)}, f32[1536]{0:T(1024)S(1)}, u32[]{:S(2)}, u32[]{:S(2)}) collective-permute-start(f32[1536]{0:T(1024)S(1)} %slice_reduce_fusion.1), channel_id=1, source_target_pairs={{0,2},{2,0},{1,3},{3,1},{4,6},{6,4},{5,7},{7,5},{8,10},{10,8},{9,1... | collective-permute-start | bytes 18440 | tf_op jit(solution)/shard_map/ppermute | solution.py:739
  (9 other events, 25.4 us)

commit v6 on v5

--- a/solution.py
+++ b/solution.py
@@ -830,19 +830,20 @@
     columns = attended.shape[1]
 
     def weight_sums(normed_t, dy_t, grad_joined, attended, gain_part, qk_part, kept, out_came):
-        first_blocks = row_blocks((normed_t, grad_joined, 2 * columns, 0))
-        blocks = row_blocks((normed_t, grad_joined, columns, 2), (dy_t, attended, columns, 0))
+        parts = (
+            row_blocks((normed_t, grad_joined, columns, 0)),
+            row_blocks((normed_t, grad_joined, columns, 1)),
+            row_blocks((normed_t, grad_joined, columns, 2), (dy_t, attended, columns, 0)),
+        )
         small = jnp.concatenate([gain_part[0], qk_part[0, :size], qk_part[0, LANES : LANES + size]])
         small = low(sum_everywhere(small, ("hid",)))
-        small, first_blocks = lax.optimization_barrier((small, first_blocks))
-        first_kept, first_came = halve(first_blocks)
-        second_kept, second_came = halve(blocks)
+        small, first = lax.optimization_barrier((small, parts[0]))
+        halves = [halve(part) for part in (first,) + parts[1:]]
         small = low(wide(small) + wide(swap(small, "dp", 1)))
         small = jnp.pad(small, (0, 8 * 4 * columns - small.shape[0])).reshape(1, 8, -1)
-        first = low(wide(first_kept) + wide(first_came))
-        second = low(wide(second_kept) + wide(second_came))
-        small = jnp.broadcast_to(small, first.shape[:1] + small.shape[1:])
-        sums = jnp.concatenate([jnp.concatenate([first, second], axis=2), small], axis=1)
+        sums = jnp.concatenate([low(wide(stays) + wide(comes)) for stays, comes in halves], axis=2)
+        small = jnp.broadcast_to(small, sums.shape[:1] + small.shape[1:])
+        sums = jnp.concatenate([sums, small], axis=1)
         return [sums[step] for step in range(sums.shape[0])], low(kept + wide(out_came))
 
     def no_sums(*operands):
@@ -852,6 +853,7 @@
     kinds = jax.eval_shape(weight_sums, *operands)
     sums, output = lax.cond(big_images[0] >= 0, weight_sums, no_sums, *operands)
     mlp_terms = rest_terms(mlp_kept, mlp_came)
+    mlp_terms, came = lax.optimization_barrier((mlp_terms, came))
     hidden = mlp_terms.shape[2] // 2
     w_in_grad = jnp.sum(wide(mlp_terms[:, :, :hidden]), axis=0)
     w_back_grad = jnp.sum(wide(mlp_terms[:, :, hidden:]), axis=0)

time: 149 us -> 148 us (level)
  waiting for transfers between devices: 31.1 us -> 29.1 us
  starting transfers between devices: 26.1 us -> 24.6 us
    all_to_all x1, starting transfers between devices: 7.47 us -> 5.09 us  [rest_terms(): lax.all_to_all(total, 'dp', 0, 0, axis_index_groups=groups, tiled=True)]
    ppermute x17 -> x19, waiting for transfers between devices: 31.1 us -> 29.1 us  [swap(): lax.ppermute(value, axis, [(place, place ^ bit) for place in range(size)])]
    pallas_call x2 -> x3, Pallas kernels: 6.16 us -> 7.41 us  [weights(): pl.pallas_call(weights_kernel, name='weights', grid=(1,), out_shape=[jax....]
    convert_element_type x6 -> x7, other arithmetic: 4.76 us -> 3.69 us  [low(): return value.astype(jnp.bfloat16)]
    ppermute x17 -> x19, starting transfers between devices: 18.6 us -> 19.5 us  [swap(): lax.ppermute(value, axis, [(place, place ^ bit) for place in range(size)])]
  transfers between devices with their start and end apart: 18 -> 20, of which waited for: 7 -> 8; matrix products, arithmetic and copies ran while one was open for 6% -> 7% of each run, Pallas kernels for 34% -> 35%
where the time goes in v6:
time: 148 us; the launch traced here: 147 us
  Pallas kernels  78.3 us (53%)
  waiting for transfers between devices  29.1 us (20%)
  starting transfers between devices  24.6 us (17%)
  other arithmetic  8.23 us (6%)
  local copies, waits for them, and re-layouts  5 us (3%)
  between operations  1.48 us (1%)
    ppermute x19, waiting for transfers between devices, swap(): lax.ppermute(value, axis, [(place, place ^ bit) for place in range(size)])  29.1 us
    pallas_call x1, Pallas kernels, dense(): pl.pallas_call(functools.partial(dense_kernel, count, tiles), name='dense...  21.7 us
    ppermute x19, starting transfers between devices, swap(): lax.ppermute(value, axis, [(place, place ^ bit) for place in range(size)])  19.5 us
    pallas_call x1, Pallas kernels, backward(): pl.pallas_call(backward_kernel, name='backward', grid=(heads // 2,), out_...  16.7 us
    pallas_call x1, Pallas kernels, forward(): pl.pallas_call(forward_kernel, name='forward', out_shape=[jax.ShapeDtypeS...  15.9 us
    pallas_call x3, Pallas kernels, weights(): pl.pallas_call(weights_kernel, name='weights', grid=(1,), out_shape=[jax....  7.41 us
    pallas_call x1, Pallas kernels, outputs(): pl.pallas_call(outputs_kernel, name='outputs', grid=(rows // tile,), out_...  5.86 us
    pallas_call x1, Pallas kernels, token_rows(): pl.pallas_call(tokens_kernel, name='token_rows', grid=(count,), out_shape...  5.44 us
  transfers between devices with their start and end apart: 20, of which 8 were waited for; matrix products, arithmetic and copies ran while one was open for 7% of the time, Pallas kernels for 35%

profile of v6, /device:TPU:0, one launch (start us, length us, event | category | flops | bytes accessed | tf_op | source)
XLA Modules:
  0.0 146.9 jit_solution(10547988578981753972)
XLA Ops:
  0.6 3.0 %collective-permute-start.8 = (bf16[1176,384]{1,0:T(8,128)(2,1)}, bf16[1176,384]{1,0:T(8,128)(2,1)S(1)}, u32[]{:S(2)}, u32[]{:S(2)}) collective-permute-start(bf16[1176,384]{1,0:T(8,128)(2,1)} %mine_ref.5), channel_id=1, source_target_pairs={{0,2},{2,0},{1,3},{3,1},{4,6},{6,4},{5,7},{7,5},{8,10},{10,8},{9,1... | collective-permute-start | bytes 2709512 | tf_op jit(solution)/shard_map/ppermute | solution.py:739
  4.8 15.9 %forward.1 = (bf16[1176,768]{1,0:T(8,128)(2,1)S(1)}, bf16[6,1280,128]{2,1,0:T(8,128)(2,1)}, bf16[6,1280,128]{2,1,0:T(8,128)(2,1)}, bf16[6,1280,128]{2,1,0:T(8,12...) custom-call(s32[1]{0:T(128)S(6)} %copy.27.flag_ref, bf16[1176,768]{1,0:T(8,128)(2,1)} %tok_ref.5, ...), custom_call_target="tpu_custom_call" | custom-call | flops 24000000000 | bytes 1048576 | tf_op jit(solution)/shard_map/forward/pallas_call | solution.py:261
  20.8 3.1 %collective-permute-done.8.other_ref = bf16[1176,384]{1,0:T(8,128)(2,1)S(1)} collective-permute-done((bf16[1176,384]{1,0:T(8,128)(2,1)}, bf16[1176,384]{1,0:T(8,128)(2,1)S(1)}, u32[]{:S(2)}, u32[]{:S(2)}) %collective-permute-start.8) | collective-permute-done | bytes 903200 | tf_op jit(solution)/shard_map/ppermute | solution.py:739
  24.0 21.7 %dense.1 = (f32[1176,768]{1,0:T(8,128)S(1)}, bf16[1176,768]{1,0:T(8,128)(2,1)S(1)}, bf16[768,1280]{1,0:T(8,128)(2,1)}, bf16[768,1280]{1,0:T(8,128)(2,1)}, bf16[2...) custom-call(bf16[1176,768]{1,0:T(8,128)(2,1)S(1)} %get-tuple-element.83.normed_ref, ...), custom_call_target="tpu_custom_call" | custom-call | flops 24000000000 | bytes 1048576 | tf_op jit(solution)/shard_map/dense/pallas_call | solution.py:491
  45.7 5.9 %outputs.1 = (f32[1176,384]{1,0:T(8,128)}, bf16[1176,384]{1,0:T(8,128)(2,1)S(1)}, bf16[6,1280,128]{2,1,0:T(8,128)(2,1)S(1)}) custom-call(f32[1176,768]{1,0:T(8,128)S(1)} %get-tuple-element.84.part_ref, bf16[1176,768]{1,0:T(8,128)(2,1)S(1)} %copy-done, bf16[1176,384]{1,0:T(8,128)(2,1)S(1)} %get-tuple-element.85.att_ref, bf16[1176,384]{1,0:T(8,128)(2,1)S(1)} %copy-done.2, ...), custom_call_target="tpu_custom_call" | custom-call | flops 6000000000 | bytes 1048576 | tf_op jit(solution)/shard_map/outputs/pallas_call | solution.py:561
  51.6 1.8 %collective-permute-start.12 = (bf16[1176,384]{1,0:T(8,128)(2,1)S(1)}, bf16[1176,384]{1,0:T(8,128)(2,1)S(1)}, u32[]{:S(2)}, u32[]{:S(2)}) collective-permute-start(bf16[1176,384]{1,0:T(8,128)(2,1)S(1)} %get-tuple-element.92), channel_id=1, source_target_pairs={{0,2},{2,0},{1,3},{3,1},{4,6},{6,4},{5,7},{7,5},{8,10},{10,8},{9,1... | collective-permute-start | bytes 2709512 | tf_op jit(solution)/shard_map/ppermute | solution.py:739
  54.2 1.6 %collective-permute-start.13 = (bf16[4,96,1536]{2,1,0:T(8,128)(2,1)S(1)}, bf16[4,96,1536]{2,1,0:T(8,128)(2,1)S(1)}, u32[]{:S(2)}, u32[]{:S(2)}) collective-permute-start(bf16[4,96,1536]{2,1,0:T(8,128)(2,1)S(1)} %get-tuple-element.128), channel_id=1, source_target_pairs={{0,4},{4,0},{8,12},{12,8},{16,20},{20,16},{24,28},{28,24},{1,5},{5... | collective-permute-start | bytes 3538952 | tf_op jit(solution)/shard_map/ppermute | solution.py:739
  55.8 16.7 %backward.1 = (bf16[1176,1152]{1,0:T(8,128)(2,1)S(1)}, f32[8,256]{1,0:T(8,128)S(1)}) custom-call(s32[1]{0:T(128)S(6)} %copy.27.flag_ref, bf16[6,1280,128]{2,1,0:T(8,128)(2,1)} %get-tuple-element.80.q_ref, bf16[6,1280,128]{2,1,0:T(8,128)(2,1)} %get-tuple-element.81.k_ref, bf16[6,1280,128]{2,1,0:T(8,128)(2,1)} %get-tuple-element.82.v_ref, ...), custom_call_target="tpu_custom_call" | custom-call | flops 35999997952 | bytes 1048576 | tf_op jit(solution)/shard_map/backward/pallas_call | solution.py:386
  72.5 1.5 %collective-permute-done.12 = bf16[1176,384]{1,0:T(8,128)(2,1)S(1)} collective-permute-done((bf16[1176,384]{1,0:T(8,128)(2,1)S(1)}, bf16[1176,384]{1,0:T(8,128)(2,1)S(1)}, u32[]{:S(2)}, u32[]{:S(2)}) %collective-permute-start.12) | collective-permute-done | bytes 903200 | tf_op jit(solution)/shard_map/ppermute | solution.py:739
  74.0 8.3 %collective-permute-done.13 = bf16[4,96,1536]{2,1,0:T(8,128)(2,1)S(1)} collective-permute-done((bf16[4,96,1536]{2,1,0:T(8,128)(2,1)S(1)}, bf16[4,96,1536]{2,1,0:T(8,128)(2,1)S(1)}, u32[]{:S(2)}, u32[]{:S(2)}) %collective-permute-start.13) | collective-permute-done | bytes 1179680 | tf_op jit(solution)/shard_map/ppermute | solution.py:739
  82.4 4.5 %features.1 = (bf16[1176,768]{1,0:T(8,128)(2,1)}, f32[8,768]{1,0:T(8,128)S(1)}) custom-call(bf16[1176,1152]{1,0:T(8,128)(2,1)S(1)} %get-tuple-element.93.joined_ref, bf16[768,1152]{1,0:T(8,128)(2,1)S(1)} %copy-done.1, bf16[1176,768]{1,0:T(8,128)(2,1)S(1)} %get-tuple-element.94.mlp_ref, bf16[1176,768]{1,0:T(8,128)(2,1)S(1)} %copy-done), custom_call_target="tpu_custom_call" | custom-call | flops 900000000 | bytes 1048576 | tf_op jit(solution)/shard_map/features/pallas_call | solution.py:600
  87.2 1.4 add_convert_fusion.6
  88.6 5.1 %all-to-all-start = ((bf16[4,96,1536]{2,1,0:T(8,128)(2,1)}), bf16[4,96,1536]{2,1,0:T(8,128)(2,1)}, u32[]{:S(2)}, u32[]{:S(2)}) async-start(bf16[4,96,1536]{2,1,0:T(8,128)(2,1)} %add_convert_fusion.6), calls=%async_computation | async-start | bytes 2359296 | tf_op jit(solution)/shard_map/all_to_all | solution.py:795
  93.7 29.0 %conditional.1 = (bf16[56,1536]{1,0:T(8,128)(2,1)S(1)}, bf16[56,1536]{1,0:T(8,128)(2,1)S(1)}, bf16[56,1536]{1,0:T(8,128)(2,1)S(1)}, bf16[56,1536]{1,0:T(8,128)(2,1)S(1)}, bf16[1176,384]{1,0:T(8,128)(2,1)}) conditional(s32[]{:T(128)} %bitcast.15, () %tuple.22, (f32[8,768]{1,0:T(8,128)S(1)}, f32[8,256]{1,0:T(8,128)S(1)}, bf16[768,1280]{1,0:T(8,128)(2,1)}, ...), branch_computations={%region_0.0_spmd, %region_1.2_spmd} | conditional | flops 9007655936 | bytes 69062016 | solution.py:854
  93.7 3.1 %weights.3 = (bf16[2,4,48,384]{3,2,1,0:T(8,128)(2,1)S(1)}, bf16[2,4,48,384]{3,2,1,0:T(8,128)(2,1)S(1)}) custom-call(bf16[768,1280]{1,0:T(8,128)(2,1)} %get-tuple-element.18.refs_0_, bf16[1176,1152]{1,0:T(8,128)(2,1)} %get-tuple-element.19.refs_1_), custom_call_target="tpu_custom_call" | custom-call | flops 3000000000 | bytes 1048576 | tf_op jit(solution)/shard_map/cond/branch_1_fun/weights/pallas_call | solution.py:653
  96.8 1.6 %collective-permute-start.1 = (bf16[2,4,48,384]{3,2,1,0:T(8,128)(2,1)S(1)}, bf16[2,4,48,384]{3,2,1,0:T(8,128)(2,1)S(1)}, u32[]{:S(2)}, u32[]{:S(2)}) collective-permute-start(bf16[2,4,48,384]{3,2,1,0:T(8,128)(2,1)S(1)} %get-tuple-element.21), channel_id=1, source_target_pairs={{0,1},{1,0},{2,3},{3,2},{4,5},{5,4},{6,7},{7,6},{8,9},{9,8},{10,11... | collective-permute-start | bytes 884744 | tf_op jit(solution)/shard_map/cond/branch_1_fun/ppermute | solution.py:739
  98.6 3.1 %weights.5 = (bf16[2,4,48,768]{3,2,1,0:T(8,128)(2,1)S(1)}, bf16[2,4,48,768]{3,2,1,0:T(8,128)(2,1)}) custom-call(bf16[768,1280]{1,0:T(8,128)(2,1)S(1)} %copy-done.22, bf16[1176,1152]{1,0:T(8,128)(2,1)S(1)} %copy-done.11, bf16[768,1280]{1,0:T(8,128)(2,1)S(1)} %copy-done.23, bf16[1176,384]{1,0:T(8,128)(2,1)S(1)} %copy-done.25), custom_call_target="tpu_custom_call" | custom-call | flops 3000000000 | bytes 1048576 | tf_op jit(solution)/shard_map/cond/branch_1_fun/weights/pallas_call | solution.py:653
  102.3 1.2 weights.4
  103.7 1.2 add_convert_fusion
  106.1 1.6 %collective-permute-start.7 = (bf16[896]{0:T(1024)(128)(2,1)S(1)}, bf16[896]{0:T(1024)(128)(2,1)S(1)}, u32[]{:S(2)}, u32[]{:S(2)}) collective-permute-start(bf16[896]{0:T(1024)(128)(2,1)S(1)} %add_convert_fusion.4), channel_id=1, source_target_pairs={{0,4},{4,0},{8,12},{12,8},{16,20},{20,16},{24,28},{28,24},{1,5},{5... | collective-permute-start | bytes 5384 | tf_op jit(solution)/shard_map/cond/branch_1_fun/ppermute | solution.py:739
  109.0 3.6 %collective-permute-done.7 = bf16[896]{0:T(1024)(128)(2,1)S(1)} collective-permute-done((bf16[896]{0:T(1024)(128)(2,1)S(1)}, bf16[896]{0:T(1024)(128)(2,1)S(1)}, u32[]{:S(2)}, u32[]{:S(2)}) %collective-permute-start.7) | collective-permute-done | bytes 1824 | tf_op jit(solution)/shard_map/cond/branch_1_fun/ppermute | solution.py:739
  112.8 1.3 add_convert_fusion.1
  114.6 0.9 collective-permute-done.4
  115.5 1.0 fusion.1
  116.5 6.0 %collective-permute-done.6 = bf16[4,48,768]{2,1,0:T(8,128)(2,1)S(1)} collective-permute-done((bf16[4,48,768]{2,1,0:T(8,128)(2,1)S(1)}, bf16[4,48,768]{2,1,0:T(8,128)(2,1)S(1)}, u32[]{:S(2)}, u32[]{:S(2)}) %collective-permute-start.6) | collective-permute-done | bytes 294944 | tf_op jit(solution)/shard_map/cond/branch_1_fun/ppermute | solution.py:739
  123.3 3.3 %collective-permute-start.14 = (bf16[56,1536]{1,0:T(8,128)(2,1)}, bf16[56,1536]{1,0:T(8,128)(2,1)S(1)}, u32[]{:S(2)}, u32[]{:S(2)}) collective-permute-start(bf16[56,1536]{1,0:T(8,128)(2,1)} %copy-done.19), channel_id=1, source_target_pairs={{0,8},{4,12},{8,0},{12,4},{16,24},{20,28},{24,16},{28,20},{1,9},{5... | collective-permute-start | bytes 516104 | tf_op jit(solution)/shard_map/ppermute | solution.py:739
  127.4 2.2 %collective-permute-start.17 = (bf16[56,1536]{1,0:T(8,128)(2,1)}, bf16[56,1536]{1,0:T(8,128)(2,1)S(1)}, u32[]{:S(2)}, u32[]{:S(2)}) collective-permute-start(bf16[56,1536]{1,0:T(8,128)(2,1)} %copy-done.21), channel_id=1, source_target_pairs={{0,24},{4,28},{8,16},{12,20},{16,8},{20,12},{24,0},{28,4},{1,25},{... | collective-permute-start | bytes 516104 | tf_op jit(solution)/shard_map/ppermute | solution.py:739
  129.6 1.2 copy-done.4
  130.8 5.4 %token_rows.1 = bf16[1176,768]{1,0:T(8,128)(2,1)} custom-call(bf16[1176,768]{1,0:T(8,128)(2,1)} %get-tuple-element.105.sent_ref, bf16[1176,768]{1,0:T(8,128)(2,1)} %collective-permute-done.15.came_ref, bf16[1176,768]{1,0:T(8,128)(2,1)S(1)} %copy-done, bf16[768]{0:T(1024)(128)(2,1)S(1)} %copy-done.5, bf16[1176,384]{1,0:T(8,128)(2,1)S(1)} %copy-done.2, ...), custom_call_target="tpu_custom_call" | custom-call | flops 900000000 | bytes 1048576 | tf_op jit(solution)/shard_map/token_rows/pallas_call | solution.py:687
  136.3 2.3 %convert_reduce_fusion = (f32[96,768]{1,0:T(8,128)}, f32[96,768]{1,0:T(8,128)}) fusion(bf16[4,96,1536]{2,1,0:T(8,128)(2,1)} %all-to-all-done), kind=kLoop, calls=%fused_computation.31 | loop fusion | flops 1032192 | bytes 1769472 | tf_op jit(solution)/shard_map/reduce_sum | solution.py:859
  138.5 2.6 %collective-permute-done.16.refs_2_ = bf16[56,1536]{1,0:T(8,128)(2,1)S(1)} collective-permute-done((bf16[56,1536]{1,0:T(8,128)(2,1)}, bf16[56,1536]{1,0:T(8,128)(2,1)S(1)}, u32[]{:S(2)}, u32[]{:S(2)}) %collective-permute-start.16) | collective-permute-done | bytes 172064 | tf_op jit(solution)/shard_map/ppermute | solution.py:739
  142.6 3.0 %collective-permute-done.18 = f32[1536]{0:T(1024)S(1)} collective-permute-done((f32[1536]{0:T(1024)S(1)}, f32[1536]{0:T(1024)S(1)}, u32[]{:S(2)}, u32[]{:S(2)}) %collective-permute-start.18) | collective-permute-done | bytes 6176 | tf_op jit(solution)/shard_map/ppermute | solution.py:739
  (100 shorter events, 10.2 us)
Async XLA Ops:
  0.6 23.3 %collective-permute-start.8 = (bf16[1176,384]{1,0:T(8,128)(2,1)}, bf16[1176,384]{1,0:T(8,128)(2,1)S(1)}, u32[]{:S(2)}, u32[]{:S(2)}) collective-permute-start(bf16[1176,384]{1,0:T(8,128)(2,1)} %mine_ref.5), channel_id=1, source_target_pairs={{0,2},{2,0},{1,3},{3,1},{4,6},{6,4},{5,7},{7,5},{8,10},{10,8},{9,1... | collective-permute-start | bytes 2709512 | tf_op jit(solution)/shard_map/ppermute | solution.py:739
  3.6 20.3 %collective-permute-start.10 = (bf16[768,768]{1,0:T(8,128)(2,1)}, bf16[768,768]{1,0:T(8,128)(2,1)S(1)}, u32[]{:S(2)}, u32[]{:S(2)}) collective-permute-start(bf16[768,768]{1,0:T(8,128)(2,1)} %refs_2_.1), channel_id=1, source_target_pairs={{0,1},{1,0},{2,3},{3,2},{4,5},{5,4},{6,7},{7,6},{8,9},{9,8},{10,11... | collective-permute-start | bytes 3538952 | tf_op jit(solution)/shard_map/ppermute | solution.py:739
  3.6 20.3 %collective-permute-start.9 = (bf16[768,768]{1,0:T(8,128)(2,1)}, bf16[768,768]{1,0:T(8,128)(2,1)S(1)}, u32[]{:S(2)}, u32[]{:S(2)}) collective-permute-start(bf16[768,768]{1,0:T(8,128)(2,1)} %refs_0_.1), channel_id=1, source_target_pairs={{0,1},{1,0},{2,3},{3,2},{4,5},{5,4},{6,7},{7,6},{8,9},{9,8},{10,11... | collective-permute-start | bytes 3538952 | tf_op jit(solution)/shard_map/ppermute | solution.py:739
  4.8 19.1 %copy-start.2 = (bf16[1176,384]{1,0:T(8,128)(2,1)S(1)}, bf16[1176,384]{1,0:T(8,128)(2,1)}, u32[]{:S(2)}) copy-start(bf16[1176,384]{1,0:T(8,128)(2,1)} %mine_ref.5) | copy-start | bytes 2709508
  4.8 19.1 %copy-start.6 = (bf16[768,768]{1,0:T(8,128)(2,1)S(1)}, bf16[768,768]{1,0:T(8,128)(2,1)}, u32[]{:S(2)}) copy-start(bf16[768,768]{1,0:T(8,128)(2,1)} %refs_0_.1) | copy-start | bytes 3538948
  4.8 19.1 %copy-start.7 = (bf16[768,768]{1,0:T(8,128)(2,1)S(1)}, bf16[768,768]{1,0:T(8,128)(2,1)}, u32[]{:S(2)}) copy-start(bf16[768,768]{1,0:T(8,128)(2,1)} %refs_2_.1) | copy-start | bytes 3538948
  20.8 24.9 %copy-start.24 = (bf16[1176,384]{1,0:T(8,128)(2,1)}, bf16[1176,384]{1,0:T(8,128)(2,1)S(1)}, u32[]{:S(2)}) copy-start(bf16[1176,384]{1,0:T(8,128)(2,1)S(1)} %get-tuple-element.85.att_ref) | copy-start | bytes 2709508
  23.9 21.8 %copy-start.3 = (bf16[1176,384]{1,0:T(8,128)(2,1)}, bf16[1176,384]{1,0:T(8,128)(2,1)S(1)}, u32[]{:S(2)}) copy-start(bf16[1176,384]{1,0:T(8,128)(2,1)S(1)} %collective-permute-done.8.other_ref) | copy-start | bytes 2709508
  23.9 21.7 %copy-start = (bf16[1176,768]{1,0:T(8,128)(2,1)S(1)}, bf16[1176,768]{1,0:T(8,128)(2,1)}, u32[]{:S(2)}) copy-start(bf16[1176,768]{1,0:T(8,128)(2,1)} %tok_ref.5) | copy-start | bytes 5419012
  23.9 21.7 %copy-start.8 = (bf16[768,384]{1,0:T(8,128)(2,1)S(1)}, bf16[768,384]{1,0:T(8,128)(2,1)}, u32[]{:S(2)}) copy-start(bf16[768,384]{1,0:T(8,128)(2,1)} %w_out_ref.1) | copy-start | bytes 1769476
  45.7 7.7 %collective-permute-start.11 = (bf16[2,4,96,1536]{3,2,1,0:T(8,128)(2,1)S(1)}, bf16[2,4,96,1536]{3,2,1,0:T(8,128)(2,1)S(1)}, u32[]{:S(2)}, u32[]{:S(2)}) collective-permute-start(bf16[2,4,96,1536]{3,2,1,0:T(8,128)(2,1)S(1)} %get-tuple-element.88), channel_id=1, source_target_pairs={{0,1},{1,0},{2,3},{3,2},{4,5},{5,4},{6,7},{7,6},{8,9},{9,8},{10,11... | collective-permute-start | bytes 7077896 | tf_op jit(solution)/shard_map/ppermute | solution.py:739
  51.6 22.5 %collective-permute-start.12 = (bf16[1176,384]{1,0:T(8,128)(2,1)S(1)}, bf16[1176,384]{1,0:T(8,128)(2,1)S(1)}, u32[]{:S(2)}, u32[]{:S(2)}) collective-permute-start(bf16[1176,384]{1,0:T(8,128)(2,1)S(1)} %get-tuple-element.92), channel_id=1, source_target_pairs={{0,2},{2,0},{1,3},{3,1},{4,6},{6,4},{5,7},{7,5},{8,10},{10,8},{9,1... | collective-permute-start | bytes 2709512 | tf_op jit(solution)/shard_map/ppermute | solution.py:739
  54.2 28.2 %collective-permute-start.13 = (bf16[4,96,1536]{2,1,0:T(8,128)(2,1)S(1)}, bf16[4,96,1536]{2,1,0:T(8,128)(2,1)S(1)}, u32[]{:S(2)}, u32[]{:S(2)}) collective-permute-start(bf16[4,96,1536]{2,1,0:T(8,128)(2,1)S(1)} %get-tuple-element.128), channel_id=1, source_target_pairs={{0,4},{4,0},{8,12},{12,8},{16,20},{20,16},{24,28},{28,24},{1,5},{5... | collective-permute-start | bytes 3538952 | tf_op jit(solution)/shard_map/ppermute | solution.py:739
  55.8 26.6 %copy-start.1 = (bf16[768,1152]{1,0:T(8,128)(2,1)S(1)}, bf16[768,1152]{1,0:T(8,128)(2,1)}, u32[]{:S(2)}) copy-start(bf16[768,1152]{1,0:T(8,128)(2,1)} %w_ref.1) | copy-start | bytes 5308420
  72.5 14.4 %copy-start.10 = (bf16[1176,1152]{1,0:T(8,128)(2,1)}, bf16[1176,1152]{1,0:T(8,128)(2,1)S(1)}, u32[]{:S(2)}) copy-start(bf16[1176,1152]{1,0:T(8,128)(2,1)S(1)} %get-tuple-element.93.joined_ref) | copy-start | bytes 8128516
  74.0 12.8 %copy-start.17 = (bf16[1176,384]{1,0:T(8,128)(2,1)}, bf16[1176,384]{1,0:T(8,128)(2,1)S(1)}, u32[]{:S(2)}) copy-start(bf16[1176,384]{1,0:T(8,128)(2,1)S(1)} %collective-permute-done.12) | copy-start | bytes 2709508
  86.9 42.8 %collective-permute-start.15 = (bf16[1176,768]{1,0:T(8,128)(2,1)}, bf16[1176,768]{1,0:T(8,128)(2,1)}, u32[]{:S(2)}, u32[]{:S(2)}) collective-permute-start(bf16[1176,768]{1,0:T(8,128)(2,1)} %get-tuple-element.105.sent_ref), channel_id=1, source_target_pairs={{0,2},{2,0},{1,3},{3,1},{4,6},{6,4},{5,7},{7,5},{8,10},{10,8},{9,1... | collective-permute-start | bytes 5419016 | tf_op jit(solution)/shard_map/ppermute | solution.py:739
  88.6 41.1 %all-to-all-start = ((bf16[4,96,1536]{2,1,0:T(8,128)(2,1)}), bf16[4,96,1536]{2,1,0:T(8,128)(2,1)}, u32[]{:S(2)}, u32[]{:S(2)}) async-start(bf16[4,96,1536]{2,1,0:T(8,128)(2,1)} %add_convert_fusion.6), calls=%async_computation | async-start | bytes 2359296 | tf_op jit(solution)/shard_map/all_to_all | solution.py:795
  93.7 36.0 %copy-start.5 = (bf16[768]{0:T(1024)(128)(2,1)S(1)}, bf16[768]{0:T(1024)(128)(2,1)}, u32[]{:S(2)}) copy-start(bf16[768]{0:T(1024)(128)(2,1)} %gain_ref.1) | copy-start | bytes 4612
  93.7 4.9 %copy-start.22 = (bf16[768,1280]{1,0:T(8,128)(2,1)S(1)}, bf16[768,1280]{1,0:T(8,128)(2,1)}, u32[]{:S(2)}) copy-start(bf16[768,1280]{1,0:T(8,128)(2,1)} %get-tuple-element.18.refs_0_) | copy-start | bytes 5898244 | tf_op jit(solution)/shard_map/cond
  96.8 8.1 %collective-permute-start.1 = (bf16[2,4,48,384]{3,2,1,0:T(8,128)(2,1)S(1)}, bf16[2,4,48,384]{3,2,1,0:T(8,128)(2,1)S(1)}, u32[]{:S(2)}, u32[]{:S(2)}) collective-permute-start(bf16[2,4,48,384]{3,2,1,0:T(8,128)(2,1)S(1)} %get-tuple-element.21), channel_id=1, source_target_pairs={{0,1},{1,0},{2,3},{3,2},{4,5},{5,4},{6,7},{7,6},{8,9},{9,8},{10,11... | collective-permute-start | bytes 884744 | tf_op jit(solution)/shard_map/cond/branch_1_fun/ppermute | solution.py:739
  98.5 6.3 %collective-permute-start = (f32[896]{0:T(1024)S(1)}, f32[896]{0:T(1024)S(1)}, u32[]{:S(2)}, u32[]{:S(2)}) collective-permute-start(f32[896]{0:T(1024)S(1)} %pad_maximum_fusion.1), channel_id=1, source_target_pairs={{0,1},{1,0},{2,3},{3,2},{4,5},{5,4},{6,7},{7,6},{8,9},{9,8},{10,11... | collective-permute-start | bytes 10760 | tf_op jit(solution)/shard_map/cond/branch_1_fun/ppermute | solution.py:739
  101.7 11.1 %collective-permute-start.5 = (bf16[2,4,48,768]{3,2,1,0:T(8,128)(2,1)}, bf16[2,4,48,768]{3,2,1,0:T(8,128)(2,1)}, u32[]{:S(2)}, u32[]{:S(2)}) collective-permute-start(bf16[2,4,48,768]{3,2,1,0:T(8,128)(2,1)} %get-tuple-element.28), channel_id=1, source_target_pairs={{0,1},{1,0},{2,3},{3,2},{4,5},{5,4},{6,7},{7,6},{8,9},{9,8},{10,11... | collective-permute-start | bytes 1769480 | tf_op jit(solution)/shard_map/cond/branch_1_fun/ppermute | solution.py:739
  103.6 4.2 %collective-permute-start.3 = (bf16[2,4,48,384]{3,2,1,0:T(8,128)(2,1)S(1)}, bf16[2,4,48,384]{3,2,1,0:T(8,128)(2,1)S(1)}, u32[]{:S(2)}, u32[]{:S(2)}) collective-permute-start(bf16[2,4,48,384]{3,2,1,0:T(8,128)(2,1)S(1)} %get-tuple-element.24), channel_id=1, source_target_pairs={{0,1},{1,0},{2,3},{3,2},{4,5},{5,4},{6,7},{7,6},{8,9},{9,8},{10,11... | collective-permute-start | bytes 884744 | tf_op jit(solution)/shard_map/cond/branch_1_fun/ppermute | solution.py:739
  105.7 8.8 %collective-permute-start.2 = (bf16[4,48,384]{2,1,0:T(8,128)(2,1)}, bf16[4,48,384]{2,1,0:T(8,128)(2,1)S(1)}, u32[]{:S(2)}, u32[]{:S(2)}) collective-permute-start(bf16[4,48,384]{2,1,0:T(8,128)(2,1)} %slice_bitcast_fusion.8), channel_id=1, source_target_pairs={{0,4},{4,0},{8,12},{12,8},{16,20},{20,16},{24,28},{28,24},{1,5},{5... | collective-permute-start | bytes 442376 | tf_op jit(solution)/shard_map/cond/branch_1_fun/ppermute | solution.py:739
  106.1 6.5 %collective-permute-start.7 = (bf16[896]{0:T(1024)(128)(2,1)S(1)}, bf16[896]{0:T(1024)(128)(2,1)S(1)}, u32[]{:S(2)}, u32[]{:S(2)}) collective-permute-start(bf16[896]{0:T(1024)(128)(2,1)S(1)} %add_convert_fusion.4), channel_id=1, source_target_pairs={{0,4},{4,0},{8,12},{12,8},{16,20},{20,16},{24,28},{28,24},{1,5},{5... | collective-permute-start | bytes 5384 | tf_op jit(solution)/shard_map/cond/branch_1_fun/ppermute | solution.py:739
  108.6 6.9 %collective-permute-start.4 = (bf16[4,48,384]{2,1,0:T(8,128)(2,1)}, bf16[4,48,384]{2,1,0:T(8,128)(2,1)}, u32[]{:S(2)}, u32[]{:S(2)}) collective-permute-start(bf16[4,48,384]{2,1,0:T(8,128)(2,1)} %slice_bitcast_fusion.6), channel_id=1, source_target_pairs={{0,4},{4,0},{8,12},{12,8},{16,20},{20,16},{24,28},{28,24},{1,5},{5... | collective-permute-start | bytes 442376 | tf_op jit(solution)/shard_map/cond/branch_1_fun/ppermute | solution.py:739
  114.1 8.4 %collective-permute-start.6 = (bf16[4,48,768]{2,1,0:T(8,128)(2,1)S(1)}, bf16[4,48,768]{2,1,0:T(8,128)(2,1)S(1)}, u32[]{:S(2)}, u32[]{:S(2)}) collective-permute-start(bf16[4,48,768]{2,1,0:T(8,128)(2,1)S(1)} %slice_bitcast_fusion), channel_id=1, source_target_pairs={{0,4},{4,0},{8,12},{12,8},{16,20},{20,16},{24,28},{28,24},{1,5},{5... | collective-permute-start | bytes 884744 | tf_op jit(solution)/shard_map/cond/branch_1_fun/ppermute | solution.py:739
  123.3 15.2 %collective-permute-start.14 = (bf16[56,1536]{1,0:T(8,128)(2,1)}, bf16[56,1536]{1,0:T(8,128)(2,1)S(1)}, u32[]{:S(2)}, u32[]{:S(2)}) collective-permute-start(bf16[56,1536]{1,0:T(8,128)(2,1)} %copy-done.19), channel_id=1, source_target_pairs={{0,8},{4,12},{8,0},{12,4},{16,24},{20,28},{24,16},{28,20},{1,9},{5... | collective-permute-start | bytes 516104 | tf_op jit(solution)/shard_map/ppermute | solution.py:739
  126.6 14.5 %collective-permute-start.16 = (bf16[56,1536]{1,0:T(8,128)(2,1)}, bf16[56,1536]{1,0:T(8,128)(2,1)S(1)}, u32[]{:S(2)}, u32[]{:S(2)}) collective-permute-start(bf16[56,1536]{1,0:T(8,128)(2,1)} %copy-done.20), channel_id=1, source_target_pairs={{0,16},{4,20},{8,24},{12,28},{16,0},{20,4},{24,8},{28,12},{1,17},{... | collective-permute-start | bytes 516104 | tf_op jit(solution)/shard_map/ppermute | solution.py:739
  127.4 13.7 %collective-permute-start.17 = (bf16[56,1536]{1,0:T(8,128)(2,1)}, bf16[56,1536]{1,0:T(8,128)(2,1)S(1)}, u32[]{:S(2)}, u32[]{:S(2)}) collective-permute-start(bf16[56,1536]{1,0:T(8,128)(2,1)} %copy-done.21), channel_id=1, source_target_pairs={{0,24},{4,28},{8,16},{12,20},{16,8},{20,12},{24,0},{28,4},{1,25},{... | collective-permute-start | bytes 516104 | tf_op jit(solution)/shard_map/ppermute | solution.py:739
  141.9 3.7 %collective-permute-start.18 = (f32[1536]{0:T(1024)S(1)}, f32[1536]{0:T(1024)S(1)}, u32[]{:S(2)}, u32[]{:S(2)}) collective-permute-start(f32[1536]{0:T(1024)S(1)} %slice_reduce_fusion.1), channel_id=1, source_target_pairs={{0,2},{2,0},{1,3},{3,1},{4,6},{6,4},{5,7},{7,5},{8,10},{10,8},{9,1... | collective-permute-start | bytes 18440 | tf_op jit(solution)/shard_map/ppermute | solution.py:739
  (14 other events, 37.8 us)

commit v7 on v6

--- a/solution.py
+++ b/solution.py
@@ -853,7 +853,6 @@
     kinds = jax.eval_shape(weight_sums, *operands)
     sums, output = lax.cond(big_images[0] >= 0, weight_sums, no_sums, *operands)
     mlp_terms = rest_terms(mlp_kept, mlp_came)
-    mlp_terms, came = lax.optimization_barrier((mlp_terms, came))
     hidden = mlp_terms.shape[2] // 2
     w_in_grad = jnp.sum(wide(mlp_terms[:, :, :hidden]), axis=0)
     w_back_grad = jnp.sum(wide(mlp_terms[:, :, hidden:]), axis=0)

time: 148 us -> 147 us (level)
  starting transfers between devices: 24.6 us -> 29.3 us
  waiting for transfers between devices: 29.1 us -> 25.8 us
    ppermute x19, starting transfers between devices: 19.5 us -> 24.2 us  [swap(): lax.ppermute(value, axis, [(place, place ^ bit) for place in range(size)])]
    ppermute x19, waiting for transfers between devices: 29.1 us -> 25.8 us  [swap(): lax.ppermute(value, axis, [(place, place ^ bit) for place in range(size)])]
  transfers between devices with their start and end apart: 20 -> 20, of which waited for: 8 -> 7; matrix products, arithmetic and copies ran while one was open for 7% -> 6% of each run, Pallas kernels for 35% -> 35%
where the time goes in v7:
time: 147 us
  Pallas kernels  78.3 us (53%)
  starting transfers between devices  29.3 us (20%)
  waiting for transfers between devices  25.8 us (18%)
  other arithmetic  8.3 us (6%)
  local copies, waits for them, and re-layouts  3.84 us (3%)
  between operations  1.48 us (1%)
    ppermute x19, waiting for transfers between devices, swap(): lax.ppermute(value, axis, [(place, place ^ bit) for place in range(size)])  25.8 us
    ppermute x19, starting transfers between devices, swap(): lax.ppermute(value, axis, [(place, place ^ bit) for place in range(size)])  24.2 us
    pallas_call x1, Pallas kernels, dense(): pl.pallas_call(functools.partial(dense_kernel, count, tiles), name='dense...  21.7 us
    pallas_call x1, Pallas kernels, backward(): pl.pallas_call(backward_kernel, name='backward', grid=(heads // 2,), out_...  16.7 us
    pallas_call x1, Pallas kernels, forward(): pl.pallas_call(forward_kernel, name='forward', out_shape=[jax.ShapeDtypeS...  15.9 us
    pallas_call x3, Pallas kernels, weights(): pl.pallas_call(weights_kernel, name='weights', grid=(1,), out_shape=[jax....  7.41 us
    pallas_call x1, Pallas kernels, outputs(): pl.pallas_call(outputs_kernel, name='outputs', grid=(rows // tile,), out_...  5.86 us
    pallas_call x1, Pallas kernels, token_rows(): pl.pallas_call(tokens_kernel, name='token_rows', grid=(count,), out_shape...  5.45 us
  transfers between devices with their start and end apart: 20, of which 7 were waited for; matrix products, arithmetic and copies ran while one was open for 6% of the time, Pallas kernels for 35%

profile of v7, /device:TPU:0, one launch (start us, length us, event | category | flops | bytes accessed | tf_op | source)
XLA Modules:
  0.0 147.2 jit_solution(12475513076722986598)
XLA Ops:
  0.6 3.0 %collective-permute-start.8 = (bf16[1176,384]{1,0:T(8,128)(2,1)}, bf16[1176,384]{1,0:T(8,128)(2,1)S(1)}, u32[]{:S(2)}, u32[]{:S(2)}) collective-permute-start(bf16[1176,384]{1,0:T(8,128)(2,1)} %mine_ref.5), channel_id=1, source_target_pairs={{0,2},{2,0},{1,3},{3,1},{4,6},{6,4},{5,7},{7,5},{8,10},{10,8},{9,1... | collective-permute-start | bytes 2709512 | tf_op jit(solution)/shard_map/ppermute | solution.py:739
  4.8 15.9 %forward.1 = (bf16[1176,768]{1,0:T(8,128)(2,1)S(1)}, bf16[6,1280,128]{2,1,0:T(8,128)(2,1)}, bf16[6,1280,128]{2,1,0:T(8,128)(2,1)}, bf16[6,1280,128]{2,1,0:T(8,12...) custom-call(s32[1]{0:T(128)S(6)} %copy.27.flag_ref, bf16[1176,768]{1,0:T(8,128)(2,1)} %tok_ref.5, ...), custom_call_target="tpu_custom_call" | custom-call | flops 24000000000 | bytes 1048576 | tf_op jit(solution)/shard_map/forward/pallas_call | solution.py:261
  20.8 3.1 %collective-permute-done.8.other_ref = bf16[1176,384]{1,0:T(8,128)(2,1)S(1)} collective-permute-done((bf16[1176,384]{1,0:T(8,128)(2,1)}, bf16[1176,384]{1,0:T(8,128)(2,1)S(1)}, u32[]{:S(2)}, u32[]{:S(2)}) %collective-permute-start.8) | collective-permute-done | bytes 903200 | tf_op jit(solution)/shard_map/ppermute | solution.py:739
  24.0 21.7 %dense.1 = (f32[1176,768]{1,0:T(8,128)S(1)}, bf16[1176,768]{1,0:T(8,128)(2,1)S(1)}, bf16[768,1280]{1,0:T(8,128)(2,1)}, bf16[768,1280]{1,0:T(8,128)(2,1)}, bf16[2...) custom-call(bf16[1176,768]{1,0:T(8,128)(2,1)S(1)} %get-tuple-element.81.normed_ref, ...), custom_call_target="tpu_custom_call" | custom-call | flops 24000000000 | bytes 1048576 | tf_op jit(solution)/shard_map/dense/pallas_call | solution.py:491
  45.7 5.9 %outputs.1 = (f32[1176,384]{1,0:T(8,128)}, bf16[1176,384]{1,0:T(8,128)(2,1)S(1)}, bf16[6,1280,128]{2,1,0:T(8,128)(2,1)S(1)}) custom-call(f32[1176,768]{1,0:T(8,128)S(1)} %get-tuple-element.82.part_ref, bf16[1176,768]{1,0:T(8,128)(2,1)S(1)} %copy-done, bf16[1176,384]{1,0:T(8,128)(2,1)S(1)} %get-tuple-element.83.att_ref, bf16[1176,384]{1,0:T(8,128)(2,1)S(1)} %copy-done.2, ...), custom_call_target="tpu_custom_call" | custom-call | flops 6000000000 | bytes 1048576 | tf_op jit(solution)/shard_map/outputs/pallas_call | solution.py:561
  51.6 1.8 %collective-permute-start.12 = (bf16[1176,384]{1,0:T(8,128)(2,1)S(1)}, bf16[1176,384]{1,0:T(8,128)(2,1)S(1)}, u32[]{:S(2)}, u32[]{:S(2)}) collective-permute-start(bf16[1176,384]{1,0:T(8,128)(2,1)S(1)} %get-tuple-element.90), channel_id=1, source_target_pairs={{0,2},{2,0},{1,3},{3,1},{4,6},{6,4},{5,7},{7,5},{8,10},{10,8},{9,1... | collective-permute-start | bytes 2709512 | tf_op jit(solution)/shard_map/ppermute | solution.py:739
  54.2 3.1 %collective-permute-start.13 = (bf16[4,96,1536]{2,1,0:T(8,128)(2,1)S(1)}, bf16[4,96,1536]{2,1,0:T(8,128)(2,1)S(1)}, u32[]{:S(2)}, u32[]{:S(2)}) collective-permute-start(bf16[4,96,1536]{2,1,0:T(8,128)(2,1)S(1)} %get-tuple-element.124), channel_id=1, source_target_pairs={{0,4},{4,0},{8,12},{12,8},{16,20},{20,16},{24,28},{28,24},{1,5},{5... | collective-permute-start | bytes 3538952 | tf_op jit(solution)/shard_map/ppermute | solution.py:739
  57.3 16.7 %backward.1 = (bf16[1176,1152]{1,0:T(8,128)(2,1)S(1)}, f32[8,256]{1,0:T(8,128)S(1)}) custom-call(s32[1]{0:T(128)S(6)} %copy.27.flag_ref, bf16[6,1280,128]{2,1,0:T(8,128)(2,1)} %get-tuple-element.78.q_ref, bf16[6,1280,128]{2,1,0:T(8,128)(2,1)} %get-tuple-element.79.k_ref, bf16[6,1280,128]{2,1,0:T(8,128)(2,1)} %get-tuple-element.80.v_ref, ...), custom_call_target="tpu_custom_call" | custom-call | flops 35999997952 | bytes 1048576 | tf_op jit(solution)/shard_map/backward/pallas_call | solution.py:386
  74.1 9.1 %collective-permute-done.13 = bf16[4,96,1536]{2,1,0:T(8,128)(2,1)S(1)} collective-permute-done((bf16[4,96,1536]{2,1,0:T(8,128)(2,1)S(1)}, bf16[4,96,1536]{2,1,0:T(8,128)(2,1)S(1)}, u32[]{:S(2)}, u32[]{:S(2)}) %collective-permute-start.13) | collective-permute-done | bytes 1179680 | tf_op jit(solution)/shard_map/ppermute | solution.py:739
  83.2 4.5 %features.1 = (bf16[1176,768]{1,0:T(8,128)(2,1)}, f32[8,768]{1,0:T(8,128)S(1)}) custom-call(bf16[1176,1152]{1,0:T(8,128)(2,1)S(1)} %get-tuple-element.91.joined_ref, bf16[768,1152]{1,0:T(8,128)(2,1)S(1)} %copy-done.1, bf16[1176,768]{1,0:T(8,128)(2,1)S(1)} %get-tuple-element.92.mlp_ref, bf16[1176,768]{1,0:T(8,128)(2,1)S(1)} %copy-done), custom_call_target="tpu_custom_call" | custom-call | flops 900000000 | bytes 1048576 | tf_op jit(solution)/shard_map/features/pallas_call | solution.py:600
  87.7 1.4 add_convert_fusion.6
  89.1 5.1 %all-to-all-start = ((bf16[4,96,1536]{2,1,0:T(8,128)(2,1)}), bf16[4,96,1536]{2,1,0:T(8,128)(2,1)}, u32[]{:S(2)}, u32[]{:S(2)}) async-start(bf16[4,96,1536]{2,1,0:T(8,128)(2,1)} %add_convert_fusion.6), calls=%async_computation | async-start | bytes 2359296 | tf_op jit(solution)/shard_map/all_to_all | solution.py:795
  94.2 1.5 %collective-permute-start.15 = (bf16[1176,768]{1,0:T(8,128)(2,1)}, bf16[1176,768]{1,0:T(8,128)(2,1)}, u32[]{:S(2)}, u32[]{:S(2)}) collective-permute-start(bf16[1176,768]{1,0:T(8,128)(2,1)} %get-tuple-element.103.sent_ref), channel_id=1, source_target_pairs={{0,2},{2,0},{1,3},{3,1},{4,6},{6,4},{5,7},{7,5},{8,10},{10,8},{9,1... | collective-permute-start | bytes 5419016 | tf_op jit(solution)/shard_map/ppermute | solution.py:739
  95.7 29.0 %conditional.1 = (bf16[56,1536]{1,0:T(8,128)(2,1)S(1)}, bf16[56,1536]{1,0:T(8,128)(2,1)S(1)}, bf16[56,1536]{1,0:T(8,128)(2,1)S(1)}, bf16[56,1536]{1,0:T(8,128)(2,1)S(1)}, bf16[1176,384]{1,0:T(8,128)(2,1)}) conditional(s32[]{:T(128)} %bitcast.15, () %tuple.21, (f32[8,768]{1,0:T(8,128)S(1)}, f32[8,256]{1,0:T(8,128)S(1)}, bf16[768,1280]{1,0:T(8,128)(2,1)}, ...), branch_computations={%region_0.0_spmd, %region_1.2_spmd} | conditional | flops 9007655936 | bytes 69062016 | solution.py:854
  95.7 3.1 %weights.3 = (bf16[2,4,48,384]{3,2,1,0:T(8,128)(2,1)S(1)}, bf16[2,4,48,384]{3,2,1,0:T(8,128)(2,1)S(1)}) custom-call(bf16[768,1280]{1,0:T(8,128)(2,1)} %get-tuple-element.18.refs_0_, bf16[1176,1152]{1,0:T(8,128)(2,1)} %get-tuple-element.19.refs_1_), custom_call_target="tpu_custom_call" | custom-call | flops 3000000000 | bytes 1048576 | tf_op jit(solution)/shard_map/cond/branch_1_fun/weights/pallas_call | solution.py:653
  98.8 1.6 %collective-permute-start.1 = (bf16[2,4,48,384]{3,2,1,0:T(8,128)(2,1)S(1)}, bf16[2,4,48,384]{3,2,1,0:T(8,128)(2,1)S(1)}, u32[]{:S(2)}, u32[]{:S(2)}) collective-permute-start(bf16[2,4,48,384]{3,2,1,0:T(8,128)(2,1)S(1)} %get-tuple-element.21), channel_id=1, source_target_pairs={{0,1},{1,0},{2,3},{3,2},{4,5},{5,4},{6,7},{7,6},{8,9},{9,8},{10,11... | collective-permute-start | bytes 884744 | tf_op jit(solution)/shard_map/cond/branch_1_fun/ppermute | solution.py:739
  100.5 3.1 %weights.5 = (bf16[2,4,48,768]{3,2,1,0:T(8,128)(2,1)S(1)}, bf16[2,4,48,768]{3,2,1,0:T(8,128)(2,1)}) custom-call(bf16[768,1280]{1,0:T(8,128)(2,1)S(1)} %copy-done.22, bf16[1176,1152]{1,0:T(8,128)(2,1)S(1)} %copy-done.11, bf16[768,1280]{1,0:T(8,128)(2,1)S(1)} %copy-done.23, bf16[1176,384]{1,0:T(8,128)(2,1)S(1)} %copy-done.25), custom_call_target="tpu_custom_call" | custom-call | flops 3000000000 | bytes 1048576 | tf_op jit(solution)/shard_map/cond/branch_1_fun/weights/pallas_call | solution.py:653
  104.3 1.2 weights.4
  105.7 1.2 add_convert_fusion
  107.7 1.9 %collective-permute-start.2 = (bf16[4,48,384]{2,1,0:T(8,128)(2,1)}, bf16[4,48,384]{2,1,0:T(8,128)(2,1)S(1)}, u32[]{:S(2)}, u32[]{:S(2)}) collective-permute-start(bf16[4,48,384]{2,1,0:T(8,128)(2,1)} %slice_bitcast_fusion.8), channel_id=1, source_target_pairs={{0,4},{4,0},{8,12},{12,8},{16,20},{20,16},{24,28},{28,24},{1,5},{5... | collective-permute-start | bytes 442376 | tf_op jit(solution)/shard_map/cond/branch_1_fun/ppermute | solution.py:739
  110.6 1.9 %collective-permute-start.4 = (bf16[4,48,384]{2,1,0:T(8,128)(2,1)}, bf16[4,48,384]{2,1,0:T(8,128)(2,1)}, u32[]{:S(2)}, u32[]{:S(2)}) collective-permute-start(bf16[4,48,384]{2,1,0:T(8,128)(2,1)} %slice_bitcast_fusion.6), channel_id=1, source_target_pairs={{0,4},{4,0},{8,12},{12,8},{16,20},{20,16},{24,28},{28,24},{1,5},{5... | collective-permute-start | bytes 442376 | tf_op jit(solution)/shard_map/cond/branch_1_fun/ppermute | solution.py:739
  112.5 2.1 %collective-permute-done.7 = bf16[896]{0:T(1024)(128)(2,1)S(1)} collective-permute-done((bf16[896]{0:T(1024)(128)(2,1)S(1)}, bf16[896]{0:T(1024)(128)(2,1)S(1)}, u32[]{:S(2)}, u32[]{:S(2)}) %collective-permute-start.7) | collective-permute-done | bytes 1824 | tf_op jit(solution)/shard_map/cond/branch_1_fun/ppermute | solution.py:739
  114.7 1.3 add_convert_fusion.1
  116.0 1.8 %collective-permute-start.6 = (bf16[4,48,768]{2,1,0:T(8,128)(2,1)S(1)}, bf16[4,48,768]{2,1,0:T(8,128)(2,1)S(1)}, u32[]{:S(2)}, u32[]{:S(2)}) collective-permute-start(bf16[4,48,768]{2,1,0:T(8,128)(2,1)S(1)} %slice_bitcast_fusion), channel_id=1, source_target_pairs={{0,4},{4,0},{8,12},{12,8},{16,20},{20,16},{24,28},{28,24},{1,5},{5... | collective-permute-start | bytes 884744 | tf_op jit(solution)/shard_map/cond/branch_1_fun/ppermute | solution.py:739
  118.9 5.5 %collective-permute-done.6 = bf16[4,48,768]{2,1,0:T(8,128)(2,1)S(1)} collective-permute-done((bf16[4,48,768]{2,1,0:T(8,128)(2,1)S(1)}, bf16[4,48,768]{2,1,0:T(8,128)(2,1)S(1)}, u32[]{:S(2)}, u32[]{:S(2)}) %collective-permute-start.6) | collective-permute-done | bytes 294944 | tf_op jit(solution)/shard_map/cond/branch_1_fun/ppermute | solution.py:739
  125.3 1.6 %collective-permute-start.14 = (bf16[56,1536]{1,0:T(8,128)(2,1)}, bf16[56,1536]{1,0:T(8,128)(2,1)S(1)}, u32[]{:S(2)}, u32[]{:S(2)}) collective-permute-start(bf16[56,1536]{1,0:T(8,128)(2,1)} %copy-done.19), channel_id=1, source_target_pairs={{0,8},{4,12},{8,0},{12,4},{16,24},{20,28},{24,16},{28,20},{1,9},{5... | collective-permute-start | bytes 516104 | tf_op jit(solution)/shard_map/ppermute | solution.py:739
  126.9 2.4 %collective-permute-start.16 = (bf16[56,1536]{1,0:T(8,128)(2,1)}, bf16[56,1536]{1,0:T(8,128)(2,1)S(1)}, u32[]{:S(2)}, u32[]{:S(2)}) collective-permute-start(bf16[56,1536]{1,0:T(8,128)(2,1)} %copy-done.20), channel_id=1, source_target_pairs={{0,16},{4,20},{8,24},{12,28},{16,0},{20,4},{24,8},{28,12},{1,17},{... | collective-permute-start | bytes 516104 | tf_op jit(solution)/shard_map/ppermute | solution.py:739
  130.0 2.4 %convert_reduce_fusion = (f32[96,768]{1,0:T(8,128)}, f32[96,768]{1,0:T(8,128)}) fusion(bf16[4,96,1536]{2,1,0:T(8,128)(2,1)} %all-to-all-done), kind=kLoop, calls=%fused_computation.31 | loop fusion | flops 1032192 | bytes 1769472 | tf_op jit(solution)/shard_map/reduce_sum | solution.py:858
  132.3 3.6 %collective-permute-done.15.came_ref = bf16[1176,768]{1,0:T(8,128)(2,1)} collective-permute-done((bf16[1176,768]{1,0:T(8,128)(2,1)}, bf16[1176,768]{1,0:T(8,128)(2,1)}, u32[]{:S(2)}, u32[]{:S(2)}) %collective-permute-start.15) | collective-permute-done | bytes 1806368 | tf_op jit(solution)/shard_map/ppermute | solution.py:739
  135.9 5.5 %token_rows.1 = bf16[1176,768]{1,0:T(8,128)(2,1)} custom-call(bf16[1176,768]{1,0:T(8,128)(2,1)} %get-tuple-element.103.sent_ref, bf16[1176,768]{1,0:T(8,128)(2,1)} %collective-permute-done.15.came_ref, bf16[1176,768]{1,0:T(8,128)(2,1)S(1)} %copy-done, bf16[768]{0:T(1024)(128)(2,1)S(1)} %copy-done.5, bf16[1176,384]{1,0:T(8,128)(2,1)S(1)} %copy-done.2, ...), custom_call_target="tpu_custom_call" | custom-call | flops 900000000 | bytes 1048576 | tf_op jit(solution)/shard_map/token_rows/pallas_call | solution.py:687
  142.3 1.5 collective-permute-start.18
  143.7 2.2 %collective-permute-done.18 = f32[1536]{0:T(1024)S(1)} collective-permute-done((f32[1536]{0:T(1024)S(1)}, f32[1536]{0:T(1024)S(1)}, u32[]{:S(2)}, u32[]{:S(2)}) %collective-permute-start.18) | collective-permute-done | bytes 6176 | tf_op jit(solution)/shard_map/ppermute | solution.py:739
  (100 shorter events, 9.0 us)
Async XLA Ops:
  0.6 23.3 %collective-permute-start.8 = (bf16[1176,384]{1,0:T(8,128)(2,1)}, bf16[1176,384]{1,0:T(8,128)(2,1)S(1)}, u32[]{:S(2)}, u32[]{:S(2)}) collective-permute-start(bf16[1176,384]{1,0:T(8,128)(2,1)} %mine_ref.5), channel_id=1, source_target_pairs={{0,2},{2,0},{1,3},{3,1},{4,6},{6,4},{5,7},{7,5},{8,10},{10,8},{9,1... | collective-permute-start | bytes 2709512 | tf_op jit(solution)/shard_map/ppermute | solution.py:739
  3.6 20.3 %collective-permute-start.10 = (bf16[768,768]{1,0:T(8,128)(2,1)}, bf16[768,768]{1,0:T(8,128)(2,1)S(1)}, u32[]{:S(2)}, u32[]{:S(2)}) collective-permute-start(bf16[768,768]{1,0:T(8,128)(2,1)} %refs_2_.1), channel_id=1, source_target_pairs={{0,1},{1,0},{2,3},{3,2},{4,5},{5,4},{6,7},{7,6},{8,9},{9,8},{10,11... | collective-permute-start | bytes 3538952 | tf_op jit(solution)/shard_map/ppermute | solution.py:739
  3.6 20.3 %collective-permute-start.9 = (bf16[768,768]{1,0:T(8,128)(2,1)}, bf16[768,768]{1,0:T(8,128)(2,1)S(1)}, u32[]{:S(2)}, u32[]{:S(2)}) collective-permute-start(bf16[768,768]{1,0:T(8,128)(2,1)} %refs_0_.1), channel_id=1, source_target_pairs={{0,1},{1,0},{2,3},{3,2},{4,5},{5,4},{6,7},{7,6},{8,9},{9,8},{10,11... | collective-permute-start | bytes 3538952 | tf_op jit(solution)/shard_map/ppermute | solution.py:739
  4.8 19.1 %copy-start.2 = (bf16[1176,384]{1,0:T(8,128)(2,1)S(1)}, bf16[1176,384]{1,0:T(8,128)(2,1)}, u32[]{:S(2)}) copy-start(bf16[1176,384]{1,0:T(8,128)(2,1)} %mine_ref.5) | copy-start | bytes 2709508
  4.8 19.1 %copy-start.6 = (bf16[768,768]{1,0:T(8,128)(2,1)S(1)}, bf16[768,768]{1,0:T(8,128)(2,1)}, u32[]{:S(2)}) copy-start(bf16[768,768]{1,0:T(8,128)(2,1)} %refs_0_.1) | copy-start | bytes 3538948
  4.8 19.1 %copy-start.7 = (bf16[768,768]{1,0:T(8,128)(2,1)S(1)}, bf16[768,768]{1,0:T(8,128)(2,1)}, u32[]{:S(2)}) copy-start(bf16[768,768]{1,0:T(8,128)(2,1)} %refs_2_.1) | copy-start | bytes 3538948
  20.8 24.9 %copy-start.24 = (bf16[1176,384]{1,0:T(8,128)(2,1)}, bf16[1176,384]{1,0:T(8,128)(2,1)S(1)}, u32[]{:S(2)}) copy-start(bf16[1176,384]{1,0:T(8,128)(2,1)S(1)} %get-tuple-element.83.att_ref) | copy-start | bytes 2709508
  23.9 21.8 %copy-start.3 = (bf16[1176,384]{1,0:T(8,128)(2,1)}, bf16[1176,384]{1,0:T(8,128)(2,1)S(1)}, u32[]{:S(2)}) copy-start(bf16[1176,384]{1,0:T(8,128)(2,1)S(1)} %collective-permute-done.8.other_ref) | copy-start | bytes 2709508
  23.9 21.7 %copy-start = (bf16[1176,768]{1,0:T(8,128)(2,1)S(1)}, bf16[1176,768]{1,0:T(8,128)(2,1)}, u32[]{:S(2)}) copy-start(bf16[1176,768]{1,0:T(8,128)(2,1)} %tok_ref.5) | copy-start | bytes 5419012
  23.9 21.7 %copy-start.8 = (bf16[768,384]{1,0:T(8,128)(2,1)S(1)}, bf16[768,384]{1,0:T(8,128)(2,1)}, u32[]{:S(2)}) copy-start(bf16[768,384]{1,0:T(8,128)(2,1)} %w_out_ref.1) | copy-start | bytes 1769476
  45.7 7.7 %collective-permute-start.11 = (bf16[2,4,96,1536]{3,2,1,0:T(8,128)(2,1)S(1)}, bf16[2,4,96,1536]{3,2,1,0:T(8,128)(2,1)S(1)}, u32[]{:S(2)}, u32[]{:S(2)}) collective-permute-start(bf16[2,4,96,1536]{3,2,1,0:T(8,128)(2,1)S(1)} %get-tuple-element.86), channel_id=1, source_target_pairs={{0,1},{1,0},{2,3},{3,2},{4,5},{5,4},{6,7},{7,6},{8,9},{9,8},{10,11... | collective-permute-start | bytes 7077896 | tf_op jit(solution)/shard_map/ppermute | solution.py:739
  51.6 22.5 %collective-permute-start.12 = (bf16[1176,384]{1,0:T(8,128)(2,1)S(1)}, bf16[1176,384]{1,0:T(8,128)(2,1)S(1)}, u32[]{:S(2)}, u32[]{:S(2)}) collective-permute-start(bf16[1176,384]{1,0:T(8,128)(2,1)S(1)} %get-tuple-element.90), channel_id=1, source_target_pairs={{0,2},{2,0},{1,3},{3,1},{4,6},{6,4},{5,7},{7,5},{8,10},{10,8},{9,1... | collective-permute-start | bytes 2709512 | tf_op jit(solution)/shard_map/ppermute | solution.py:739
  54.2 29.0 %collective-permute-start.13 = (bf16[4,96,1536]{2,1,0:T(8,128)(2,1)S(1)}, bf16[4,96,1536]{2,1,0:T(8,128)(2,1)S(1)}, u32[]{:S(2)}, u32[]{:S(2)}) collective-permute-start(bf16[4,96,1536]{2,1,0:T(8,128)(2,1)S(1)} %get-tuple-element.124), channel_id=1, source_target_pairs={{0,4},{4,0},{8,12},{12,8},{16,20},{20,16},{24,28},{28,24},{1,5},{5... | collective-permute-start | bytes 3538952 | tf_op jit(solution)/shard_map/ppermute | solution.py:739
  57.3 25.9 %copy-start.1 = (bf16[768,1152]{1,0:T(8,128)(2,1)S(1)}, bf16[768,1152]{1,0:T(8,128)(2,1)}, u32[]{:S(2)}) copy-start(bf16[768,1152]{1,0:T(8,128)(2,1)} %w_ref.1) | copy-start | bytes 5308420
  74.1 13.6 %copy-start.10 = (bf16[1176,1152]{1,0:T(8,128)(2,1)}, bf16[1176,1152]{1,0:T(8,128)(2,1)S(1)}, u32[]{:S(2)}) copy-start(bf16[1176,1152]{1,0:T(8,128)(2,1)S(1)} %get-tuple-element.91.joined_ref) | copy-start | bytes 8128516
  74.1 13.6 %copy-start.17 = (bf16[1176,384]{1,0:T(8,128)(2,1)}, bf16[1176,384]{1,0:T(8,128)(2,1)S(1)}, u32[]{:S(2)}) copy-start(bf16[1176,384]{1,0:T(8,128)(2,1)S(1)} %collective-permute-done.12) | copy-start | bytes 2709508
  89.1 40.9 %all-to-all-start = ((bf16[4,96,1536]{2,1,0:T(8,128)(2,1)}), bf16[4,96,1536]{2,1,0:T(8,128)(2,1)}, u32[]{:S(2)}, u32[]{:S(2)}) async-start(bf16[4,96,1536]{2,1,0:T(8,128)(2,1)} %add_convert_fusion.6), calls=%async_computation | async-start | bytes 2359296 | tf_op jit(solution)/shard_map/all_to_all | solution.py:795
  94.2 41.8 %collective-permute-start.15 = (bf16[1176,768]{1,0:T(8,128)(2,1)}, bf16[1176,768]{1,0:T(8,128)(2,1)}, u32[]{:S(2)}, u32[]{:S(2)}) collective-permute-start(bf16[1176,768]{1,0:T(8,128)(2,1)} %get-tuple-element.103.sent_ref), channel_id=1, source_target_pairs={{0,2},{2,0},{1,3},{3,1},{4,6},{6,4},{5,7},{7,5},{8,10},{10,8},{9,1... | collective-permute-start | bytes 5419016 | tf_op jit(solution)/shard_map/ppermute | solution.py:739
  95.7 40.3 %copy-start.5 = (bf16[768]{0:T(1024)(128)(2,1)S(1)}, bf16[768]{0:T(1024)(128)(2,1)}, u32[]{:S(2)}) copy-start(bf16[768]{0:T(1024)(128)(2,1)} %gain_ref.1) | copy-start | bytes 4612
  98.8 8.1 %collective-permute-start.1 = (bf16[2,4,48,384]{3,2,1,0:T(8,128)(2,1)S(1)}, bf16[2,4,48,384]{3,2,1,0:T(8,128)(2,1)S(1)}, u32[]{:S(2)}, u32[]{:S(2)}) collective-permute-start(bf16[2,4,48,384]{3,2,1,0:T(8,128)(2,1)S(1)} %get-tuple-element.21), channel_id=1, source_target_pairs={{0,1},{1,0},{2,3},{3,2},{4,5},{5,4},{6,7},{7,6},{8,9},{9,8},{10,11... | collective-permute-start | bytes 884744 | tf_op jit(solution)/shard_map/cond/branch_1_fun/ppermute | solution.py:739
  100.5 6.3 %collective-permute-start = (f32[896]{0:T(1024)S(1)}, f32[896]{0:T(1024)S(1)}, u32[]{:S(2)}, u32[]{:S(2)}) collective-permute-start(f32[896]{0:T(1024)S(1)} %pad_maximum_fusion.1), channel_id=1, source_target_pairs={{0,1},{1,0},{2,3},{3,2},{4,5},{5,4},{6,7},{7,6},{8,9},{9,8},{10,11... | collective-permute-start | bytes 10760 | tf_op jit(solution)/shard_map/cond/branch_1_fun/ppermute | solution.py:739
  103.6 11.1 %collective-permute-start.5 = (bf16[2,4,48,768]{3,2,1,0:T(8,128)(2,1)}, bf16[2,4,48,768]{3,2,1,0:T(8,128)(2,1)}, u32[]{:S(2)}, u32[]{:S(2)}) collective-permute-start(bf16[2,4,48,768]{3,2,1,0:T(8,128)(2,1)} %get-tuple-element.28), channel_id=1, source_target_pairs={{0,1},{1,0},{2,3},{3,2},{4,5},{5,4},{6,7},{7,6},{8,9},{9,8},{10,11... | collective-permute-start | bytes 1769480 | tf_op jit(solution)/shard_map/cond/branch_1_fun/ppermute | solution.py:739
  105.6 4.2 %collective-permute-start.3 = (bf16[2,4,48,384]{3,2,1,0:T(8,128)(2,1)S(1)}, bf16[2,4,48,384]{3,2,1,0:T(8,128)(2,1)S(1)}, u32[]{:S(2)}, u32[]{:S(2)}) collective-permute-start(bf16[2,4,48,384]{3,2,1,0:T(8,128)(2,1)S(1)} %get-tuple-element.24), channel_id=1, source_target_pairs={{0,1},{1,0},{2,3},{3,2},{4,5},{5,4},{6,7},{7,6},{8,9},{9,8},{10,11... | collective-permute-start | bytes 884744 | tf_op jit(solution)/shard_map/cond/branch_1_fun/ppermute | solution.py:739
  107.7 10.2 %collective-permute-start.2 = (bf16[4,48,384]{2,1,0:T(8,128)(2,1)}, bf16[4,48,384]{2,1,0:T(8,128)(2,1)S(1)}, u32[]{:S(2)}, u32[]{:S(2)}) collective-permute-start(bf16[4,48,384]{2,1,0:T(8,128)(2,1)} %slice_bitcast_fusion.8), channel_id=1, source_target_pairs={{0,4},{4,0},{8,12},{12,8},{16,20},{20,16},{24,28},{28,24},{1,5},{5... | collective-permute-start | bytes 442376 | tf_op jit(solution)/shard_map/cond/branch_1_fun/ppermute | solution.py:739
  109.6 5.0 %collective-permute-start.7 = (bf16[896]{0:T(1024)(128)(2,1)S(1)}, bf16[896]{0:T(1024)(128)(2,1)S(1)}, u32[]{:S(2)}, u32[]{:S(2)}) collective-permute-start(bf16[896]{0:T(1024)(128)(2,1)S(1)} %add_convert_fusion.4), channel_id=1, source_target_pairs={{0,4},{4,0},{8,12},{12,8},{16,20},{20,16},{24,28},{28,24},{1,5},{5... | collective-permute-start | bytes 5384 | tf_op jit(solution)/shard_map/cond/branch_1_fun/ppermute | solution.py:739
  110.6 7.3 %collective-permute-start.4 = (bf16[4,48,384]{2,1,0:T(8,128)(2,1)}, bf16[4,48,384]{2,1,0:T(8,128)(2,1)}, u32[]{:S(2)}, u32[]{:S(2)}) collective-permute-start(bf16[4,48,384]{2,1,0:T(8,128)(2,1)} %slice_bitcast_fusion.6), channel_id=1, source_target_pairs={{0,4},{4,0},{8,12},{12,8},{16,20},{20,16},{24,28},{28,24},{1,5},{5... | collective-permute-start | bytes 442376 | tf_op jit(solution)/shard_map/cond/branch_1_fun/ppermute | solution.py:739
  116.0 8.4 %collective-permute-start.6 = (bf16[4,48,768]{2,1,0:T(8,128)(2,1)S(1)}, bf16[4,48,768]{2,1,0:T(8,128)(2,1)S(1)}, u32[]{:S(2)}, u32[]{:S(2)}) collective-permute-start(bf16[4,48,768]{2,1,0:T(8,128)(2,1)S(1)} %slice_bitcast_fusion), channel_id=1, source_target_pairs={{0,4},{4,0},{8,12},{12,8},{16,20},{20,16},{24,28},{28,24},{1,5},{5... | collective-permute-start | bytes 884744 | tf_op jit(solution)/shard_map/cond/branch_1_fun/ppermute | solution.py:739
  125.3 16.1 %collective-permute-start.14 = (bf16[56,1536]{1,0:T(8,128)(2,1)}, bf16[56,1536]{1,0:T(8,128)(2,1)S(1)}, u32[]{:S(2)}, u32[]{:S(2)}) collective-permute-start(bf16[56,1536]{1,0:T(8,128)(2,1)} %copy-done.19), channel_id=1, source_target_pairs={{0,8},{4,12},{8,0},{12,4},{16,24},{20,28},{24,16},{28,20},{1,9},{5... | collective-permute-start | bytes 516104 | tf_op jit(solution)/shard_map/ppermute | solution.py:739
  126.9 14.5 %collective-permute-start.16 = (bf16[56,1536]{1,0:T(8,128)(2,1)}, bf16[56,1536]{1,0:T(8,128)(2,1)S(1)}, u32[]{:S(2)}, u32[]{:S(2)}) collective-permute-start(bf16[56,1536]{1,0:T(8,128)(2,1)} %copy-done.20), channel_id=1, source_target_pairs={{0,16},{4,20},{8,24},{12,28},{16,0},{20,4},{24,8},{28,12},{1,17},{... | collective-permute-start | bytes 516104 | tf_op jit(solution)/shard_map/ppermute | solution.py:739
  129.3 12.2 %collective-permute-start.17 = (bf16[56,1536]{1,0:T(8,128)(2,1)}, bf16[56,1536]{1,0:T(8,128)(2,1)S(1)}, u32[]{:S(2)}, u32[]{:S(2)}) collective-permute-start(bf16[56,1536]{1,0:T(8,128)(2,1)} %copy-done.21), channel_id=1, source_target_pairs={{0,24},{4,28},{8,16},{12,20},{16,8},{20,12},{24,0},{28,4},{1,25},{... | collective-permute-start | bytes 516104 | tf_op jit(solution)/shard_map/ppermute | solution.py:739
  130.0 6.0 %copy-start.4 = (bf16[1176,384]{1,0:T(8,128)(2,1)S(1)}, bf16[1176,384]{1,0:T(8,128)(2,1)}, u32[]{:S(2)}) copy-start(bf16[1176,384]{1,0:T(8,128)(2,1)} %copy-done.3) | copy-start | bytes 2709508
  142.3 3.7 %collective-permute-start.18 = (f32[1536]{0:T(1024)S(1)}, f32[1536]{0:T(1024)S(1)}, u32[]{:S(2)}, u32[]{:S(2)}) collective-permute-start(f32[1536]{0:T(1024)S(1)} %slice_reduce_fusion.1), channel_id=1, source_target_pairs={{0,2},{2,0},{1,3},{3,1},{4,6},{6,4},{5,7},{7,5},{8,10},{10,8},{9,1... | collective-permute-start | bytes 18440 | tf_op jit(solution)/shard_map/ppermute | solution.py:739
  (14 other events, 43.2 us)
